TPU v7x, 256 devices: a whole 4x4x8 slice. The times are simulated.
256 devices in a mesh: region: 32 (over z, x), tm: 8 (over y, core).
Axes of the slice: x: 4, y: 4, z: 8, core: 2. Of those that a mesh axis runs over, the one named last changes fastest.
Arguments:
- observations: bfloat16 [32, 8, 2048, 512], P('region', 'tm'), may hold values from -160 to 160
- counts: int32 [32, 8], P('region', 'tm'), may hold values from 1 to 8, as said below
- visible: int32 [32, 32], replicated, may hold values 0 or 1
- latents: bfloat16 [32, 32, 512], P('region'), may hold values from -6 to 6
- lat_gain: float32 [512], replicated, may hold values from 0.5 to 1.5
- mlp_gain: float32 [512], replicated, may hold values from 0.5 to 1.5
- w_query: bfloat16 [512, 512], replicated, may hold values from -0.25 to 0.25
- w_keyval: bfloat16 [512, 1024], replicated, may hold values from -0.25 to 0.25
- w_out: bfloat16 [512, 512], replicated, may hold values from -0.25 to 0.25
- w_up: bfloat16 [512, 2048], P(None, 'tm'), may hold values from -0.25 to 0.25
- w_down: bfloat16 [2048, 512], P('tm'), may hold values from -0.125 to 0.125
Outputs:
- encoded: bfloat16 [32, 32, 512], P('region')
Inputs may be any that keep to these rules, and one draw needn't show every extreme that they name: `counts`: some region and time slot holds 8 blocks.
All inputs are finite; a program needn't handle non-finite values.
Results may differ from a plain program's by a relative error of at most 0.0055.
The roundings to bfloat16 on the way count: a program that leaves them out, or rounds other values in their place, can miss the bound.
Values may be sent and summed in bfloat16 or wider, within the bound.
No kernel may reach another device: no remote copies, remote signals or barrier semaphores. Data moves between devices by JAX's collectives and lax.ppermute only.
A program may use at most 64 MiB of HBM per device.

v0:
```python
import functools

import jax
import jax.numpy as jnp
from jax import lax
from jax.experimental import pallas as pl
from jax.experimental.pallas import tpu as pltpu
from jax.sharding import PartitionSpec as P

H = 8
BLK = 256
NZ, NX = 8, 4
EPS = 1e-05
NEG = -1e30
D = 512
DH = 64
LR = 32
WIDE = D + 128
BF = jnp.bfloat16
F32 = jnp.float32


def lanes_of(shape):
    return lax.broadcasted_iota(jnp.int32, shape, len(shape) - 1)


def norm_rows(values, gain):
    average = jnp.mean(values, axis=-1, keepdims=True)
    centered = values - average
    variance = jnp.mean(centered * centered, axis=-1, keepdims=True)
    return centered * lax.rsqrt(variance + EPS) * gain


def whole(shape):
    return pl.BlockSpec(shape, lambda *_: (0,) * len(shape))


def query_kernel(half_ref, lat_ref, gain_ref, wq_ref, out_ref, q_s):
    normed = norm_rows(lat_ref[...].astype(F32), gain_ref[...]).astype(BF)
    q = jnp.dot(normed, wq_ref[...], preferred_element_type=F32).astype(BF)
    q_s[...] = q * jnp.asarray(DH ** -0.5, BF)
    rows = q_s[pl.ds(pl.multiple_of(half_ref[0] * 16, 16), 16), :]
    out_ref[...] = jnp.broadcast_to(rows[None], out_ref.shape)


def pack_stats(lse):
    lane = lanes_of(lse.shape)
    high = lse.astype(BF).astype(F32)
    rest = lse - high
    mid = rest.astype(BF).astype(F32)
    low = rest - mid
    kept = jnp.where(lane < 8, high, jnp.where(lane < 16, mid, jnp.where(lane < 24, low, 0.0)))
    return kept.astype(BF)


def attend_kernel(meta_ref, vis_ref, near_ref, far_ref, kt_ref, va_ref, out_ref, list_ref, q_s):
    count = meta_ref[0]
    own, core, column = meta_ref[1], meta_ref[2], meta_ref[3]
    seen = jnp.int32(0)
    for e in range(NZ):
        region = e * NX + column
        list_ref[seen] = jnp.int32(e)
        sees = (vis_ref[region] > 0) | (region == own)
        seen = seen + sees.astype(jnp.int32)
    last = list_ref[jnp.maximum(seen - 1, 0)]
    for k in range(3):
        list_ref[seen + k] = last

    lane = lanes_of((LR, 128))
    out_ref[:, :, :D] = jnp.zeros((NZ, LR, D), BF)
    out_ref[:, :, D:] = jnp.broadcast_to(
        jnp.where(lane < 8, NEG, 0.0).astype(BF)[None], (NZ, LR, 128)
    )

    def group(g, blocks):
        keys = blocks * BLK
        entries = [list_ref[4 * g + k] for k in range(4)]
        for k, e in enumerate(entries):
            region = e * NX + column
            q_s[pl.ds(pl.multiple_of(32 * k + 16 * core, 16), 16), :] = near_ref[region]
            q_s[pl.ds(pl.multiple_of(32 * k + 16 - 16 * core, 16), 16), :] = far_ref[region]
        wide = lanes_of((128, 128))
        low_half = wide < DH
        odd_live = lax.rem(count, 2) == 0

        def pair(p, stats):
            here = pl.ds(pl.multiple_of(128 * p, 128), 128)
            even_at = pl.ds(pl.multiple_of(256 * p, 128), 128)
            odd_at = pl.ds(pl.multiple_of(256 * p + 128, 128), 128)
            qp = q_s[:, here]
            zero = jnp.zeros_like(qp)
            both = jnp.concatenate([jnp.where(low_half, qp, zero), jnp.where(low_half, zero, qp)], 0)
            scores = jnp.dot(both, kt_ref[here, :keys], preferred_element_type=F32)
            tail = jnp.where(odd_live, scores[:, keys - BLK :], NEG)
            scores = jnp.concatenate([scores[:, : keys - BLK], tail], 1)
            peak = jnp.max(scores, axis=-1, keepdims=True)
            weights = jnp.exp(scores - peak).astype(BF)
            even = jnp.dot(weights[:128], va_ref[:keys, even_at], preferred_element_type=F32)
            odd = jnp.dot(weights[128:], va_ref[:keys, odd_at], preferred_element_type=F32)
            total = pltpu.roll(jnp.where(low_half, odd, even), DH, 1)
            value = (jnp.where(low_half, even, odd) / total).astype(BF)
            lse = jnp.where(low_half, peak[:128], peak[128:]) + jnp.log(total)
            turned = pltpu.roll(lse, DH, 1)
            within = wide & 7
            stats = jnp.where(within == 2 * p, lse, jnp.where(within == 2 * p + 1, turned, stats))
            for k, e in enumerate(entries):
                out_ref[e, :, here] = value[32 * k : 32 * (k + 1)]
            return stats

        unroll = 2 if blocks == 8 else 1

        def pairs(i, stats):
            for k in range(unroll):
                stats = pair(i * unroll + k, stats)
            return stats

        stats = lax.fori_loop(0, H // 2 // unroll, pairs, jnp.zeros((128, 128), F32))
        packed = pack_stats(stats)
        for k, e in enumerate(entries):
            out_ref[e, :, D:] = packed[32 * k : 32 * (k + 1)]

    groups = (seen + 3) // 4
    for half in range(1, 5):

        @pl.when((count + 1) // 2 == half)
        def _():
            def body(g, carry):
                group(g, 2 * half)
                return carry

            lax.fori_loop(0, groups, body, 0)


def attend(meta, seen_by, near, far, keys_t, values):
    scalars = pl.BlockSpec(memory_space=pltpu.SMEM)
    vectors = pl.BlockSpec(memory_space=pltpu.VMEM)
    return pl.pallas_call(
        attend_kernel,
        out_shape=jax.ShapeDtypeStruct((NZ, LR, WIDE), BF),
        in_specs=[scalars] * 2 + [vectors] * 4,
        out_specs=vectors,
        scratch_shapes=[pltpu.SMEM((16,), jnp.int32), pltpu.VMEM((128, D), BF)],
        compiler_params=pltpu.CompilerParams(vmem_limit_bytes=20 << 20),
        cost_estimate=pl.CostEstimate(flops=2 << 30, bytes_accessed=8 << 20, transcendentals=2 << 20),
        name="attend",
    )(meta, seen_by, near, far, keys_t, values)


def spread_matrix():
    row = lax.broadcasted_iota(jnp.int32, (128, WIDE), 0)
    col = lax.broadcasted_iota(jnp.int32, (128, WIDE), 1)
    head = jnp.where(col < D, col // DH, jnp.where(col < D + 24, col & 7, -1))
    return jnp.where((row < 24) & ((row & 7) == head), 1.0, 0.0).astype(BF)


def join(pieces, spread):
    lses = [jnp.dot(p[:, D:], spread, preferred_element_type=F32) for p in pieces]
    highest = functools.reduce(jnp.maximum, lses)
    scales = [jnp.exp(l - highest) for l in lses]
    total = functools.reduce(jnp.add, scales)
    value = functools.reduce(
        jnp.add, [p[:, :D].astype(F32) * s[:, :D] for p, s in zip(pieces, scales)]
    )
    return value / total[:, :D], (highest + jnp.log(total))[:, D:]


def join_kernel(*refs):
    *ins, out = refs
    pieces = [r[...] for r in ins] if len(ins) > 1 else [ins[0][k] for k in range(ins[0].shape[0])]
    value, lse = join(pieces, spread_matrix())
    out[..., :D] = jnp.broadcast_to(value.astype(BF), (*out.shape[:-1], D))
    out[..., D:] = jnp.broadcast_to(pack_stats(lse), (*out.shape[:-1], 128))


def joined(pieces, shape):
    return pl.pallas_call(
        join_kernel,
        out_shape=jax.ShapeDtypeStruct(shape, BF),
        in_specs=[pl.BlockSpec(memory_space=pltpu.VMEM)] * len(pieces),
        out_specs=pl.BlockSpec(memory_space=pltpu.VMEM),
        compiler_params=pltpu.CompilerParams(vmem_limit_bytes=16 << 20),
        name="join_pieces",
    )(*pieces)


def final_kernel(row_ref, pieces_ref, lat_ref, gain_ref, wo_ref, *refs):
    weights, (res_ref, part_ref, sums) = refs[:4], refs[4:]
    pieces = [pieces_ref[k] for k in range(8)]
    value, _ = join(pieces, spread_matrix())
    attended = value.astype(BF)
    residual = lat_ref[...].astype(F32) + jnp.dot(attended, wo_ref[...], preferred_element_type=F32)
    normed = norm_rows(residual, gain_ref[...]).astype(BF)
    res_ref[...] = residual
    for k, w in enumerate(weights):
        v = jnp.dot(normed, w[:, :256], preferred_element_type=F32)
        hidden = jax.nn.gelu(v, approximate=True).astype(BF)
        down = jnp.concatenate([w[:256, 256:], w[256:, 256:]], 1)
        sums[lax.rem(row_ref[0] - k + 4, 4)] = jnp.dot(hidden, down, preferred_element_type=F32)
    part_ref[...] = (sums[0] + sums[1]) + (sums[2] + sums[3])


def shifted_x(a, by):
    pairs = [
        (zz * NX + xx, zz * NX + (xx + by) % NX) for zz in range(NZ) for xx in range(NX)
    ]
    return lax.ppermute(a, "region", pairs) if by % NX else a


def shifted_y(a, by):
    return lax.ppermute(a, "tm", [(k, (k + 2 * by) % 8) for k in range(8)]) if by % 4 else a


def core_swapped(a):
    return lax.ppermute(a, "tm", [(k, k ^ 1) for k in range(8)])


def on_device(
    observations,
    counts,
    visible,
    latents,
    lat_gain,
    mlp_gain,
    w_query,
    w_keyval,
    w_out,
    w_up,
    w_down,
):
    own = lax.axis_index("region")
    slot = lax.axis_index("tm")
    x, row, core = own % NX, slot // 2, slot % 2
    observed = observations[0, 0]
    lat = latents[0]
    scalars = pl.BlockSpec(memory_space=pltpu.SMEM)
    vectors = pl.BlockSpec(memory_space=pltpu.VMEM)

    with jax.named_scope("queries"):
        q = pl.pallas_call(
            query_kernel,
            out_shape=jax.ShapeDtypeStruct((NZ * NX, 16, D), BF),
            in_specs=[scalars] + [vectors] * 3,
            out_specs=vectors,
            scratch_shapes=[pltpu.VMEM((LR, D), BF)],
            name="queries",
        )(core[None], lat, lat_gain[None], w_query)
    with jax.named_scope("gather"):
        near = lax.all_to_all(q, "region", 0, 0, tiled=True)
        far = core_swapped(near)

    with jax.named_scope("weights"):
        mlp = jnp.concatenate([w_up, jnp.concatenate([w_down[:, :256], w_down[:, 256:]], 0)], 1)
        shards = [shifted_y(mlp, k) for k in range(4)]

    with jax.named_scope("keyval"):
        keys_t = lax.dot_general(
            w_keyval[:, :D], observed, (((0,), (1,)), ((), ())), preferred_element_type=F32
        ).astype(BF)
        wv = w_keyval[:, D:].reshape(D, H // 2, 2, DH)
        gap = jnp.zeros((D, H // 2, DH), BF)
        wide = jnp.concatenate([wv[:, :, 0], gap, gap, wv[:, :, 1]], -1).reshape(D, 2 * D)
        place = lax.iota(jnp.int32, 2 * D) % 256
        ones = jnp.where((place >= DH) & (place < 3 * DH), 1.0, 0.0)
        values = (jnp.dot(observed, wide, preferred_element_type=F32) + ones).astype(BF)

    seen_by = lax.dynamic_slice_in_dim(visible, own, 1, 1)[:, 0]
    with jax.named_scope("attend"):
        pieces = []
        for d in (2, 1, 3, 0):
            meta = jnp.stack([counts[0, 0], own, core, (x - d) % NX]).astype(jnp.int32)
            if d == 0:
                meta, *shards = lax.optimization_barrier((meta, *shards))
            part = attend(meta, seen_by, near, far, keys_t, values)
            pieces.append(shifted_x(part.reshape(NZ * LR, WIDE), -d))
    with jax.named_scope("join_x"):
        part = joined(pieces, (NZ * LR, WIDE)).reshape(NZ, LR, WIDE)
    with jax.named_scope("join_z"):
        groups = [[zz * NX + xx for zz in range(NZ)] for xx in range(NX)]
        part = lax.all_to_all(part, "region", 0, 0, axis_index_groups=groups, tiled=True)
        part = joined([part], (8, LR, WIDE))
    with jax.named_scope("join_t"):
        pieces = lax.all_to_all(part, "tm", 0, 0, tiled=True)
    with jax.named_scope("final"):
        residual, mine = pl.pallas_call(
            final_kernel,
            out_shape=[jax.ShapeDtypeStruct((LR, D), F32)] * 2,
            in_specs=[scalars] + [vectors] * 8,
            out_specs=[vectors] * 2,
            scratch_shapes=[pltpu.VMEM((4, LR, D), F32)],
            compiler_params=pltpu.CompilerParams(vmem_limit_bytes=16 << 20),
            name="final",
        )(row[None], pieces, lat, mlp_gain[None], w_out, *shards)
        out = residual + (mine + core_swapped(mine))
    return out.astype(BF)[None]


def solution(mesh):
    placed = (
        P("region", "tm", None, None),
        P("region", "tm"),
        P(),
        P("region", None, None),
        P(),
        P(),
        P(),
        P(),
        P(),
        P(None, "tm"),
        P("tm", None),
    )
    return jax.shard_map(
        on_device, mesh=mesh, in_specs=placed, out_specs=P("region", None, None), check_vma=False
    )
```

profile of v0, /device:TPU:1, one launch (start us, length us, event | category | flops | bytes accessed | tf_op | source)
XLA Modules:
  0.0 115.2 jit_solution(8916720028253904024)
XLA Ops:
  0.0 1.1 fusion.12
  1.1 1.0 maximum_maximum_fusion.refs_0_
  2.1 3.6 %collective-permute-start.6 = (bf16[512,512]{1,0:T(8,128)(2,1)S(1)}, bf16[512,512]{1,0:T(8,128)(2,1)}, u32[]{:S(2)}, u32[]{:S(2)}) collective-permute-start(bf16[512,512]{1,0:T(8,128)(2,1)S(1)} %maximum_maximum_fusion.refs_0_), channel_id=1, source_target_pairs={{0,6},{1,7},{2,0},{3,1},{4,2},{5,3},{6,4},{7,5},{8,14},{9,15},{10,... | collective-permute-start | bytes 1572872 | tf_op jit(solution)/shard_map/weights/ppermute | solution.py:210
  5.8 0.3 collective-permute-start.5
  6.1 0.7 collective-permute-start.4
  6.8 2.3 %queries.1 = bf16[32,16,512]{2,1,0:T(8,128)(2,1)} custom-call(s32[1]{0:T(128)} %bitcast.3.half_ref, bf16[32,512]{1,0:T(8,128)(2,1)} %bitcast.36, f32[1,512]{1,0:T(1,128)} %bitcast.45, bf16[512,512]{1,0:T(8,128)(2,1)} %wq_ref.1), custom_call_target="tpu_custom_call" | custom-call | tf_op jit(solution)/shard_map/queries/queries/pallas_call | solution.py:239
  9.1 11.0 %all-to-all-start = ((bf16[32,16,512]{2,1,0:T(8,128)(2,1)}), bf16[32,16,512]{2,1,0:T(8,128)(2,1)S(1)}, u32[]{:S(2)}, u32[]{:S(2)}) async-start(bf16[32,16,512]{2,1,0:T(8,128)(2,1)} %queries.1), calls=%async_computation | async-start | bytes 1048576 | tf_op jit(solution)/shard_map/gather/all_to_all | solution.py:248
  20.8 1.9 %slice.19 = bf16[512,512]{1,0:T(8,128)(2,1)} slice(bf16[512,1024]{1,0:T(8,128)(2,1)} %param.18), slice={[0:512], [512:1024]} | slice | bytes 1048576 | tf_op jit(solution)/shard_map/keyval/slice | solution.py:259
  22.7 2.0 %copy.18 = bf16[512,512]{0,1:T(8,128)(2,1)} copy(bf16[512,512]{1,0:T(8,128)(2,1)} %slice.19) | data formatting | bytes 1048576
  24.8 1.8 %slice_bitcast_fusion.1 = (bf16[512,4,64]{0,2,1:T(8,128)(2,1)}, bf16[512,4,64]{0,2,1:T(8,128)(2,1)S(1)}) fusion(bf16[512,4,2,64]{0,3,2,1:T(8,128)(2,1)} %bitcast.43), kind=kLoop, calls=%fused_computation.9 | loop fusion | bytes 1048576 | tf_op jit(solution)/shard_map/keyval/squeeze | solution.py:261
  26.5 2.0 %copy.14 = bf16[512,4,64]{2,1,0:T(4,128)(2,1)} copy(bf16[512,4,64]{0,2,1:T(8,128)(2,1)} %get-tuple-element.21) | data formatting | bytes 524288 | tf_op jit(solution)/shard_map/keyval/squeeze | solution.py:261
  28.5 1.1 copy.15
  29.6 0.1 pad.16.clone
  29.7 2.1 %pad_maximum_fusion = bf16[512,4,256]{2,1,0:T(4,128)(2,1)S(1)} fusion(bf16[512,4,64]{2,1,0:T(4,128)(2,1)} %copy.15, bf16[512,4,64]{2,1,0:T(4,128)(2,1)} %copy.14, bf16[256]{0:T(256)(128)(2,1)S(1)} %pad.16.clone), kind=kLoop, calls=%fused_computation.5 | loop fusion | flops 3145728 | bytes 1573376 | tf_op jit(solution)/shard_map/keyval/concatenate | solution.py:261
  31.8 1.2 %copy.19 = bf16[64,8,4,256]{3,1,2,0:T(8,128)(2,1)} copy(bf16[64,8,4,256]{3,2,1,0:T(4,128)(2,1)S(1)} %bitcast.42) | data formatting | bytes 2097152
  33.0 0.2 dynamic-slice_reduce_fusion.vis_ref
  33.2 0.1 pad_add_fusion.4
  33.2 0.1 pad_add_fusion.3
  33.3 3.7 %convolution_convert_fusion.kt_ref = bf16[512,2048]{1,0:T(8,128)(2,1)} fusion(bf16[1,1,2048,512]{3,2,1,0:T(8,128)(2,1)S(1)} %copy-done, bf16[512,1024]{1,0:T(8,128)(2,1)} %param.18), kind=kOutput, calls=%fused_computation.2 | convolution fusion | flops 1074790400 | bytes 4718592 | tf_op jit(solution)/shard_map/keyval/dot_general | solution.py:256
  37.0 0.0 all-to-all-done.near_ref
  37.0 1.9 %collective-permute-start = (bf16[32,16,512]{2,1,0:T(8,128)(2,1)S(1)}, bf16[32,16,512]{2,1,0:T(8,128)(2,1)S(1)}, u32[]{:S(2)}, u32[]{:S(2)}) collective-permute-start(bf16[32,16,512]{2,1,0:T(8,128)(2,1)S(1)} %all-to-all-done.near_ref), channel_id=1, source_target_pairs={{0,1},{1,0},{2,3},{3,2},{4,5},{5,4},{6,7},{7,6},{8,9},{9,8},{10,11... | collective-permute-start | bytes 1572872 | tf_op jit(solution)/shard_map/gather/ppermute | solution.py:214
  38.9 3.7 %fusion.va_ref = bf16[2048,1024]{1,0:T(8,128)(2,1)S(1)} fusion(f32[1024]{0:T(1024)S(1)} %fusion.10, bf16[512,1024]{1,0:T(8,128)(2,1)} %bitcast.44, bf16[1,1,2048,512]{3,2,1,0:T(8,128)(2,1)S(1)} %copy-done), kind=kOutput, calls=%fused_computation.1 | convolution fusion | flops 2151677952 | bytes 7344128 | tf_op jit(solution)/shard_map/keyval/dot_general | solution.py:264
  42.7 0.0 collective-permute-done.far_ref
  42.7 5.6 %attend.5 = bf16[8,32,640]{2,1,0:T(8,128)(2,1)S(1)} custom-call(s32[4]{0:T(128)S(1)} %get-tuple-element.26.meta_ref, s32[32]{0:T(128)S(1)} %dynamic-slice_reduce_fusion.vis_ref, bf16[32,16,512]{2,1,0:T(8,128)(2,1)S(1)} %all-to-all-done.near_ref, bf16[32,16,512]{2,1,0:T(8,128)(2,1)S(1)} %collective-permute-done.far_ref, bf16[512,2048]{1,0:T(8,128)(2,1)S(1)} %copy-done.4, ...), custom_call_target="tpu_custom_call" | custom-call | flops 2147483648 | bytes 8388608 | tf_op jit(solution)/shard_map/attend/attend/pallas_call | solution.py:137
  48.3 0.3 collective-permute-start.2
  48.6 5.4 %attend.4 = bf16[8,32,640]{2,1,0:T(8,128)(2,1)S(1)} custom-call(s32[4]{0:T(128)S(1)} %get-tuple-element.27.meta_ref, s32[32]{0:T(128)S(1)} %dynamic-slice_reduce_fusion.vis_ref, bf16[32,16,512]{2,1,0:T(8,128)(2,1)S(1)} %all-to-all-done.near_ref, bf16[32,16,512]{2,1,0:T(8,128)(2,1)S(1)} %collective-permute-done.far_ref, bf16[512,2048]{1,0:T(8,128)(2,1)S(1)} %copy-done.4, ...), custom_call_target="tpu_custom_call" | custom-call | flops 2147483648 | bytes 8388608 | tf_op jit(solution)/shard_map/attend/attend/pallas_call | solution.py:137
  54.0 0.7 collective-permute-start.1
  54.6 3.0 %attend.6 = bf16[8,32,640]{2,1,0:T(8,128)(2,1)S(1)} custom-call(s32[4]{0:T(128)S(1)} %get-tuple-element.25.meta_ref, s32[32]{0:T(128)S(1)} %dynamic-slice_reduce_fusion.vis_ref, bf16[32,16,512]{2,1,0:T(8,128)(2,1)S(1)} %all-to-all-done.near_ref, bf16[32,16,512]{2,1,0:T(8,128)(2,1)S(1)} %collective-permute-done.far_ref, bf16[512,2048]{1,0:T(8,128)(2,1)S(1)} %copy-done.4, ...), custom_call_target="tpu_custom_call" | custom-call | flops 2147483648 | bytes 8388608 | tf_op jit(solution)/shard_map/attend/attend/pallas_call | solution.py:137
  57.7 0.0 collective-permute-done.6.refs_3_
  57.7 0.8 collective-permute-start.3
  58.5 0.0 collective-permute-done.5.refs_2_
  58.5 0.0 collective-permute-done.4.refs_1_
  58.5 5.6 %attend.7 = bf16[8,32,640]{2,1,0:T(8,128)(2,1)S(1)} custom-call(s32[4]{0:T(128)S(1)} %get-tuple-element.12.meta_ref, s32[32]{0:T(128)S(1)} %dynamic-slice_reduce_fusion.vis_ref, bf16[32,16,512]{2,1,0:T(8,128)(2,1)S(1)} %all-to-all-done.near_ref, bf16[32,16,512]{2,1,0:T(8,128)(2,1)S(1)} %collective-permute-done.far_ref, bf16[512,2048]{1,0:T(8,128)(2,1)S(1)} %copy-done.4, ...), custom_call_target="tpu_custom_call" | custom-call | flops 2147483648 | bytes 8388608 | tf_op jit(solution)/shard_map/attend/attend/pallas_call | solution.py:137
  64.1 0.0 copy-start.1
  64.1 0.0 copy-start.2
  64.1 0.0 copy-start.3
  64.1 0.0 collective-permute-done.2.refs_1_
  64.1 0.4 collective-permute-done.1.refs_0_
  64.6 7.7 %collective-permute-done.3.refs_2_ = bf16[256,640]{1,0:T(8,128)(2,1)S(1)} collective-permute-done((bf16[256,640]{1,0:T(8,128)(2,1)S(1)}, bf16[256,640]{1,0:T(8,128)(2,1)S(1)}, u32[]{:S(2)}, u32[]{:S(2)}) %collective-permute-start.3) | collective-permute-done | bytes 327712 | tf_op jit(solution)/shard_map/attend/ppermute | solution.py:206
  72.2 1.0 join_pieces.2
  73.3 21.4 %all_to_all.15.refs_0_ = bf16[8,32,640]{2,1,0:T(8,128)(2,1)S(1)} all-to-all(bf16[8,32,640]{2,1,0:T(8,128)(2,1)S(1)} %bitcast.34), channel_id=1, replica_groups={{0,32,64,96,128,160,192,224},{8,40,72,104,136,168,200,232},{16,48,80,11..., dimensions={0} | all-to-all | bytes 655360 | tf_op jit(solution)/shard_map/join_z/all_to_all | solution.py:279
  94.7 1.1 join_pieces.3
  95.8 7.0 %all-to-all-start.2 = ((bf16[8,32,640]{2,1,0:T(8,128)(2,1)}), bf16[8,32,640]{2,1,0:T(8,128)(2,1)S(1)}, u32[]{:S(2)}, u32[]{:S(2)}) async-start(bf16[8,32,640]{2,1,0:T(8,128)(2,1)} %join_pieces.3), calls=%async_computation.2 | async-start | bytes 655360 | tf_op jit(solution)/shard_map/join_t/all_to_all | solution.py:282
  102.8 7.1 %all-to-all-done.2.pieces_ref = bf16[8,32,640]{2,1,0:T(8,128)(2,1)S(1)} async-done(((bf16[8,32,640]{2,1,0:T(8,128)(2,1)}), bf16[8,32,640]{2,1,0:T(8,128)(2,1)S(1)}, u32[]{:S(2)}, u32[]{:S(2)}) %all-to-all-start.2) | async-done | bytes 327712 | tf_op jit(solution)/shard_map/join_t/all_to_all | solution.py:282
  109.9 2.5 %final.1 = (f32[32,512]{1,0:T(8,128)S(1)}, f32[32,512]{1,0:T(8,128)S(1)}) custom-call(s32[1]{0:T(128)} %bitcast.row_ref, bf16[8,32,640]{2,1,0:T(8,128)(2,1)S(1)} %all-to-all-done.2.pieces_ref, bf16[32,512]{1,0:T(8,128)(2,1)S(1)} %bitcast.37, f32[1,512]{1,0:T(1,128)S(1)} %bitcast.38, bf16[512,512]{1,0:T(8,128)(2,1)S(1)} %copy-done.1, ...), custom_call_target="tpu_custom_call" | custom-call | tf_op jit(solution)/shard_map/final/final/pallas_call | solution.py:284
  112.5 1.2 %collective-permute-start.7 = (f32[32,512]{1,0:T(8,128)S(1)}, f32[32,512]{1,0:T(8,128)S(1)}, u32[]{:S(2)}, u32[]{:S(2)}) collective-permute-start(f32[32,512]{1,0:T(8,128)S(1)} %get-tuple-element.18), channel_id=1, source_target_pairs={{0,1},{1,0},{2,3},{3,2},{4,5},{5,4},{6,7},{7,6},{8,9},{9,8},{10,11... | collective-permute-start | bytes 196616 | tf_op jit(solution)/shard_map/final/ppermute | solution.py:214
  113.7 0.9 collective-permute-done.7
  114.6 0.6 fusion.4
  (11 shorter events, 0.0 us)
Async XLA Ops:
  0.0 33.3 %copy-start = (bf16[1,1,2048,512]{3,2,1,0:T(8,128)(2,1)S(1)}, bf16[1,1,2048,512]{3,2,1,0:T(8,128)(2,1)}, u32[]{:S(2)}) copy-start(bf16[1,1,2048,512]{3,2,1,0:T(8,128)(2,1)} %param.11) | copy-start | bytes 6291460
  2.1 55.5 %collective-permute-start.6 = (bf16[512,512]{1,0:T(8,128)(2,1)S(1)}, bf16[512,512]{1,0:T(8,128)(2,1)}, u32[]{:S(2)}, u32[]{:S(2)}) collective-permute-start(bf16[512,512]{1,0:T(8,128)(2,1)S(1)} %maximum_maximum_fusion.refs_0_), channel_id=1, source_target_pairs={{0,6},{1,7},{2,0},{3,1},{4,2},{5,3},{6,4},{7,5},{8,14},{9,15},{10,... | collective-permute-start | bytes 1572872 | tf_op jit(solution)/shard_map/weights/ppermute | solution.py:210
  5.8 52.7 %collective-permute-start.5 = (bf16[512,512]{1,0:T(8,128)(2,1)S(1)}, bf16[512,512]{1,0:T(8,128)(2,1)}, u32[]{:S(2)}, u32[]{:S(2)}) collective-permute-start(bf16[512,512]{1,0:T(8,128)(2,1)S(1)} %maximum_maximum_fusion.refs_0_), channel_id=1, source_target_pairs={{0,4},{1,5},{2,6},{3,7},{4,0},{5,1},{6,2},{7,3},{8,12},{9,13},{10,... | collective-permute-start | bytes 1572872 | tf_op jit(solution)/shard_map/weights/ppermute | solution.py:210
  6.1 52.3 %collective-permute-start.4 = (bf16[512,512]{1,0:T(8,128)(2,1)S(1)}, bf16[512,512]{1,0:T(8,128)(2,1)}, u32[]{:S(2)}, u32[]{:S(2)}) collective-permute-start(bf16[512,512]{1,0:T(8,128)(2,1)S(1)} %maximum_maximum_fusion.refs_0_), channel_id=1, source_target_pairs={{0,2},{1,3},{2,4},{3,5},{4,6},{5,7},{6,0},{7,1},{8,10},{9,11},{10,... | collective-permute-start | bytes 1572872 | tf_op jit(solution)/shard_map/weights/ppermute | solution.py:210
  9.1 27.9 %all-to-all-start = ((bf16[32,16,512]{2,1,0:T(8,128)(2,1)}), bf16[32,16,512]{2,1,0:T(8,128)(2,1)S(1)}, u32[]{:S(2)}, u32[]{:S(2)}) async-start(bf16[32,16,512]{2,1,0:T(8,128)(2,1)} %queries.1), calls=%async_computation | async-start | bytes 1048576 | tf_op jit(solution)/shard_map/gather/all_to_all | solution.py:248
  29.7 3.3 %copy-start.5 = (s32[32,32]{1,0:T(8,128)S(1)}, s32[32,32]{1,0:T(8,128)}, u32[]{:S(2)}) copy-start(s32[32,32]{1,0:T(8,128)} %param.13) | copy-start | bytes 12292
  37.0 5.6 %collective-permute-start = (bf16[32,16,512]{2,1,0:T(8,128)(2,1)S(1)}, bf16[32,16,512]{2,1,0:T(8,128)(2,1)S(1)}, u32[]{:S(2)}, u32[]{:S(2)}) collective-permute-start(bf16[32,16,512]{2,1,0:T(8,128)(2,1)S(1)} %all-to-all-done.near_ref), channel_id=1, source_target_pairs={{0,1},{1,0},{2,3},{3,2},{4,5},{5,4},{6,7},{7,6},{8,9},{9,8},{10,11... | collective-permute-start | bytes 1572872 | tf_op jit(solution)/shard_map/gather/ppermute | solution.py:214
  38.9 3.7 %copy-start.4 = (bf16[512,2048]{1,0:T(8,128)(2,1)S(1)}, bf16[512,2048]{1,0:T(8,128)(2,1)}, u32[]{:S(2)}) copy-start(bf16[512,2048]{1,0:T(8,128)(2,1)} %convolution_convert_fusion.kt_ref) | copy-start | bytes 6291460
  48.3 15.9 %collective-permute-start.2 = (bf16[256,640]{1,0:T(8,128)(2,1)S(1)}, bf16[256,640]{1,0:T(8,128)(2,1)S(1)}, u32[]{:S(2)}, u32[]{:S(2)}) collective-permute-start(bf16[256,640]{1,0:T(8,128)(2,1)S(1)} %bitcast.39), channel_id=1, source_target_pairs={{0,24},{8,0},{16,8},{24,16},{32,56},{40,32},{48,40},{56,48},{64,88... | collective-permute-start | bytes 983048 | tf_op jit(solution)/shard_map/attend/ppermute | solution.py:206
  54.0 10.6 %collective-permute-start.1 = (bf16[256,640]{1,0:T(8,128)(2,1)S(1)}, bf16[256,640]{1,0:T(8,128)(2,1)S(1)}, u32[]{:S(2)}, u32[]{:S(2)}) collective-permute-start(bf16[256,640]{1,0:T(8,128)(2,1)S(1)} %bitcast.40), channel_id=1, source_target_pairs={{0,16},{8,24},{16,0},{24,8},{32,48},{40,56},{48,32},{56,40},{64,80... | collective-permute-start | bytes 983048 | tf_op jit(solution)/shard_map/attend/ppermute | solution.py:206
  57.7 14.6 %collective-permute-start.3 = (bf16[256,640]{1,0:T(8,128)(2,1)S(1)}, bf16[256,640]{1,0:T(8,128)(2,1)S(1)}, u32[]{:S(2)}, u32[]{:S(2)}) collective-permute-start(bf16[256,640]{1,0:T(8,128)(2,1)S(1)} %bitcast.41), channel_id=1, source_target_pairs={{0,8},{8,16},{16,24},{24,0},{32,40},{40,48},{48,56},{56,32},{64,72... | collective-permute-start | bytes 983048 | tf_op jit(solution)/shard_map/attend/ppermute | solution.py:206
  64.1 45.8 %copy-start.1 = (bf16[512,512]{1,0:T(8,128)(2,1)S(1)}, bf16[512,512]{1,0:T(8,128)(2,1)}, u32[]{:S(2)}) copy-start(bf16[512,512]{1,0:T(8,128)(2,1)} %wo_ref.1) | copy-start | bytes 1572868
  64.1 45.8 %copy-start.2 = (bf16[1,32,512]{2,1,0:T(8,128)(2,1)S(1)}, bf16[1,32,512]{2,1,0:T(8,128)(2,1)}, u32[]{:S(2)}) copy-start(bf16[1,32,512]{2,1,0:T(8,128)(2,1)} %param.14) | copy-start | bytes 98308
  64.1 45.8 %copy-start.3 = (f32[512]{0:T(512)S(1)}, f32[512]{0:T(512)}, u32[]{:S(2)}) copy-start(f32[512]{0:T(512)} %param.16) | copy-start | bytes 6148
  95.8 14.1 %all-to-all-start.2 = ((bf16[8,32,640]{2,1,0:T(8,128)(2,1)}), bf16[8,32,640]{2,1,0:T(8,128)(2,1)S(1)}, u32[]{:S(2)}, u32[]{:S(2)}) async-start(bf16[8,32,640]{2,1,0:T(8,128)(2,1)} %join_pieces.3), calls=%async_computation.2 | async-start | bytes 655360 | tf_op jit(solution)/shard_map/join_t/all_to_all | solution.py:282
  112.5 2.1 %collective-permute-start.7 = (f32[32,512]{1,0:T(8,128)S(1)}, f32[32,512]{1,0:T(8,128)S(1)}, u32[]{:S(2)}, u32[]{:S(2)}) collective-permute-start(f32[32,512]{1,0:T(8,128)S(1)} %get-tuple-element.18), channel_id=1, source_target_pairs={{0,1},{1,0},{2,3},{3,2},{4,5},{5,4},{6,7},{7,6},{8,9},{9,8},{10,11... | collective-permute-start | bytes 196616 | tf_op jit(solution)/shard_map/final/ppermute | solution.py:214
where the time goes:
time: 115 us
  starting transfers between devices  27.6 us (24%)
  Pallas kernels  26.6 us (23%)
  blocking collectives  21.4 us (19%)
  waiting for transfers between devices  16.1 us (14%)
  local copies, waits for them, and re-layouts  11.4 us (10%)
  matrix products  7.41 us (6%)
  other arithmetic  3.84 us (3%)
    all_to_all x1, blocking collectives, on_device(): lax.all_to_all(part, 'region', 0, 0, axis_index_groups=groups, tiled=True)  21.4 us
    pallas_call x4, Pallas kernels, attend(): pl.pallas_call(attend_kernel, out_shape=jax.ShapeDtypeStruct((NZ, LR, WID...  19.6 us
    all_to_all x1, starting transfers between devices, on_device(): near = lax.all_to_all(q, 'region', 0, 0, tiled=True)  11 us
    ppermute x3, waiting for transfers between devices, shifted_x(): return lax.ppermute(a, 'region', pairs) if by % NX else a  8.1 us
    all_to_all x1, waiting for transfers between devices, on_device(): pieces = lax.all_to_all(part, 'tm', 0, 0, tiled=True)  7.12 us
    all_to_all x1, starting transfers between devices, on_device(): pieces = lax.all_to_all(part, 'tm', 0, 0, tiled=True)  6.97 us
    ppermute x3, starting transfers between devices, shifted_y(): lax.ppermute(a, 'tm', [(k, (k + 2 * by) % 8) for k in range(8)])  4.68 us
    squeeze x2, local copies, waits for them, and re-layouts, on_device(): wv[:, :, 0]  3.79 us
  transfers between devices with their start and end apart: 10, of which 4 were waited for; matrix products, arithmetic and copies ran while one was open for 17% of the time, Pallas kernels for 19%

commit v1 on v0

--- a/solution.py
+++ b/solution.py
@@ -43,6 +43,23 @@
     out_ref[...] = jnp.broadcast_to(rows[None], out_ref.shape)
 
 
+def keyval_kernel(obs_ref, w_ref, up_ref, down_ref, k_ref, va_ref, mlp_ref):
+    @pl.when(pl.program_id(0) == 0)
+    def _():
+        mlp_ref[:, :256] = up_ref[...]
+        mlp_ref[:256, 256:] = down_ref[:, :256]
+        mlp_ref[256:, 256:] = down_ref[:, 256:]
+
+    kv = jnp.dot(obs_ref[...], w_ref[...], preferred_element_type=F32).astype(BF)
+    k_ref[...] = kv[:, :D]
+    low_half = lanes_of((kv.shape[0], 128)) < DH
+    ones = jnp.ones((kv.shape[0], 128), BF)
+    for p in range(H // 2):
+        v = kv[:, D + 128 * p : D + 128 * (p + 1)]
+        va_ref[:, 256 * p : 256 * p + 128] = jnp.where(low_half, v, ones)
+        va_ref[:, 256 * p + 128 : 256 * p + 256] = jnp.where(low_half, ones, v)
+
+
 def pack_stats(lse):
     lane = lanes_of(lse.shape)
     high = lse.astype(BF).astype(F32)
@@ -53,7 +70,7 @@
     return kept.astype(BF)
 
 
-def attend_kernel(meta_ref, vis_ref, near_ref, far_ref, kt_ref, va_ref, out_ref, list_ref, q_s):
+def attend_kernel(meta_ref, vis_ref, near_ref, far_ref, k_ref, va_ref, out_ref, list_ref, q_s):
     count = meta_ref[0]
     own, core, column = meta_ref[1], meta_ref[2], meta_ref[3]
     seen = jnp.int32(0)
@@ -72,34 +89,38 @@
         jnp.where(lane < 8, NEG, 0.0).astype(BF)[None], (NZ, LR, 128)
     )
 
-    def group(g, blocks):
-        keys = blocks * BLK
-        entries = [list_ref[4 * g + k] for k in range(4)]
+    def group(start, regions, blocks, unroll):
+        keys, rows = blocks * BLK, regions * LR
+        entries = [list_ref[start + k] for k in range(regions)]
         for k, e in enumerate(entries):
             region = e * NX + column
             q_s[pl.ds(pl.multiple_of(32 * k + 16 * core, 16), 16), :] = near_ref[region]
             q_s[pl.ds(pl.multiple_of(32 * k + 16 - 16 * core, 16), 16), :] = far_ref[region]
-        wide = lanes_of((128, 128))
+        wide = lanes_of((rows, 128))
         low_half = wide < DH
-        odd_live = lax.rem(count, 2) == 0
+        sure = max(1, blocks // 2 + (blocks > 2))
 
         def pair(p, stats):
             here = pl.ds(pl.multiple_of(128 * p, 128), 128)
             even_at = pl.ds(pl.multiple_of(256 * p, 128), 128)
             odd_at = pl.ds(pl.multiple_of(256 * p + 128, 128), 128)
-            qp = q_s[:, here]
+            qp = q_s[:rows, here]
             zero = jnp.zeros_like(qp)
             both = jnp.concatenate([jnp.where(low_half, qp, zero), jnp.where(low_half, zero, qp)], 0)
-            scores = jnp.dot(both, kt_ref[here, :keys], preferred_element_type=F32)
-            tail = jnp.where(odd_live, scores[:, keys - BLK :], NEG)
-            scores = jnp.concatenate([scores[:, : keys - BLK], tail], 1)
+            scores = lax.dot_general(
+                both, k_ref[:keys, here], (((1,), (1,)), ((), ())), preferred_element_type=F32
+            )
+            parts = [scores[:, : sure * BLK]]
+            for j in range(sure, blocks):
+                parts.append(jnp.where(count > j, scores[:, j * BLK : (j + 1) * BLK], NEG))
+            scores = jnp.concatenate(parts, 1)
             peak = jnp.max(scores, axis=-1, keepdims=True)
             weights = jnp.exp(scores - peak).astype(BF)
-            even = jnp.dot(weights[:128], va_ref[:keys, even_at], preferred_element_type=F32)
-            odd = jnp.dot(weights[128:], va_ref[:keys, odd_at], preferred_element_type=F32)
+            even = jnp.dot(weights[:rows], va_ref[:keys, even_at], preferred_element_type=F32)
+            odd = jnp.dot(weights[rows:], va_ref[:keys, odd_at], preferred_element_type=F32)
             total = pltpu.roll(jnp.where(low_half, odd, even), DH, 1)
             value = (jnp.where(low_half, even, odd) / total).astype(BF)
-            lse = jnp.where(low_half, peak[:128], peak[128:]) + jnp.log(total)
+            lse = jnp.where(low_half, peak[:rows], peak[rows:]) + jnp.log(total)
             turned = pltpu.roll(lse, DH, 1)
             within = wide & 7
             stats = jnp.where(within == 2 * p, lse, jnp.where(within == 2 * p + 1, turned, stats))
@@ -107,31 +128,34 @@
                 out_ref[e, :, here] = value[32 * k : 32 * (k + 1)]
             return stats
 
-        unroll = 2 if blocks == 8 else 1
-
         def pairs(i, stats):
             for k in range(unroll):
                 stats = pair(i * unroll + k, stats)
             return stats
 
-        stats = lax.fori_loop(0, H // 2 // unroll, pairs, jnp.zeros((128, 128), F32))
+        stats = lax.fori_loop(0, H // 2 // unroll, pairs, jnp.zeros((rows, 128), F32))
         packed = pack_stats(stats)
         for k, e in enumerate(entries):
             out_ref[e, :, D:] = packed[32 * k : 32 * (k + 1)]
 
-    groups = (seen + 3) // 4
-    for half in range(1, 5):
-
-        @pl.when((count + 1) // 2 == half)
+    for least, blocks in ((1, 2), (3, 4)):
+
+        @pl.when((count >= least) & (count <= blocks))
         def _():
             def body(g, carry):
-                group(g, 2 * half)
+                group(4 * g, 4, blocks, 1)
                 return carry
 
-            lax.fori_loop(0, groups, body, 0)
-
-
-def attend(meta, seen_by, near, far, keys_t, values):
+            lax.fori_loop(0, (seen + 3) // 4, body, 0)
+
+    for fewest, regions, unroll in ((1, 4, 1), (5, 6, 2), (7, 8, 1)):
+
+        @pl.when((count > 4) & (seen >= fewest) & (seen <= regions))
+        def _():
+            group(0, regions, 8, unroll)
+
+
+def attend(meta, seen_by, near, far, keys, values):
     scalars = pl.BlockSpec(memory_space=pltpu.SMEM)
     vectors = pl.BlockSpec(memory_space=pltpu.VMEM)
     return pl.pallas_call(
@@ -139,11 +163,11 @@
         out_shape=jax.ShapeDtypeStruct((NZ, LR, WIDE), BF),
         in_specs=[scalars] * 2 + [vectors] * 4,
         out_specs=vectors,
-        scratch_shapes=[pltpu.SMEM((16,), jnp.int32), pltpu.VMEM((128, D), BF)],
-        compiler_params=pltpu.CompilerParams(vmem_limit_bytes=20 << 20),
+        scratch_shapes=[pltpu.SMEM((16,), jnp.int32), pltpu.VMEM((256, D), BF)],
+        compiler_params=pltpu.CompilerParams(vmem_limit_bytes=24 << 20),
         cost_estimate=pl.CostEstimate(flops=2 << 30, bytes_accessed=8 << 20, transcendentals=2 << 20),
         name="attend",
-    )(meta, seen_by, near, far, keys_t, values)
+    )(meta, seen_by, near, far, keys, values)
 
 
 def spread_matrix():
@@ -246,22 +270,37 @@
         )(core[None], lat, lat_gain[None], w_query)
     with jax.named_scope("gather"):
         near = lax.all_to_all(q, "region", 0, 0, tiled=True)
+
+    with jax.named_scope("keyval"):
+        keys, values, mlp = pl.pallas_call(
+            keyval_kernel,
+            grid=(observed.shape[0] // BLK,),
+            out_shape=[
+                jax.ShapeDtypeStruct((observed.shape[0], D), BF),
+                jax.ShapeDtypeStruct((observed.shape[0], 2 * D), BF),
+                jax.ShapeDtypeStruct((D, D), BF),
+            ],
+            in_specs=[
+                pl.BlockSpec((BLK, D), lambda i: (i, 0)),
+                pl.BlockSpec((D, 2 * D), lambda i: (0, 0)),
+                pl.BlockSpec((D, 256), lambda i: (0, 0)),
+                pl.BlockSpec((256, D), lambda i: (0, 0)),
+            ],
+            out_specs=[
+                pl.BlockSpec((BLK, D), lambda i: (i, 0)),
+                pl.BlockSpec((BLK, 2 * D), lambda i: (i, 0)),
+                pl.BlockSpec((D, D), lambda i: (0, 0)),
+            ],
+            compiler_params=pltpu.CompilerParams(vmem_limit_bytes=16 << 20),
+            cost_estimate=pl.CostEstimate(flops=2 << 30, bytes_accessed=9 << 20, transcendentals=0),
+            name="keyval",
+        )(observed, w_keyval, w_up, w_down)
+
+    near, values = lax.optimization_barrier((near, values))
+    with jax.named_scope("gather"):
         far = core_swapped(near)
-
     with jax.named_scope("weights"):
-        mlp = jnp.concatenate([w_up, jnp.concatenate([w_down[:, :256], w_down[:, 256:]], 0)], 1)
         shards = [shifted_y(mlp, k) for k in range(4)]
-
-    with jax.named_scope("keyval"):
-        keys_t = lax.dot_general(
-            w_keyval[:, :D], observed, (((0,), (1,)), ((), ())), preferred_element_type=F32
-        ).astype(BF)
-        wv = w_keyval[:, D:].reshape(D, H // 2, 2, DH)
-        gap = jnp.zeros((D, H // 2, DH), BF)
-        wide = jnp.concatenate([wv[:, :, 0], gap, gap, wv[:, :, 1]], -1).reshape(D, 2 * D)
-        place = lax.iota(jnp.int32, 2 * D) % 256
-        ones = jnp.where((place >= DH) & (place < 3 * DH), 1.0, 0.0)
-        values = (jnp.dot(observed, wide, preferred_element_type=F32) + ones).astype(BF)
 
     seen_by = lax.dynamic_slice_in_dim(visible, own, 1, 1)[:, 0]
     with jax.named_scope("attend"):
@@ -270,7 +309,7 @@
             meta = jnp.stack([counts[0, 0], own, core, (x - d) % NX]).astype(jnp.int32)
             if d == 0:
                 meta, *shards = lax.optimization_barrier((meta, *shards))
-            part = attend(meta, seen_by, near, far, keys_t, values)
+            part = attend(meta, seen_by, near, far, keys, values)
             pieces.append(shifted_x(part.reshape(NZ * LR, WIDE), -d))
     with jax.named_scope("join_x"):
         part = joined(pieces, (NZ * LR, WIDE)).reshape(NZ, LR, WIDE)

time: 115 us -> 104 us (0.904)
  blocking collectives: 21.4 us -> 12.7 us
  matrix products: 7.41 us -> 0 us
  starting transfers between devices: 27.6 us -> 34.8 us
  waiting for transfers between devices: 16.1 us -> 19.2 us
  other arithmetic: 3.84 us -> 0.78 us
  Pallas kernels: 26.6 us -> 24.5 us
    all_to_all x1, blocking collectives: 21.4 us -> 12.7 us  [on_device(): lax.all_to_all(part, 'region', 0, 0, axis_index_groups=groups, tiled=True)]
    dot_general x2 -> x0, matrix products: 7.41 us -> none  [the longest x1 3.71 us: on_device(): jnp.dot(observed, wide, preferred_element_type=F32) + ones]
    unnamed x14 -> x24, local copies, waits for them, and re-layouts: 3.28 us -> 10.2 us
    ppermute x3, starting transfers between devices: 1.73 us -> 7.88 us  [shifted_x(): return lax.ppermute(a, 'region', pairs) if by % NX else a]
    all_to_all x1, waiting for transfers between devices: 0.01 us -> 6.09 us  [on_device(): near = lax.all_to_all(q, 'region', 0, 0, tiled=True)]
    squeeze x3 -> x0, local copies, waits for them, and re-layouts: 4.86 us -> none  [the longest x2 3.79 us: on_device(): wv[:, :, 0]]
    pallas_call x4, Pallas kernels: 19.6 us -> 14.9 us  [attend(): pl.pallas_call(attend_kernel, out_shape=jax.ShapeDtypeStruct((NZ, LR, WID...]
    ppermute x3, waiting for transfers between devices: 8.1 us -> 4.13 us  [shifted_x(): return lax.ppermute(a, 'region', pairs) if by % NX else a]
  transfers between devices with their start and end apart: 10 -> 10, of which waited for: 4 -> 5; matrix products, arithmetic and copies ran while one was open for 17% -> 0% of each run, Pallas kernels for 19% -> 18%
where the time goes in v1:
time: 104 us; the launch traced here: 103 us
  starting transfers between devices  34.8 us (33%)
  Pallas kernels  24.5 us (24%)
  waiting for transfers between devices  19.2 us (18%)
  blocking collectives  12.7 us (12%)
  local copies, waits for them, and re-layouts  10.4 us (10%)
    pallas_call x4, Pallas kernels, attend(): pl.pallas_call(attend_kernel, out_shape=jax.ShapeDtypeStruct((NZ, LR, WID...  14.9 us
    all_to_all x1, blocking collectives, on_device(): lax.all_to_all(part, 'region', 0, 0, axis_index_groups=groups, tiled=True)  12.7 us
    all_to_all x1, starting transfers between devices, on_device(): near = lax.all_to_all(q, 'region', 0, 0, tiled=True)  11.9 us
    unnamed x24, local copies, waits for them, and re-layouts  10.2 us
    ppermute x3, starting transfers between devices, shifted_x(): return lax.ppermute(a, 'region', pairs) if by % NX else a  7.88 us
    all_to_all x1, starting transfers between devices, on_device(): pieces = lax.all_to_all(part, 'tm', 0, 0, tiled=True)  7.7 us
    all_to_all x1, waiting for transfers between devices, on_device(): pieces = lax.all_to_all(part, 'tm', 0, 0, tiled=True)  7.12 us
    all_to_all x1, waiting for transfers between devices, on_device(): near = lax.all_to_all(q, 'region', 0, 0, tiled=True)  6.09 us
  transfers between devices with their start and end apart: 10, of which 5 were waited for; matrix products, arithmetic and copies ran while one was open for 0% of the time, Pallas kernels for 18%

profile of v1, /device:TPU:1, one launch (start us, length us, event | category | flops | bytes accessed | tf_op | source)
XLA Modules:
  0.0 103.2 jit_solution(7292288441847860786)
XLA Ops:
  0.0 0.0 copy-start
  0.0 2.4 %queries.1 = bf16[32,16,512]{2,1,0:T(8,128)(2,1)} custom-call(s32[1]{0:T(128)} %bitcast.3.half_ref, bf16[32,512]{1,0:T(8,128)(2,1)} %bitcast.22, f32[1,512]{1,0:T(1,128)} %bitcast.29, bf16[512,512]{1,0:T(8,128)(2,1)} %wq_ref.1), custom_call_target="tpu_custom_call" | custom-call | tf_op jit(solution)/shard_map/queries/queries/pallas_call | solution.py:263
  2.4 11.9 %all-to-all-start = ((bf16[32,16,512]{2,1,0:T(8,128)(2,1)}), bf16[32,16,512]{2,1,0:T(8,128)(2,1)S(1)}, u32[]{:S(2)}, u32[]{:S(2)}) async-start(bf16[32,16,512]{2,1,0:T(8,128)(2,1)} %queries.1), calls=%async_computation | async-start | bytes 1048576 | tf_op jit(solution)/shard_map/gather/all_to_all | solution.py:272
  14.3 0.0 copy-done.4
  14.3 0.0 copy-start.5
  14.3 1.2 %copy-done.5 = bf16[512,1024]{1,0:T(8,128)(2,1)S(1)} copy-done((bf16[512,1024]{1,0:T(8,128)(2,1)S(1)}, bf16[512,1024]{1,0:T(8,128)(2,1)}, u32[]{:S(2)}) %copy-start.5) | copy-done | bytes 1048600
  15.5 0.9 copy-done.6
  16.5 0.9 copy-done.7
  17.4 3.8 %keyval.1 = (bf16[2048,512]{1,0:T(8,128)(2,1)S(1)}, bf16[2048,1024]{1,0:T(8,128)(2,1)S(1)}, bf16[512,512]{1,0:T(8,128)(2,1)S(1)}) custom-call(bf16[2048,512]{1,0:T(8,128)(2,1)S(1)} %bitcast.25, bf16[512,1024]{1,0:T(8,128)(2,1)S(1)} %copy-done.5, bf16[512,256]{1,0:T(8,128)(2,1)S(1)} %copy-done.6, bf16[256,512]{1,0:T(8,128)(2,1)S(1)} %copy-done.7), custom_call_target="tpu_custom_call" | custom-call | flops 2147483648 | bytes 9437184 | tf_op jit(solution)/shard_map/keyval/keyval/pallas_call | solution.py:275
  21.2 1.9 %copy-done.8 = bf16[2048,1024]{1,0:T(8,128)(2,1)} copy-done((bf16[2048,1024]{1,0:T(8,128)(2,1)}, bf16[2048,1024]{1,0:T(8,128)(2,1)S(1)}, u32[]{:S(2)}) %copy-start.8) | copy-done | bytes 4194328
  23.1 1.3 %copy-done.10 = bf16[2048,512]{1,0:T(8,128)(2,1)} copy-done((bf16[2048,512]{1,0:T(8,128)(2,1)}, bf16[2048,512]{1,0:T(8,128)(2,1)S(1)}, u32[]{:S(2)}) %copy-start.10) | copy-done | bytes 2097176
  24.5 6.1 %all-to-all-done.near_ref = bf16[32,16,512]{2,1,0:T(8,128)(2,1)S(1)} async-done(((bf16[32,16,512]{2,1,0:T(8,128)(2,1)}), bf16[32,16,512]{2,1,0:T(8,128)(2,1)S(1)}, u32[]{:S(2)}, u32[]{:S(2)}) %all-to-all-start) | async-done | bytes 524320 | tf_op jit(solution)/shard_map/gather/all_to_all | solution.py:272
  30.6 2.4 %collective-permute-start = (bf16[32,16,512]{2,1,0:T(8,128)(2,1)S(1)}, bf16[32,16,512]{2,1,0:T(8,128)(2,1)S(1)}, u32[]{:S(2)}, u32[]{:S(2)}) collective-permute-start(bf16[32,16,512]{2,1,0:T(8,128)(2,1)S(1)} %all-to-all-done.near_ref), channel_id=1, source_target_pairs={{0,1},{1,0},{2,3},{3,2},{4,5},{5,4},{6,7},{7,6},{8,9},{9,8},{10,11... | collective-permute-start | bytes 1572872 | tf_op jit(solution)/shard_map/gather/ppermute | solution.py:238
  33.0 2.7 %collective-permute-start.6 = (bf16[512,512]{1,0:T(8,128)(2,1)S(1)}, bf16[512,512]{1,0:T(8,128)(2,1)S(1)}, u32[]{:S(2)}, u32[]{:S(2)}) collective-permute-start(bf16[512,512]{1,0:T(8,128)(2,1)S(1)} %get-tuple-element.23.refs_0_), channel_id=1, source_target_pairs={{0,6},{1,7},{2,0},{3,1},{4,2},{5,3},{6,4},{7,5},{8,14},{9,15},{10,... | collective-permute-start | bytes 1572872 | tf_op jit(solution)/shard_map/weights/ppermute | solution.py:234
  35.7 0.3 collective-permute-start.5
  36.0 0.7 collective-permute-start.4
  37.4 0.2 dynamic-slice_reduce_fusion.vis_ref
  37.6 0.1 pad_add_fusion.4
  37.7 0.1 pad_add_fusion.3
  37.8 0.0 collective-permute-done.far_ref
  37.8 2.2 %copy-done.9 = bf16[2048,1024]{1,0:T(8,128)(2,1)S(1)} copy-done((bf16[2048,1024]{1,0:T(8,128)(2,1)S(1)}, bf16[2048,1024]{1,0:T(8,128)(2,1)}, u32[]{:S(2)}) %copy-start.9) | copy-done | bytes 4194328
  40.0 1.6 %copy-done.11 = bf16[2048,512]{1,0:T(8,128)(2,1)S(1)} copy-done((bf16[2048,512]{1,0:T(8,128)(2,1)S(1)}, bf16[2048,512]{1,0:T(8,128)(2,1)}, u32[]{:S(2)}) %copy-start.11) | copy-done | bytes 2097176
  41.5 5.5 %attend.4 = bf16[8,32,640]{2,1,0:T(8,128)(2,1)S(1)} custom-call(s32[4]{0:T(128)S(1)} %get-tuple-element.33.meta_ref, s32[32]{0:T(128)S(1)} %dynamic-slice_reduce_fusion.vis_ref, bf16[32,16,512]{2,1,0:T(8,128)(2,1)S(1)} %all-to-all-done.near_ref, bf16[32,16,512]{2,1,0:T(8,128)(2,1)S(1)} %collective-permute-done.far_ref, bf16[2048,512]{1,0:T(8,128)(2,1)S(1)} %copy-done.11, ...), custom_call_target="tpu_custom_call" | custom-call | flops 2147483648 | bytes 8388608 | tf_op jit(solution)/shard_map/attend/attend/pallas_call | solution.py:161
  47.1 3.9 %collective-permute-start.1 = (bf16[256,640]{1,0:T(8,128)(2,1)S(1)}, bf16[256,640]{1,0:T(8,128)(2,1)S(1)}, u32[]{:S(2)}, u32[]{:S(2)}) collective-permute-start(bf16[256,640]{1,0:T(8,128)(2,1)S(1)} %bitcast.26), channel_id=1, source_target_pairs={{0,16},{8,24},{16,0},{24,8},{32,48},{40,56},{48,32},{56,40},{64,80... | collective-permute-start | bytes 983048 | tf_op jit(solution)/shard_map/attend/ppermute | solution.py:230
  51.0 3.3 %attend.5 = bf16[8,32,640]{2,1,0:T(8,128)(2,1)S(1)} custom-call(s32[4]{0:T(128)S(1)} %get-tuple-element.32.meta_ref, s32[32]{0:T(128)S(1)} %dynamic-slice_reduce_fusion.vis_ref, bf16[32,16,512]{2,1,0:T(8,128)(2,1)S(1)} %all-to-all-done.near_ref, bf16[32,16,512]{2,1,0:T(8,128)(2,1)S(1)} %collective-permute-done.far_ref, bf16[2048,512]{1,0:T(8,128)(2,1)S(1)} %copy-done.11, ...), custom_call_target="tpu_custom_call" | custom-call | flops 2147483648 | bytes 8388608 | tf_op jit(solution)/shard_map/attend/attend/pallas_call | solution.py:161
  54.2 1.5 %collective-permute-start.2 = (bf16[256,640]{1,0:T(8,128)(2,1)S(1)}, bf16[256,640]{1,0:T(8,128)(2,1)S(1)}, u32[]{:S(2)}, u32[]{:S(2)}) collective-permute-start(bf16[256,640]{1,0:T(8,128)(2,1)S(1)} %bitcast.27), channel_id=1, source_target_pairs={{0,24},{8,0},{16,8},{24,16},{32,56},{40,32},{48,40},{56,48},{64,88... | collective-permute-start | bytes 983048 | tf_op jit(solution)/shard_map/attend/ppermute | solution.py:230
  55.7 3.1 %attend.6 = bf16[8,32,640]{2,1,0:T(8,128)(2,1)S(1)} custom-call(s32[4]{0:T(128)S(1)} %get-tuple-element.31.meta_ref, s32[32]{0:T(128)S(1)} %dynamic-slice_reduce_fusion.vis_ref, bf16[32,16,512]{2,1,0:T(8,128)(2,1)S(1)} %all-to-all-done.near_ref, bf16[32,16,512]{2,1,0:T(8,128)(2,1)S(1)} %collective-permute-done.far_ref, bf16[2048,512]{1,0:T(8,128)(2,1)S(1)} %copy-done.11, ...), custom_call_target="tpu_custom_call" | custom-call | flops 2147483648 | bytes 8388608 | tf_op jit(solution)/shard_map/attend/attend/pallas_call | solution.py:161
  58.8 0.0 collective-permute-done.6.refs_3_
  58.8 2.5 %collective-permute-start.3 = (bf16[256,640]{1,0:T(8,128)(2,1)S(1)}, bf16[256,640]{1,0:T(8,128)(2,1)S(1)}, u32[]{:S(2)}, u32[]{:S(2)}) collective-permute-start(bf16[256,640]{1,0:T(8,128)(2,1)S(1)} %bitcast.28), channel_id=1, source_target_pairs={{0,8},{8,16},{16,24},{24,0},{32,40},{40,48},{48,56},{56,32},{64,72... | collective-permute-start | bytes 983048 | tf_op jit(solution)/shard_map/attend/ppermute | solution.py:230
  61.3 0.0 collective-permute-done.5.refs_2_
  61.3 1.0 collective-permute-done.4.refs_1_
  62.3 3.1 %attend.7 = bf16[8,32,640]{2,1,0:T(8,128)(2,1)S(1)} custom-call(s32[4]{0:T(128)S(1)} %get-tuple-element.22.meta_ref, s32[32]{0:T(128)S(1)} %dynamic-slice_reduce_fusion.vis_ref, bf16[32,16,512]{2,1,0:T(8,128)(2,1)S(1)} %all-to-all-done.near_ref, bf16[32,16,512]{2,1,0:T(8,128)(2,1)S(1)} %collective-permute-done.far_ref, bf16[2048,512]{1,0:T(8,128)(2,1)S(1)} %copy-done.11, ...), custom_call_target="tpu_custom_call" | custom-call | flops 2147483648 | bytes 8388608 | tf_op jit(solution)/shard_map/attend/attend/pallas_call | solution.py:161
  65.4 0.0 copy-start.1
  65.4 0.0 copy-start.2
  65.4 0.0 copy-start.3
  65.4 0.0 collective-permute-done.1.refs_0_
  65.4 0.0 collective-permute-done.2.refs_1_
  65.4 4.1 %collective-permute-done.3.refs_2_ = bf16[256,640]{1,0:T(8,128)(2,1)S(1)} collective-permute-done((bf16[256,640]{1,0:T(8,128)(2,1)S(1)}, bf16[256,640]{1,0:T(8,128)(2,1)S(1)}, u32[]{:S(2)}, u32[]{:S(2)}) %collective-permute-start.3) | collective-permute-done | bytes 327712 | tf_op jit(solution)/shard_map/attend/ppermute | solution.py:230
  69.6 1.1 %join_pieces.2 = bf16[256,640]{1,0:T(8,128)(2,1)S(1)} custom-call(bf16[256,640]{1,0:T(8,128)(2,1)S(1)} %collective-permute-done.1.refs_0_, bf16[256,640]{1,0:T(8,128)(2,1)S(1)} %collective-permute-done.2.refs_1_, bf16[256,640]{1,0:T(8,128)(2,1)S(1)} %collective-permute-done.3.refs_2_, bf16[256,640]{1,0:T(8,128)(2,1)S(1)} %bitcast.21), custom_call_target="tpu_custom_call" | custom-call | tf_op jit(solution)/shard_map/join_x/join_pieces/pallas_call | solution.py:200
  70.6 12.7 %all_to_all.15.refs_0_ = bf16[8,32,640]{2,1,0:T(8,128)(2,1)S(1)} all-to-all(bf16[8,32,640]{2,1,0:T(8,128)(2,1)S(1)} %bitcast.20), channel_id=1, replica_groups={{0,32,64,96,128,160,192,224},{8,40,72,104,136,168,200,232},{16,48,80,11..., dimensions={0} | all-to-all | bytes 655360 | tf_op jit(solution)/shard_map/join_z/all_to_all | solution.py:318
  83.3 1.1 %join_pieces.3 = bf16[8,32,640]{2,1,0:T(8,128)(2,1)} custom-call(bf16[8,32,640]{2,1,0:T(8,128)(2,1)S(1)} %all_to_all.15.refs_0_), custom_call_target="tpu_custom_call" | custom-call | tf_op jit(solution)/shard_map/join_z/join_pieces/pallas_call | solution.py:200
  84.4 7.7 %all-to-all-start.2 = ((bf16[8,32,640]{2,1,0:T(8,128)(2,1)}), bf16[8,32,640]{2,1,0:T(8,128)(2,1)S(1)}, u32[]{:S(2)}, u32[]{:S(2)}) async-start(bf16[8,32,640]{2,1,0:T(8,128)(2,1)} %join_pieces.3), calls=%async_computation.2 | async-start | bytes 655360 | tf_op jit(solution)/shard_map/join_t/all_to_all | solution.py:321
  92.1 7.1 %all-to-all-done.2.pieces_ref = bf16[8,32,640]{2,1,0:T(8,128)(2,1)S(1)} async-done(((bf16[8,32,640]{2,1,0:T(8,128)(2,1)}), bf16[8,32,640]{2,1,0:T(8,128)(2,1)S(1)}, u32[]{:S(2)}, u32[]{:S(2)}) %all-to-all-start.2) | async-done | bytes 327712 | tf_op jit(solution)/shard_map/join_t/all_to_all | solution.py:321
  99.3 0.0 copy-done.3
  99.3 1.2 %final.1 = (f32[32,512]{1,0:T(8,128)S(1)}, f32[32,512]{1,0:T(8,128)S(1)}) custom-call(s32[1]{0:T(128)} %bitcast.row_ref, bf16[8,32,640]{2,1,0:T(8,128)(2,1)S(1)} %all-to-all-done.2.pieces_ref, bf16[32,512]{1,0:T(8,128)(2,1)S(1)} %bitcast.23, f32[1,512]{1,0:T(1,128)S(1)} %bitcast.24, bf16[512,512]{1,0:T(8,128)(2,1)S(1)} %copy-done.1, ...), custom_call_target="tpu_custom_call" | custom-call | tf_op jit(solution)/shard_map/final/final/pallas_call | solution.py:323
  100.5 1.2 %collective-permute-start.7 = (f32[32,512]{1,0:T(8,128)S(1)}, f32[32,512]{1,0:T(8,128)S(1)}, u32[]{:S(2)}, u32[]{:S(2)}) collective-permute-start(f32[32,512]{1,0:T(8,128)S(1)} %get-tuple-element.28), channel_id=1, source_target_pairs={{0,1},{1,0},{2,3},{3,2},{4,5},{5,4},{6,7},{7,6},{8,9},{9,8},{10,11... | collective-permute-start | bytes 196616 | tf_op jit(solution)/shard_map/final/ppermute | solution.py:238
  101.7 0.9 collective-permute-done.7
  102.6 0.6 fusion
  (10 shorter events, 0.0 us)
Async XLA Ops:
  0.0 37.4 %copy-start = (s32[32,32]{1,0:T(8,128)S(1)}, s32[32,32]{1,0:T(8,128)}, u32[]{:S(2)}) copy-start(s32[32,32]{1,0:T(8,128)} %param.13) | copy-start | bytes 12292
  0.0 14.3 %copy-start.4 = (bf16[1,1,2048,512]{3,2,1,0:T(8,128)(2,1)S(1)}, bf16[1,1,2048,512]{3,2,1,0:T(8,128)(2,1)}, u32[]{:S(2)}) copy-start(bf16[1,1,2048,512]{3,2,1,0:T(8,128)(2,1)} %param.11) | copy-start | bytes 6291460
  2.4 28.2 %all-to-all-start = ((bf16[32,16,512]{2,1,0:T(8,128)(2,1)}), bf16[32,16,512]{2,1,0:T(8,128)(2,1)S(1)}, u32[]{:S(2)}, u32[]{:S(2)}) async-start(bf16[32,16,512]{2,1,0:T(8,128)(2,1)} %queries.1), calls=%async_computation | async-start | bytes 1048576 | tf_op jit(solution)/shard_map/gather/all_to_all | solution.py:272
  14.3 1.2 %copy-start.5 = (bf16[512,1024]{1,0:T(8,128)(2,1)S(1)}, bf16[512,1024]{1,0:T(8,128)(2,1)}, u32[]{:S(2)}) copy-start(bf16[512,1024]{1,0:T(8,128)(2,1)} %w_ref.1) | copy-start | bytes 3145732
  15.5 0.9 copy-start.6
  16.5 0.9 copy-start.7
  21.2 1.9 %copy-start.8 = (bf16[2048,1024]{1,0:T(8,128)(2,1)}, bf16[2048,1024]{1,0:T(8,128)(2,1)S(1)}, u32[]{:S(2)}) copy-start(bf16[2048,1024]{1,0:T(8,128)(2,1)S(1)} %get-tuple-element.20.va_ref) | copy-start | bytes 12582916
  23.1 1.3 %copy-start.10 = (bf16[2048,512]{1,0:T(8,128)(2,1)}, bf16[2048,512]{1,0:T(8,128)(2,1)S(1)}, u32[]{:S(2)}) copy-start(bf16[2048,512]{1,0:T(8,128)(2,1)S(1)} %get-tuple-element.19.k_ref) | copy-start | bytes 6291460
  30.6 7.2 %collective-permute-start = (bf16[32,16,512]{2,1,0:T(8,128)(2,1)S(1)}, bf16[32,16,512]{2,1,0:T(8,128)(2,1)S(1)}, u32[]{:S(2)}, u32[]{:S(2)}) collective-permute-start(bf16[32,16,512]{2,1,0:T(8,128)(2,1)S(1)} %all-to-all-done.near_ref), channel_id=1, source_target_pairs={{0,1},{1,0},{2,3},{3,2},{4,5},{5,4},{6,7},{7,6},{8,9},{9,8},{10,11... | collective-permute-start | bytes 1572872 | tf_op jit(solution)/shard_map/gather/ppermute | solution.py:238
  33.0 25.8 %collective-permute-start.6 = (bf16[512,512]{1,0:T(8,128)(2,1)S(1)}, bf16[512,512]{1,0:T(8,128)(2,1)S(1)}, u32[]{:S(2)}, u32[]{:S(2)}) collective-permute-start(bf16[512,512]{1,0:T(8,128)(2,1)S(1)} %get-tuple-element.23.refs_0_), channel_id=1, source_target_pairs={{0,6},{1,7},{2,0},{3,1},{4,2},{5,3},{6,4},{7,5},{8,14},{9,15},{10,... | collective-permute-start | bytes 1572872 | tf_op jit(solution)/shard_map/weights/ppermute | solution.py:234
  35.7 25.6 %collective-permute-start.5 = (bf16[512,512]{1,0:T(8,128)(2,1)S(1)}, bf16[512,512]{1,0:T(8,128)(2,1)S(1)}, u32[]{:S(2)}, u32[]{:S(2)}) collective-permute-start(bf16[512,512]{1,0:T(8,128)(2,1)S(1)} %get-tuple-element.23.refs_0_), channel_id=1, source_target_pairs={{0,4},{1,5},{2,6},{3,7},{4,0},{5,1},{6,2},{7,3},{8,12},{9,13},{10,... | collective-permute-start | bytes 1572872 | tf_op jit(solution)/shard_map/weights/ppermute | solution.py:234
  36.0 26.2 %collective-permute-start.4 = (bf16[512,512]{1,0:T(8,128)(2,1)S(1)}, bf16[512,512]{1,0:T(8,128)(2,1)S(1)}, u32[]{:S(2)}, u32[]{:S(2)}) collective-permute-start(bf16[512,512]{1,0:T(8,128)(2,1)S(1)} %get-tuple-element.23.refs_0_), channel_id=1, source_target_pairs={{0,2},{1,3},{2,4},{3,5},{4,6},{5,7},{6,0},{7,1},{8,10},{9,11},{10,... | collective-permute-start | bytes 1572872 | tf_op jit(solution)/shard_map/weights/ppermute | solution.py:234
  37.8 2.2 %copy-start.9 = (bf16[2048,1024]{1,0:T(8,128)(2,1)S(1)}, bf16[2048,1024]{1,0:T(8,128)(2,1)}, u32[]{:S(2)}) copy-start(bf16[2048,1024]{1,0:T(8,128)(2,1)} %copy-done.8) | copy-start | bytes 12582916
  40.0 1.6 %copy-start.11 = (bf16[2048,512]{1,0:T(8,128)(2,1)S(1)}, bf16[2048,512]{1,0:T(8,128)(2,1)}, u32[]{:S(2)}) copy-start(bf16[2048,512]{1,0:T(8,128)(2,1)} %copy-done.10) | copy-start | bytes 6291460
  47.1 18.3 %collective-permute-start.1 = (bf16[256,640]{1,0:T(8,128)(2,1)S(1)}, bf16[256,640]{1,0:T(8,128)(2,1)S(1)}, u32[]{:S(2)}, u32[]{:S(2)}) collective-permute-start(bf16[256,640]{1,0:T(8,128)(2,1)S(1)} %bitcast.26), channel_id=1, source_target_pairs={{0,16},{8,24},{16,0},{24,8},{32,48},{40,56},{48,32},{56,40},{64,80... | collective-permute-start | bytes 983048 | tf_op jit(solution)/shard_map/attend/ppermute | solution.py:230
  54.2 11.2 %collective-permute-start.2 = (bf16[256,640]{1,0:T(8,128)(2,1)S(1)}, bf16[256,640]{1,0:T(8,128)(2,1)S(1)}, u32[]{:S(2)}, u32[]{:S(2)}) collective-permute-start(bf16[256,640]{1,0:T(8,128)(2,1)S(1)} %bitcast.27), channel_id=1, source_target_pairs={{0,24},{8,0},{16,8},{24,16},{32,56},{40,32},{48,40},{56,48},{64,88... | collective-permute-start | bytes 983048 | tf_op jit(solution)/shard_map/attend/ppermute | solution.py:230
  58.8 10.8 %collective-permute-start.3 = (bf16[256,640]{1,0:T(8,128)(2,1)S(1)}, bf16[256,640]{1,0:T(8,128)(2,1)S(1)}, u32[]{:S(2)}, u32[]{:S(2)}) collective-permute-start(bf16[256,640]{1,0:T(8,128)(2,1)S(1)} %bitcast.28), channel_id=1, source_target_pairs={{0,8},{8,16},{16,24},{24,0},{32,40},{40,48},{48,56},{56,32},{64,72... | collective-permute-start | bytes 983048 | tf_op jit(solution)/shard_map/attend/ppermute | solution.py:230
  65.4 33.9 %copy-start.1 = (bf16[512,512]{1,0:T(8,128)(2,1)S(1)}, bf16[512,512]{1,0:T(8,128)(2,1)}, u32[]{:S(2)}) copy-start(bf16[512,512]{1,0:T(8,128)(2,1)} %wo_ref.1) | copy-start | bytes 1572868
  65.4 33.9 %copy-start.2 = (bf16[1,32,512]{2,1,0:T(8,128)(2,1)S(1)}, bf16[1,32,512]{2,1,0:T(8,128)(2,1)}, u32[]{:S(2)}) copy-start(bf16[1,32,512]{2,1,0:T(8,128)(2,1)} %param.14) | copy-start | bytes 98308
  65.4 33.9 %copy-start.3 = (f32[512]{0:T(512)S(1)}, f32[512]{0:T(512)}, u32[]{:S(2)}) copy-start(f32[512]{0:T(512)} %param.16) | copy-start | bytes 6148
  84.4 14.8 %all-to-all-start.2 = ((bf16[8,32,640]{2,1,0:T(8,128)(2,1)}), bf16[8,32,640]{2,1,0:T(8,128)(2,1)S(1)}, u32[]{:S(2)}, u32[]{:S(2)}) async-start(bf16[8,32,640]{2,1,0:T(8,128)(2,1)} %join_pieces.3), calls=%async_computation.2 | async-start | bytes 655360 | tf_op jit(solution)/shard_map/join_t/all_to_all | solution.py:321
  100.5 2.1 %collective-permute-start.7 = (f32[32,512]{1,0:T(8,128)S(1)}, f32[32,512]{1,0:T(8,128)S(1)}, u32[]{:S(2)}, u32[]{:S(2)}) collective-permute-start(f32[32,512]{1,0:T(8,128)S(1)} %get-tuple-element.28), channel_id=1, source_target_pairs={{0,1},{1,0},{2,3},{3,2},{4,5},{5,4},{6,7},{7,6},{8,9},{9,8},{10,11... | collective-permute-start | bytes 196616 | tf_op jit(solution)/shard_map/final/ppermute | solution.py:238

commit v2 on v1

v2 whole, which is shorter than its diff:
```python
import functools

import jax
import jax.numpy as jnp
from jax import lax
from jax.experimental import pallas as pl
from jax.experimental.pallas import tpu as pltpu
from jax.sharding import PartitionSpec as P

H = 8
BLK = 256
NZ, NX = 8, 4
EPS = 1e-05
NEG = -1e30
D = 512
DH = 64
LR = 32
WIDE = D + 128
HALF = LR // 2
ROOM = 28 << 20
BF = jnp.bfloat16
F32 = jnp.float32


def lanes_of(shape):
    return lax.broadcasted_iota(jnp.int32, shape, len(shape) - 1)


def norm_rows(values, gain):
    average = jnp.mean(values, axis=-1, keepdims=True)
    centered = values - average
    variance = jnp.mean(centered * centered, axis=-1, keepdims=True)
    return centered * lax.rsqrt(variance + EPS) * gain


def whole(shape):
    return pl.BlockSpec(shape, lambda *_: (0,) * len(shape))


def query_kernel(half_ref, lat_ref, gain_ref, wq_ref, out_ref, q_s):
    normed = norm_rows(lat_ref[...].astype(F32), gain_ref[...]).astype(BF)
    q = jnp.dot(normed, wq_ref[...], preferred_element_type=F32).astype(BF)
    q_s[...] = q * jnp.asarray(DH ** -0.5, BF)
    rows = q_s[pl.ds(pl.multiple_of(half_ref[0] * 16, 16), 16), :]
    out_ref[...] = jnp.broadcast_to(rows[None], out_ref.shape)


def keyval_kernel(mine_ref, other_ref, w_ref, up_ref, down_ref, k_ref, va_ref, mlp_ref):
    @pl.when(pl.program_id(0) == 0)
    def _():
        mlp_ref[:, :256] = up_ref[...]
        mlp_ref[:256, 256:] = down_ref[:, :256]
        mlp_ref[256:, 256:] = down_ref[:, 256:]

    low_half = lanes_of((BLK, 128)) < DH
    ones = jnp.ones((BLK, 128), BF)
    for slot, obs_ref in enumerate((mine_ref, other_ref)):
        kv = jnp.dot(obs_ref[...], w_ref[...], preferred_element_type=F32).astype(BF)
        k_ref[slot] = kv[:, :D]
        for p in range(H // 2):
            v = kv[:, D + 128 * p : D + 128 * (p + 1)]
            va_ref[slot, :, 256 * p : 256 * p + 128] = jnp.where(low_half, v, ones)
            va_ref[slot, :, 256 * p + 128 : 256 * p + 256] = jnp.where(low_half, ones, v)


def pack_stats(lse):
    lane = lanes_of(lse.shape)
    high = lse.astype(BF).astype(F32)
    rest = lse - high
    mid = rest.astype(BF).astype(F32)
    low = rest - mid
    kept = jnp.where(lane < 8, high, jnp.where(lane < 16, mid, jnp.where(lane < 24, low, 0.0)))
    return kept.astype(BF)


def attend_kernel(shifts, meta_ref, vis_ref, near_ref, k_ref, va_ref, *rest):
    outs = rest[: len(shifts)]
    list_ref, q_s, v_s, l_s, out_s = rest[len(shifts) :]
    own, x = meta_ref[2], meta_ref[3]
    limit = NZ * len(shifts)
    columns = [lax.rem(x - d + NX, NX) for d in shifts]
    seen = jnp.int32(0)
    for j, column in enumerate(columns):
        for e in range(NZ):
            region = e * NX + column
            list_ref[0, seen] = region
            list_ref[1, seen] = jnp.int32(j * NZ + e)
            sees = (vis_ref[region] > 0) | (region == own)
            seen = seen + sees.astype(jnp.int32)
    last = jnp.maximum(seen - 1, 0)
    for k in range(7):
        for row in range(2):
            list_ref[row, seen + k] = list_ref[row, last]

    lane = lanes_of((HALF, 128))
    out_s[:, :, :D] = jnp.zeros((limit, HALF, D), BF)
    out_s[:, :, D:] = jnp.broadcast_to(
        jnp.where(lane < 8, NEG, 0.0).astype(BF)[None], (limit, HALF, 128)
    )

    def attend_slot(slot, count, rows, blocks, sure):
        keys = blocks * BLK
        low_half = lanes_of((rows, 128)) < DH

        def pair(p, carry):
            here = pl.ds(pl.multiple_of(128 * p, 128), 128)
            even_at = pl.ds(pl.multiple_of(256 * p, 128), 128)
            odd_at = pl.ds(pl.multiple_of(256 * p + 128, 128), 128)
            qp = q_s[:rows, here]
            zero = jnp.zeros_like(qp)
            both = jnp.concatenate([jnp.where(low_half, qp, zero), jnp.where(low_half, zero, qp)], 0)
            scores = lax.dot_general(
                both, k_ref[slot, :keys, here], (((1,), (1,)), ((), ())), preferred_element_type=F32
            )
            parts = [scores[:, : sure * BLK]]
            for j in range(sure, blocks):
                parts.append(jnp.where(count > j, scores[:, j * BLK : (j + 1) * BLK], NEG))
            scores = jnp.concatenate(parts, 1)
            peak = jnp.max(scores, axis=-1, keepdims=True)
            weights = jnp.exp(scores - peak).astype(BF)
            even = jnp.dot(weights[:rows], va_ref[slot, :keys, even_at], preferred_element_type=F32)
            odd = jnp.dot(weights[rows:], va_ref[slot, :keys, odd_at], preferred_element_type=F32)
            total = pltpu.roll(jnp.where(low_half, odd, even), DH, 1)
            value = jnp.where(low_half, even, odd) / total
            lse = jnp.where(low_half, peak[:rows], peak[rows:]) + jnp.log(total)
            before = l_s[:rows, here]
            highest = jnp.maximum(before, lse)
            old, new = jnp.exp(before - highest), jnp.exp(lse - highest)
            v_s[:rows, here] = (v_s[:rows, here] * old + value * new) / (old + new)
            l_s[:rows, here] = highest + jnp.log(old + new)
            return carry

        lax.fori_loop(0, H // 2, pair, 0)

    def run(regions):
        rows = regions * HALF
        for k in range(regions):
            q_s[HALF * k : HALF * (k + 1), :] = near_ref[list_ref[0, k]]
        v_s[:rows, :] = jnp.zeros((rows, D), F32)
        l_s[:rows, :] = jnp.full((rows, D), NEG, F32)

        def one_slot(slot, carry):
            count = meta_ref[slot]
            for fewest, blocks in ((1, 2), (3, 4), (5, 6), (7, 8)):

                @pl.when((count >= fewest) & (count <= blocks))
                def _():
                    attend_slot(slot, count, rows, blocks, fewest)

            return carry

        lax.fori_loop(0, 2, one_slot, 0)
        within = lanes_of((rows, 128)) & 7
        stats = jnp.zeros((rows, 128), F32)
        for p in range(H // 2):
            lse = l_s[:rows, 128 * p : 128 * (p + 1)]
            turned = pltpu.roll(lse, DH, 1)
            stats = jnp.where(within == 2 * p, lse, jnp.where(within == 2 * p + 1, turned, stats))
        packed = pack_stats(stats)
        value = v_s[:rows, :].astype(BF)
        for k in range(regions):
            e = list_ref[1, k]
            out_s[e, :, :D] = value[HALF * k : HALF * (k + 1)]
            out_s[e, :, D:] = packed[HALF * k : HALF * (k + 1)]

    sizes = [r for r in (8, 12, 16, 24) if r <= limit]
    for below, regions in zip([0] + sizes, sizes):

        @pl.when((seen > below) & (seen <= regions))
        def _():
            run(regions)

    for j, out in enumerate(outs):
        out[...] = out_s[NZ * j : NZ * (j + 1)]


def attend(shifts, meta, seen_by, near, keys, values):
    scalars = pl.BlockSpec(memory_space=pltpu.SMEM)
    vectors = pl.BlockSpec(memory_space=pltpu.VMEM)
    limit = NZ * len(shifts)
    return pl.pallas_call(
        functools.partial(attend_kernel, shifts),
        out_shape=[jax.ShapeDtypeStruct((NZ, HALF, WIDE), BF)] * len(shifts),
        in_specs=[scalars] * 2 + [vectors] * 3,
        out_specs=[vectors] * len(shifts),
        scratch_shapes=[
            pltpu.SMEM((2, 32), jnp.int32),
            pltpu.VMEM((limit * HALF, D), BF),
            pltpu.VMEM((limit * HALF, D), F32),
            pltpu.VMEM((limit * HALF, D), F32),
            pltpu.VMEM((limit, HALF, WIDE), BF),
        ],
        compiler_params=pltpu.CompilerParams(vmem_limit_bytes=ROOM),
        cost_estimate=pl.CostEstimate(flops=4 << 30, bytes_accessed=12 << 20, transcendentals=4 << 20),
        name="attend",
    )(meta, seen_by, near, keys, values)


def spread_matrix():
    row = lax.broadcasted_iota(jnp.int32, (128, WIDE), 0)
    col = lax.broadcasted_iota(jnp.int32, (128, WIDE), 1)
    head = jnp.where(col < D, col // DH, jnp.where(col < D + 24, col & 7, -1))
    return jnp.where((row < 24) & ((row & 7) == head), 1.0, 0.0).astype(BF)


def join(pieces, spread):
    lses = [jnp.dot(p[:, D:], spread, preferred_element_type=F32) for p in pieces]
    highest = functools.reduce(jnp.maximum, lses)
    scales = [jnp.exp(l - highest) for l in lses]
    total = functools.reduce(jnp.add, scales)
    value = functools.reduce(
        jnp.add, [p[:, :D].astype(F32) * s[:, :D] for p, s in zip(pieces, scales)]
    )
    return value / total[:, :D], (highest + jnp.log(total))[:, D:]


def join_kernel(*refs):
    *ins, out = refs
    pieces = [r[...] for r in ins] if len(ins) > 1 else [ins[0][k] for k in range(ins[0].shape[0])]
    value, lse = join(pieces, spread_matrix())
    out[..., :D] = jnp.broadcast_to(value.astype(BF), (*out.shape[:-1], D))
    out[..., D:] = jnp.broadcast_to(pack_stats(lse), (*out.shape[:-1], 128))


def joined(pieces, shape):
    return pl.pallas_call(
        join_kernel,
        out_shape=jax.ShapeDtypeStruct(shape, BF),
        in_specs=[pl.BlockSpec(memory_space=pltpu.VMEM)] * len(pieces),
        out_specs=pl.BlockSpec(memory_space=pltpu.VMEM),
        compiler_params=pltpu.CompilerParams(vmem_limit_bytes=ROOM),
        name="join_pieces",
    )(*pieces)


def final_kernel(place_ref, pieces_ref, lat_ref, gain_ref, wo_ref, own_ref, other_ref, out_ref, sums):
    row, core = place_ref[0], place_ref[1]
    pieces = [pieces_ref[k] for k in range(pieces_ref.shape[0])]
    value, _ = join(pieces, spread_matrix())
    attended = value.astype(BF)
    lat = lat_ref[pl.ds(pl.multiple_of(core * HALF, HALF), HALF), :]
    residual = lat.astype(F32) + jnp.dot(attended, wo_ref[...], preferred_element_type=F32)
    normed = norm_rows(residual, gain_ref[...]).astype(BF)
    for side, ref in enumerate((own_ref, other_ref)):
        for k in range(4):
            v = jnp.dot(normed, ref[k, :, :256], preferred_element_type=F32)
            hidden = jax.nn.gelu(v, approximate=True).astype(BF)
            down = jnp.concatenate([ref[k, :256, 256:], ref[k, 256:, 256:]], 1)
            at = 4 * side + lax.rem(row - k + 4, 4)
            sums[at] = jnp.dot(hidden, down, preferred_element_type=F32)
    total = residual
    for k in range(8):
        total = total + sums[k]
    out_ref[...] = total.astype(BF)


def shifted_x(a, by):
    pairs = [
        (zz * NX + xx, zz * NX + (xx + by) % NX) for zz in range(NZ) for xx in range(NX)
    ]
    return lax.ppermute(a, "region", pairs) if by % NX else a


def shifted_y(a, by):
    return lax.ppermute(a, "tm", [(k, (k + 2 * by) % 8) for k in range(8)]) if by % 4 else a


def core_swapped(a):
    return lax.ppermute(a, "tm", [(k, k ^ 1) for k in range(8)])


def on_device(
    observations,
    counts,
    visible,
    latents,
    lat_gain,
    mlp_gain,
    w_query,
    w_keyval,
    w_out,
    w_up,
    w_down,
):
    own = lax.axis_index("region")
    slot = lax.axis_index("tm")
    x, row, core = own % NX, slot // 2, slot % 2
    observed = observations[0, 0]
    lat = latents[0]
    scalars = pl.BlockSpec(memory_space=pltpu.SMEM)
    vectors = pl.BlockSpec(memory_space=pltpu.VMEM)

    with jax.named_scope("queries"):
        q = pl.pallas_call(
            query_kernel,
            out_shape=jax.ShapeDtypeStruct((NZ * NX, HALF, D), BF),
            in_specs=[scalars] + [vectors] * 3,
            out_specs=vectors,
            scratch_shapes=[pltpu.VMEM((LR, D), BF)],
            name="queries",
        )(core[None], lat, lat_gain[None], w_query)
    with jax.named_scope("gather"):
        near = lax.all_to_all(q, "region", 0, 0, tiled=True)

    with jax.named_scope("keyval"):
        other = core_swapped(observed)
        count = counts[0, 0]
        other_count = core_swapped(count)
        length = observed.shape[0]
        block = pl.BlockSpec((BLK, D), lambda i: (i, 0))
        keys, values, mlp = pl.pallas_call(
            keyval_kernel,
            grid=(length // BLK,),
            out_shape=[
                jax.ShapeDtypeStruct((2, length, D), BF),
                jax.ShapeDtypeStruct((2, length, 2 * D), BF),
                jax.ShapeDtypeStruct((D, D), BF),
            ],
            in_specs=[
                block,
                block,
                pl.BlockSpec((D, 2 * D), lambda i: (0, 0)),
                pl.BlockSpec((D, 256), lambda i: (0, 0)),
                pl.BlockSpec((256, D), lambda i: (0, 0)),
            ],
            out_specs=[
                pl.BlockSpec((2, BLK, D), lambda i: (0, i, 0)),
                pl.BlockSpec((2, BLK, 2 * D), lambda i: (0, i, 0)),
                pl.BlockSpec((D, D), lambda i: (0, 0)),
            ],
            compiler_params=pltpu.CompilerParams(vmem_limit_bytes=ROOM),
            cost_estimate=pl.CostEstimate(flops=4 << 30, bytes_accessed=18 << 20, transcendentals=0),
            name="keyval",
        )(observed, other, w_keyval, w_up, w_down)

    with jax.named_scope("weights"):
        shards = [shifted_y(mlp, k) for k in range(4)]

    seen_by = lax.dynamic_slice_in_dim(visible, own, 1, 1)[:, 0]
    meta = jnp.stack([count, other_count, own, x]).astype(jnp.int32)
    with jax.named_scope("attend"):
        pieces = []
        for shifts in ((2, 1, 3), (0,)):
            parts = attend(shifts, meta, seen_by, near, keys, values)
            for d, part in zip(shifts, parts):
                pieces.append(shifted_x(part.reshape(NZ * HALF, WIDE), -d))
    with jax.named_scope("join_x"):
        part = joined(pieces, (NZ * HALF, WIDE))
        part, *shards = lax.optimization_barrier((part, *shards))
    with jax.named_scope("join_z"):
        groups = [[zz * NX + xx for zz in range(NZ)] for xx in range(NX)]
        part = lax.all_to_all(
            part.reshape(NZ, HALF, WIDE), "region", 0, 0, axis_index_groups=groups, tiled=True
        )
        part = joined([part], (4, HALF, WIDE))
    with jax.named_scope("weights"):
        near_shards = jnp.stack(shards)
        far_shards = core_swapped(near_shards)
    with jax.named_scope("join_t"):
        groups = [[2 * k + c for k in range(4)] for c in range(2)]
        pieces = lax.all_to_all(part, "tm", 0, 0, axis_index_groups=groups, tiled=True)
    with jax.named_scope("final"):
        mine = pl.pallas_call(
            final_kernel,
            out_shape=jax.ShapeDtypeStruct((HALF, D), BF),
            in_specs=[scalars] + [vectors] * 6,
            out_specs=vectors,
            scratch_shapes=[pltpu.VMEM((8, HALF, D), F32)],
            compiler_params=pltpu.CompilerParams(vmem_limit_bytes=ROOM),
            name="final",
        )(jnp.stack([row, core]), pieces, lat, mlp_gain[None], w_out, near_shards, far_shards)
        theirs = core_swapped(mine)
        first = jnp.where(core == 0, mine, theirs)
        second = jnp.where(core == 0, theirs, mine)
    return jnp.concatenate([first, second])[None]


def solution(mesh):
    placed = (
        P("region", "tm", None, None),
        P("region", "tm"),
        P(),
        P("region", None, None),
        P(),
        P(),
        P(),
        P(),
        P(),
        P(None, "tm"),
        P("tm", None),
    )
    return jax.shard_map(
        on_device, mesh=mesh, in_specs=placed, out_specs=P("region", None, None), check_vma=False
    )
```

time: 104 us -> 118 us (1.13)
  blocking collectives: 12.7 us -> 0 us
  waiting for transfers between devices: 19.2 us -> 27.6 us
  starting transfers between devices: 34.8 us -> 43.1 us
  local copies, waits for them, and re-layouts: 10.4 us -> 18.7 us
  Pallas kernels: 24.5 us -> 25.9 us
    all_to_all x1 -> x0, blocking collectives: 12.7 us -> none  [on_device(): lax.all_to_all(part, 'region', 0, 0, axis_index_groups=groups, tiled=True)]
    ppermute x3, waiting for transfers between devices: 0.96 us -> 10.8 us  [shifted_y(): lax.ppermute(a, 'tm', [(k, (k + 2 * by) % 8) for k in range(8)])]
    unnamed x24 -> x28, local copies, waits for them, and re-layouts: 10.2 us -> 18.5 us
    all_to_all x1 -> x2, waiting for transfers between devices: 7.12 us -> 13.6 us  [the longest x1 9.2 us: on_device(): lax.all_to_all(part.reshape(NZ, HALF, WIDE), 'region', 0, 0, axis_index_g...]
    all_to_all x1, waiting for transfers between devices: 6.09 us -> 0.01 us  [on_device(): near = lax.all_to_all(q, 'region', 0, 0, tiled=True)]
    all_to_all x1 -> x2, starting transfers between devices: 7.7 us -> 11.8 us  [the longest x1 8.54 us: on_device(): lax.all_to_all(part.reshape(NZ, HALF, WIDE), 'region', 0, 0, axis_index_g...]
    ppermute x2 -> x4, starting transfers between devices: 3.6 us -> 6.97 us  [core_swapped(): return lax.ppermute(a, 'tm', [(k, k ^ 1) for k in range(8)])]
    ppermute x3, starting transfers between devices: 7.88 us -> 11.2 us  [shifted_x(): return lax.ppermute(a, 'region', pairs) if by % NX else a]
  transfers between devices with their start and end apart: 10 -> 13, of which waited for: 5 -> 7; matrix products, arithmetic and copies ran while one was open for 0% -> 1% of each run, Pallas kernels for 18% -> 14%
where the time goes in v2:
time: 118 us
  starting transfers between devices  43.1 us (37%)
  waiting for transfers between devices  27.6 us (23%)
  Pallas kernels  25.9 us (22%)
  local copies, waits for them, and re-layouts  18.7 us (16%)
  other arithmetic  1.61 us (1%)
    unnamed x28, local copies, waits for them, and re-layouts  18.5 us
    pallas_call x2, Pallas kernels, attend(): pl.pallas_call(functools.partial(attend_kernel, shifts), out_shape=[jax.S...  11.7 us
    ppermute x3, starting transfers between devices, shifted_x(): return lax.ppermute(a, 'region', pairs) if by % NX else a  11.2 us
    ppermute x3, waiting for transfers between devices, shifted_y(): lax.ppermute(a, 'tm', [(k, (k + 2 * by) % 8) for k in range(8)])  10.8 us
    all_to_all x1, starting transfers between devices, on_device(): near = lax.all_to_all(q, 'region', 0, 0, tiled=True)  9.3 us
    all_to_all x1, waiting for transfers between devices, on_device(): lax.all_to_all(part.reshape(NZ, HALF, WIDE), 'region', 0, 0, axis_index_g...  9.2 us
    all_to_all x1, starting transfers between devices, on_device(): lax.all_to_all(part.reshape(NZ, HALF, WIDE), 'region', 0, 0, axis_index_g...  8.54 us
    ppermute x4, starting transfers between devices, core_swapped(): return lax.ppermute(a, 'tm', [(k, k ^ 1) for k in range(8)])  6.97 us
  transfers between devices with their start and end apart: 13, of which 7 were waited for; matrix products, arithmetic and copies ran while one was open for 1% of the time, Pallas kernels for 14%

profile of v2, /device:TPU:1, one launch (start us, length us, event | category | flops | bytes accessed | tf_op | source)
XLA Modules:
  0.0 117.6 jit_solution(9836560363601506999)
XLA Ops:
  0.0 3.2 %collective-permute-start.1 = (bf16[2048,512]{1,0:T(8,128)(2,1)}, bf16[2048,512]{1,0:T(8,128)(2,1)S(1)}, u32[]{:S(2)}, u32[]{:S(2)}) collective-permute-start(bf16[2048,512]{1,0:T(8,128)(2,1)} %bitcast.28), channel_id=1, source_target_pairs={{0,1},{1,0},{2,3},{3,2},{4,5},{5,4},{6,7},{7,6},{8,9},{9,8},{10,11... | collective-permute-start | bytes 6291464 | tf_op jit(solution)/shard_map/keyval/ppermute | solution.py:269
  3.2 2.3 %queries.1 = bf16[32,16,512]{2,1,0:T(8,128)(2,1)} custom-call(s32[1]{0:T(128)} %bitcast.1.half_ref, bf16[32,512]{1,0:T(8,128)(2,1)} %bitcast.25, f32[1,512]{1,0:T(1,128)} %bitcast.36, bf16[512,512]{1,0:T(8,128)(2,1)} %wq_ref.1), custom_call_target="tpu_custom_call" | custom-call | tf_op jit(solution)/shard_map/queries/queries/pallas_call | solution.py:294
  5.6 9.3 %all-to-all-start = ((bf16[32,16,512]{2,1,0:T(8,128)(2,1)}), bf16[32,16,512]{2,1,0:T(8,128)(2,1)S(1)}, u32[]{:S(2)}, u32[]{:S(2)}) async-start(bf16[32,16,512]{2,1,0:T(8,128)(2,1)} %queries.1), calls=%async_computation | async-start | bytes 1048576 | tf_op jit(solution)/shard_map/gather/all_to_all | solution.py:303
  14.9 0.4 collective-permute-start
  15.9 0.2 dynamic-slice_reduce_fusion.vis_ref
  16.1 0.2 collective-permute-done
  16.4 0.6 pad_add_fusion.1.meta_ref
  17.0 0.0 collective-permute-done.1.other_ref
  17.0 1.4 %copy-done.5 = bf16[2048,512]{1,0:T(8,128)(2,1)} copy-done((bf16[2048,512]{1,0:T(8,128)(2,1)}, bf16[2048,512]{1,0:T(8,128)(2,1)S(1)}, u32[]{:S(2)}) %copy-start.5) | copy-done | bytes 2097176
  18.4 1.6 %copy-done.4 = bf16[1,1,2048,512]{3,2,1,0:T(8,128)(2,1)S(1)} copy-done((bf16[1,1,2048,512]{3,2,1,0:T(8,128)(2,1)S(1)}, bf16[1,1,2048,512]{3,2,1,0:T(8,128)(2,1)}, u32[]{:S(2)}) %copy-start.4) | copy-done | bytes 2097176
  20.0 1.6 %copy-done.6 = bf16[2048,512]{1,0:T(8,128)(2,1)S(1)} copy-done((bf16[2048,512]{1,0:T(8,128)(2,1)S(1)}, bf16[2048,512]{1,0:T(8,128)(2,1)}, u32[]{:S(2)}) %copy-start.6) | copy-done | bytes 2097176
  21.5 1.2 %copy-done.7 = bf16[512,1024]{1,0:T(8,128)(2,1)S(1)} copy-done((bf16[512,1024]{1,0:T(8,128)(2,1)S(1)}, bf16[512,1024]{1,0:T(8,128)(2,1)}, u32[]{:S(2)}) %copy-start.7) | copy-done | bytes 1048600
  22.8 0.9 copy-done.8
  23.7 0.9 copy-done.9
  24.7 6.9 %keyval.1 = (bf16[2,2048,512]{2,1,0:T(8,128)(2,1)S(1)}, bf16[2,2048,1024]{2,1,0:T(8,128)(2,1)S(1)}, bf16[512,512]{1,0:T(8,128)(2,1)S(1)}) custom-call(bf16[2048,512]{1,0:T(8,128)(2,1)S(1)} %bitcast.29, bf16[2048,512]{1,0:T(8,128)(2,1)S(1)} %copy-done.6, bf16[512,1024]{1,0:T(8,128)(2,1)S(1)} %copy-done.7, bf16[512,256]{1,0:T(8,128)(2,1)S(1)} %copy-done.8, ...), custom_call_target="tpu_custom_call" | custom-call | flops 4294967296 | bytes 18874368 | tf_op jit(solution)/shard_map/keyval/keyval/pallas_call | solution.py:311
  31.6 3.3 %copy-done.10 = bf16[2,2048,1024]{2,1,0:T(8,128)(2,1)} copy-done((bf16[2,2048,1024]{2,1,0:T(8,128)(2,1)}, bf16[2,2048,1024]{2,1,0:T(8,128)(2,1)S(1)}, u32[]{:S(2)}) %copy-start.10) | copy-done | bytes 8388632
  34.9 2.0 %copy-done.12 = bf16[2,2048,512]{2,1,0:T(8,128)(2,1)} copy-done((bf16[2,2048,512]{2,1,0:T(8,128)(2,1)}, bf16[2,2048,512]{2,1,0:T(8,128)(2,1)S(1)}, u32[]{:S(2)}) %copy-start.12) | copy-done | bytes 4194328
  36.8 0.0 all-to-all-done.near_ref
  36.9 3.4 %copy-done.11 = bf16[2,2048,1024]{2,1,0:T(8,128)(2,1)S(1)} copy-done((bf16[2,2048,1024]{2,1,0:T(8,128)(2,1)S(1)}, bf16[2,2048,1024]{2,1,0:T(8,128)(2,1)}, u32[]{:S(2)}) %copy-start.11) | copy-done | bytes 8388632
  40.2 2.2 %copy-done.13 = bf16[2,2048,512]{2,1,0:T(8,128)(2,1)S(1)} copy-done((bf16[2,2048,512]{2,1,0:T(8,128)(2,1)S(1)}, bf16[2,2048,512]{2,1,0:T(8,128)(2,1)}, u32[]{:S(2)}) %copy-start.13) | copy-done | bytes 4194328
  42.4 6.2 %attend.2 = (bf16[8,16,640]{2,1,0:T(8,128)(2,1)S(1)}, bf16[8,16,640]{2,1,0:T(8,128)(2,1)S(1)}, bf16[8,16,640]{2,1,0:T(8,128)(2,1)S(1)}) custom-call(s32[4]{0:T(128)S(1)} %pad_add_fusion.1.meta_ref, s32[32]{0:T(128)S(1)} %dynamic-slice_reduce_fusion.vis_ref, bf16[32,16,512]{2,1,0:T(8,128)(2,1)S(1)} %all-to-all-done.near_ref, ...), custom_call_target="tpu_custom_call" | custom-call | flops 4294967296 | bytes 12582912 | tf_op jit(solution)/shard_map/attend/attend/pallas_call | solution.py:181
  48.7 5.2 %collective-permute-start.3 = (bf16[128,640]{1,0:T(8,128)(2,1)S(1)}, bf16[128,640]{1,0:T(8,128)(2,1)S(1)}, u32[]{:S(2)}, u32[]{:S(2)}) collective-permute-start(bf16[128,640]{1,0:T(8,128)(2,1)S(1)} %bitcast.32), channel_id=1, source_target_pairs={{0,24},{8,0},{16,8},{24,16},{32,56},{40,32},{48,40},{56,48},{64,88... | collective-permute-start | bytes 491528 | tf_op jit(solution)/shard_map/attend/ppermute | solution.py:261
  53.8 2.7 %collective-permute-start.7 = (bf16[512,512]{1,0:T(8,128)(2,1)S(1)}, bf16[512,512]{1,0:T(8,128)(2,1)S(1)}, u32[]{:S(2)}, u32[]{:S(2)}) collective-permute-start(bf16[512,512]{1,0:T(8,128)(2,1)S(1)} %get-tuple-element.23), channel_id=1, source_target_pairs={{0,6},{1,7},{2,0},{3,1},{4,2},{5,3},{6,4},{7,5},{8,14},{9,15},{10,... | collective-permute-start | bytes 1572872 | tf_op jit(solution)/shard_map/weights/ppermute | solution.py:265
  56.6 0.4 collective-permute-start.6
  56.9 0.7 collective-permute-start.5
  57.6 6.0 %collective-permute-start.2 = (bf16[128,640]{1,0:T(8,128)(2,1)S(1)}, bf16[128,640]{1,0:T(8,128)(2,1)S(1)}, u32[]{:S(2)}, u32[]{:S(2)}) collective-permute-start(bf16[128,640]{1,0:T(8,128)(2,1)S(1)} %bitcast.31), channel_id=1, source_target_pairs={{0,16},{8,24},{16,0},{24,8},{32,48},{40,56},{48,32},{56,40},{64,80... | collective-permute-start | bytes 491528 | tf_op jit(solution)/shard_map/attend/ppermute | solution.py:261
  63.6 0.0 collective-permute-done.3.refs_1_
  63.6 0.0 collective-permute-start.4
  63.6 5.4 %attend.3 = bf16[8,16,640]{2,1,0:T(8,128)(2,1)S(1)} custom-call(s32[4]{0:T(128)S(1)} %pad_add_fusion.1.meta_ref, s32[32]{0:T(128)S(1)} %dynamic-slice_reduce_fusion.vis_ref, bf16[32,16,512]{2,1,0:T(8,128)(2,1)S(1)} %all-to-all-done.near_ref, bf16[2,2048,512]{2,1,0:T(8,128)(2,1)S(1)} %copy-done.13, bf16[2,2048,1024]{2,1,0:T(8,128)(2,1)S(1)} %copy-done.11), custom_call_target="tpu_custom_call" | custom-call | flops 4294967296 | bytes 12582912 | tf_op jit(solution)/shard_map/attend/attend/pallas_call | solution.py:181
  69.1 0.0 collective-permute-done.2.refs_0_
  69.1 2.0 %collective-permute-done.4.refs_2_ = bf16[128,640]{1,0:T(8,128)(2,1)S(1)} collective-permute-done((bf16[128,640]{1,0:T(8,128)(2,1)S(1)}, bf16[128,640]{1,0:T(8,128)(2,1)S(1)}, u32[]{:S(2)}, u32[]{:S(2)}) %collective-permute-start.4) | collective-permute-done | bytes 163872 | tf_op jit(solution)/shard_map/attend/ppermute | solution.py:261
  71.0 1.3 %join_pieces.2 = bf16[128,640]{1,0:T(8,128)(2,1)} custom-call(bf16[128,640]{1,0:T(8,128)(2,1)S(1)} %collective-permute-done.2.refs_0_, bf16[128,640]{1,0:T(8,128)(2,1)S(1)} %collective-permute-done.3.refs_1_, bf16[128,640]{1,0:T(8,128)(2,1)S(1)} %collective-permute-done.4.refs_2_, bf16[128,640]{1,0:T(8,128)(2,1)S(1)} %bitcast.24), custom_call_target="tpu_custom_call" | custom-call | tf_op jit(solution)/shard_map/join_x/join_pieces/pallas_call | solution.py:226
  72.3 6.0 %collective-permute-done.7 = bf16[512,512]{1,0:T(8,128)(2,1)S(1)} collective-permute-done((bf16[512,512]{1,0:T(8,128)(2,1)S(1)}, bf16[512,512]{1,0:T(8,128)(2,1)S(1)}, u32[]{:S(2)}, u32[]{:S(2)}) %collective-permute-start.7) | collective-permute-done | bytes 524320 | tf_op jit(solution)/shard_map/weights/ppermute | solution.py:265
  78.4 0.0 collective-permute-done.6
  78.4 4.8 %collective-permute-done.5 = bf16[512,512]{1,0:T(8,128)(2,1)S(1)} collective-permute-done((bf16[512,512]{1,0:T(8,128)(2,1)S(1)}, bf16[512,512]{1,0:T(8,128)(2,1)S(1)}, u32[]{:S(2)}, u32[]{:S(2)}) %collective-permute-start.5) | collective-permute-done | bytes 524320 | tf_op jit(solution)/shard_map/weights/ppermute | solution.py:265
  83.2 0.3 pad_maximum_fusion.own_ref
  83.4 0.6 collective-permute-start.8
  84.0 8.5 %all-to-all-start.1 = ((bf16[8,16,640]{2,1,0:T(8,128)(2,1)}), bf16[8,16,640]{2,1,0:T(8,128)(2,1)S(1)}, u32[]{:S(2)}, u32[]{:S(2)}) async-start(bf16[8,16,640]{2,1,0:T(8,128)(2,1)} %bitcast.14), calls=%async_computation.1 | async-start | bytes 327680 | tf_op jit(solution)/shard_map/join_z/all_to_all | solution.py:352
  92.6 9.2 %all-to-all-done.1.refs_0_ = bf16[8,16,640]{2,1,0:T(8,128)(2,1)S(1)} async-done(((bf16[8,16,640]{2,1,0:T(8,128)(2,1)}), bf16[8,16,640]{2,1,0:T(8,128)(2,1)S(1)}, u32[]{:S(2)}, u32[]{:S(2)}) %all-to-all-start.1) | async-done | bytes 163872 | tf_op jit(solution)/shard_map/join_z/all_to_all | solution.py:352
  101.8 0.9 join_pieces.3
  102.6 3.3 %all-to-all-start.2 = ((bf16[4,16,640]{2,1,0:T(8,128)(2,1)}), bf16[4,16,640]{2,1,0:T(8,128)(2,1)S(1)}, u32[]{:S(2)}, u32[]{:S(2)}) async-start(bf16[4,16,640]{2,1,0:T(8,128)(2,1)} %join_pieces.3), calls=%async_computation.2 | async-start | bytes 163840 | tf_op jit(solution)/shard_map/join_t/all_to_all | solution.py:361
  105.9 0.1 pad_add_fusion.place_ref
  106.0 4.5 %all-to-all-done.2.pieces_ref = bf16[4,16,640]{2,1,0:T(8,128)(2,1)S(1)} async-done(((bf16[4,16,640]{2,1,0:T(8,128)(2,1)}), bf16[4,16,640]{2,1,0:T(8,128)(2,1)S(1)}, u32[]{:S(2)}, u32[]{:S(2)}) %all-to-all-start.2) | async-done | bytes 81952 | tf_op jit(solution)/shard_map/join_t/all_to_all | solution.py:361
  110.5 0.0 collective-permute-done.8.other_ref
  110.5 2.9 %final.1 = bf16[16,512]{1,0:T(8,128)(2,1)S(1)} custom-call(s32[2]{0:T(128)S(1)} %pad_add_fusion.place_ref, bf16[4,16,640]{2,1,0:T(8,128)(2,1)S(1)} %all-to-all-done.2.pieces_ref, bf16[32,512]{1,0:T(8,128)(2,1)S(1)} %bitcast.26, f32[1,512]{1,0:T(1,128)S(1)} %bitcast.27, bf16[512,512]{1,0:T(8,128)(2,1)S(1)} %copy-done.1, ...), custom_call_target="tpu_custom_call" | custom-call | tf_op jit(solution)/shard_map/final/final/pallas_call | solution.py:363
  113.4 2.8 %collective-permute-start.9 = (bf16[16,512]{1,0:T(8,128)(2,1)S(1)}, bf16[16,512]{1,0:T(8,128)(2,1)S(1)}, u32[]{:S(2)}, u32[]{:S(2)}) collective-permute-start(bf16[16,512]{1,0:T(8,128)(2,1)S(1)} %final.1), channel_id=1, source_target_pairs={{0,1},{1,0},{2,3},{3,2},{4,5},{5,4},{6,7},{7,6},{8,9},{9,8},{10,11... | collective-permute-start | bytes 49160 | tf_op jit(solution)/shard_map/final/ppermute | solution.py:269
  116.2 0.8 collective-permute-done.9
  117.0 0.6 maximum_bitcast_fusion
  (19 shorter events, 0.0 us)
Async XLA Ops:
  0.0 15.9 %copy-start = (s32[32,32]{1,0:T(8,128)S(1)}, s32[32,32]{1,0:T(8,128)}, u32[]{:S(2)}) copy-start(s32[32,32]{1,0:T(8,128)} %param.13) | copy-start | bytes 12292
  0.0 17.0 %collective-permute-start.1 = (bf16[2048,512]{1,0:T(8,128)(2,1)}, bf16[2048,512]{1,0:T(8,128)(2,1)S(1)}, u32[]{:S(2)}, u32[]{:S(2)}) collective-permute-start(bf16[2048,512]{1,0:T(8,128)(2,1)} %bitcast.28), channel_id=1, source_target_pairs={{0,1},{1,0},{2,3},{3,2},{4,5},{5,4},{6,7},{7,6},{8,9},{9,8},{10,11... | collective-permute-start | bytes 6291464 | tf_op jit(solution)/shard_map/keyval/ppermute | solution.py:269
  5.6 31.3 %all-to-all-start = ((bf16[32,16,512]{2,1,0:T(8,128)(2,1)}), bf16[32,16,512]{2,1,0:T(8,128)(2,1)S(1)}, u32[]{:S(2)}, u32[]{:S(2)}) async-start(bf16[32,16,512]{2,1,0:T(8,128)(2,1)} %queries.1), calls=%async_computation | async-start | bytes 1048576 | tf_op jit(solution)/shard_map/gather/all_to_all | solution.py:303
  14.9 1.5 %collective-permute-start = (s32[]{:T(128)}, s32[]{:T(128)}, u32[]{:S(2)}, u32[]{:S(2)}) collective-permute-start(s32[]{:T(128)} %bitcast.3), channel_id=1, source_target_pairs={{0,1},{1,0},{2,3},{3,2},{4,5},{5,4},{6,7},{7,6},{8,9},{9,8},{10,11... | collective-permute-start | bytes 20 | tf_op jit(solution)/shard_map/keyval/ppermute | solution.py:269
  17.0 1.4 %copy-start.5 = (bf16[2048,512]{1,0:T(8,128)(2,1)}, bf16[2048,512]{1,0:T(8,128)(2,1)S(1)}, u32[]{:S(2)}) copy-start(bf16[2048,512]{1,0:T(8,128)(2,1)S(1)} %collective-permute-done.1.other_ref) | copy-start | bytes 6291460
  18.4 1.6 %copy-start.4 = (bf16[1,1,2048,512]{3,2,1,0:T(8,128)(2,1)S(1)}, bf16[1,1,2048,512]{3,2,1,0:T(8,128)(2,1)}, u32[]{:S(2)}) copy-start(bf16[1,1,2048,512]{3,2,1,0:T(8,128)(2,1)} %param.11) | copy-start | bytes 6291460
  19.9 1.6 %copy-start.6 = (bf16[2048,512]{1,0:T(8,128)(2,1)S(1)}, bf16[2048,512]{1,0:T(8,128)(2,1)}, u32[]{:S(2)}) copy-start(bf16[2048,512]{1,0:T(8,128)(2,1)} %copy-done.5) | copy-start | bytes 6291460
  21.5 1.2 %copy-start.7 = (bf16[512,1024]{1,0:T(8,128)(2,1)S(1)}, bf16[512,1024]{1,0:T(8,128)(2,1)}, u32[]{:S(2)}) copy-start(bf16[512,1024]{1,0:T(8,128)(2,1)} %w_ref.1) | copy-start | bytes 3145732
  22.8 0.9 copy-start.8
  23.7 0.9 copy-start.9
  31.6 3.3 %copy-start.10 = (bf16[2,2048,1024]{2,1,0:T(8,128)(2,1)}, bf16[2,2048,1024]{2,1,0:T(8,128)(2,1)S(1)}, u32[]{:S(2)}) copy-start(bf16[2,2048,1024]{2,1,0:T(8,128)(2,1)S(1)} %get-tuple-element.17.va_ref) | copy-start | bytes 25165828
  34.8 2.0 %copy-start.12 = (bf16[2,2048,512]{2,1,0:T(8,128)(2,1)}, bf16[2,2048,512]{2,1,0:T(8,128)(2,1)S(1)}, u32[]{:S(2)}) copy-start(bf16[2,2048,512]{2,1,0:T(8,128)(2,1)S(1)} %get-tuple-element.16.k_ref) | copy-start | bytes 12582916
  36.8 3.4 %copy-start.11 = (bf16[2,2048,1024]{2,1,0:T(8,128)(2,1)S(1)}, bf16[2,2048,1024]{2,1,0:T(8,128)(2,1)}, u32[]{:S(2)}) copy-start(bf16[2,2048,1024]{2,1,0:T(8,128)(2,1)} %copy-done.10) | copy-start | bytes 25165828
  40.2 2.2 %copy-start.13 = (bf16[2,2048,512]{2,1,0:T(8,128)(2,1)S(1)}, bf16[2,2048,512]{2,1,0:T(8,128)(2,1)}, u32[]{:S(2)}) copy-start(bf16[2,2048,512]{2,1,0:T(8,128)(2,1)} %copy-done.12) | copy-start | bytes 12582916
  48.7 15.0 %collective-permute-start.3 = (bf16[128,640]{1,0:T(8,128)(2,1)S(1)}, bf16[128,640]{1,0:T(8,128)(2,1)S(1)}, u32[]{:S(2)}, u32[]{:S(2)}) collective-permute-start(bf16[128,640]{1,0:T(8,128)(2,1)S(1)} %bitcast.32), channel_id=1, source_target_pairs={{0,24},{8,0},{16,8},{24,16},{32,56},{40,32},{48,40},{56,48},{64,88... | collective-permute-start | bytes 491528 | tf_op jit(solution)/shard_map/attend/ppermute | solution.py:261
  53.8 24.5 %collective-permute-start.7 = (bf16[512,512]{1,0:T(8,128)(2,1)S(1)}, bf16[512,512]{1,0:T(8,128)(2,1)S(1)}, u32[]{:S(2)}, u32[]{:S(2)}) collective-permute-start(bf16[512,512]{1,0:T(8,128)(2,1)S(1)} %get-tuple-element.23), channel_id=1, source_target_pairs={{0,6},{1,7},{2,0},{3,1},{4,2},{5,3},{6,4},{7,5},{8,14},{9,15},{10,... | collective-permute-start | bytes 1572872 | tf_op jit(solution)/shard_map/weights/ppermute | solution.py:265
  56.6 21.8 %collective-permute-start.6 = (bf16[512,512]{1,0:T(8,128)(2,1)S(1)}, bf16[512,512]{1,0:T(8,128)(2,1)S(1)}, u32[]{:S(2)}, u32[]{:S(2)}) collective-permute-start(bf16[512,512]{1,0:T(8,128)(2,1)S(1)} %get-tuple-element.23), channel_id=1, source_target_pairs={{0,4},{1,5},{2,6},{3,7},{4,0},{5,1},{6,2},{7,3},{8,12},{9,13},{10,... | collective-permute-start | bytes 1572872 | tf_op jit(solution)/shard_map/weights/ppermute | solution.py:265
  56.9 26.2 %collective-permute-start.5 = (bf16[512,512]{1,0:T(8,128)(2,1)S(1)}, bf16[512,512]{1,0:T(8,128)(2,1)S(1)}, u32[]{:S(2)}, u32[]{:S(2)}) collective-permute-start(bf16[512,512]{1,0:T(8,128)(2,1)S(1)} %get-tuple-element.23), channel_id=1, source_target_pairs={{0,2},{1,3},{2,4},{3,5},{4,6},{5,7},{6,0},{7,1},{8,10},{9,11},{10,... | collective-permute-start | bytes 1572872 | tf_op jit(solution)/shard_map/weights/ppermute | solution.py:265
  57.6 11.5 %collective-permute-start.2 = (bf16[128,640]{1,0:T(8,128)(2,1)S(1)}, bf16[128,640]{1,0:T(8,128)(2,1)S(1)}, u32[]{:S(2)}, u32[]{:S(2)}) collective-permute-start(bf16[128,640]{1,0:T(8,128)(2,1)S(1)} %bitcast.31), channel_id=1, source_target_pairs={{0,16},{8,24},{16,0},{24,8},{32,48},{40,56},{48,32},{56,40},{64,80... | collective-permute-start | bytes 491528 | tf_op jit(solution)/shard_map/attend/ppermute | solution.py:261
  63.6 7.4 %collective-permute-start.4 = (bf16[128,640]{1,0:T(8,128)(2,1)S(1)}, bf16[128,640]{1,0:T(8,128)(2,1)S(1)}, u32[]{:S(2)}, u32[]{:S(2)}) collective-permute-start(bf16[128,640]{1,0:T(8,128)(2,1)S(1)} %bitcast.30), channel_id=1, source_target_pairs={{0,8},{8,16},{16,24},{24,0},{32,40},{40,48},{48,56},{56,32},{64,72... | collective-permute-start | bytes 491528 | tf_op jit(solution)/shard_map/attend/ppermute | solution.py:261
  83.2 27.3 %copy-start.1 = (bf16[512,512]{1,0:T(8,128)(2,1)S(1)}, bf16[512,512]{1,0:T(8,128)(2,1)}, u32[]{:S(2)}) copy-start(bf16[512,512]{1,0:T(8,128)(2,1)} %wo_ref.1) | copy-start | bytes 1572868
  83.2 27.3 %copy-start.2 = (bf16[1,32,512]{2,1,0:T(8,128)(2,1)S(1)}, bf16[1,32,512]{2,1,0:T(8,128)(2,1)}, u32[]{:S(2)}) copy-start(bf16[1,32,512]{2,1,0:T(8,128)(2,1)} %param.14) | copy-start | bytes 98308
  83.2 27.3 %copy-start.3 = (f32[512]{0:T(512)S(1)}, f32[512]{0:T(512)}, u32[]{:S(2)}) copy-start(f32[512]{0:T(512)} %param.16) | copy-start | bytes 6148
  83.4 27.0 %collective-permute-start.8 = (bf16[4,512,512]{2,1,0:T(8,128)(2,1)S(1)}, bf16[4,512,512]{2,1,0:T(8,128)(2,1)}, u32[]{:S(2)}, u32[]{:S(2)}) collective-permute-start(bf16[4,512,512]{2,1,0:T(8,128)(2,1)S(1)} %pad_maximum_fusion.own_ref), channel_id=1, source_target_pairs={{0,1},{1,0},{2,3},{3,2},{4,5},{5,4},{6,7},{7,6},{8,9},{9,8},{10,11... | collective-permute-start | bytes 6291464 | tf_op jit(solution)/shard_map/weights/ppermute | solution.py:269
  84.0 17.7 %all-to-all-start.1 = ((bf16[8,16,640]{2,1,0:T(8,128)(2,1)}), bf16[8,16,640]{2,1,0:T(8,128)(2,1)S(1)}, u32[]{:S(2)}, u32[]{:S(2)}) async-start(bf16[8,16,640]{2,1,0:T(8,128)(2,1)} %bitcast.14), calls=%async_computation.1 | async-start | bytes 327680 | tf_op jit(solution)/shard_map/join_z/all_to_all | solution.py:352
  102.6 7.8 %all-to-all-start.2 = ((bf16[4,16,640]{2,1,0:T(8,128)(2,1)}), bf16[4,16,640]{2,1,0:T(8,128)(2,1)S(1)}, u32[]{:S(2)}, u32[]{:S(2)}) async-start(bf16[4,16,640]{2,1,0:T(8,128)(2,1)} %join_pieces.3), calls=%async_computation.2 | async-start | bytes 163840 | tf_op jit(solution)/shard_map/join_t/all_to_all | solution.py:361
  113.4 3.6 %collective-permute-start.9 = (bf16[16,512]{1,0:T(8,128)(2,1)S(1)}, bf16[16,512]{1,0:T(8,128)(2,1)S(1)}, u32[]{:S(2)}, u32[]{:S(2)}) collective-permute-start(bf16[16,512]{1,0:T(8,128)(2,1)S(1)} %final.1), channel_id=1, source_target_pairs={{0,1},{1,0},{2,3},{3,2},{4,5},{5,4},{6,7},{7,6},{8,9},{9,8},{10,11... | collective-permute-start | bytes 49160 | tf_op jit(solution)/shard_map/final/ppermute | solution.py:269

commit v3 on v2

v3 whole, which is shorter than its diff:
```python
import functools

import jax
import jax.numpy as jnp
from jax import lax
from jax.experimental import pallas as pl
from jax.experimental.pallas import tpu as pltpu
from jax.sharding import PartitionSpec as P

H = 8
BLK = 256
NZ, NX = 8, 4
EPS = 1e-05
NEG = -1e30
D = 512
DH = 64
LR = 32
WIDE = D + 128
HALF = LR // 2
ROOM = 28 << 20
BF = jnp.bfloat16
F32 = jnp.float32


def lanes_of(shape):
    return lax.broadcasted_iota(jnp.int32, shape, len(shape) - 1)


def norm_rows(values, gain):
    average = jnp.mean(values, axis=-1, keepdims=True)
    centered = values - average
    variance = jnp.mean(centered * centered, axis=-1, keepdims=True)
    return centered * lax.rsqrt(variance + EPS) * gain


def whole(shape):
    return pl.BlockSpec(shape, lambda *_: (0,) * len(shape))


def query_kernel(half_ref, lat_ref, gain_ref, wq_ref, out_ref, q_s):
    normed = norm_rows(lat_ref[...].astype(F32), gain_ref[...]).astype(BF)
    q = jnp.dot(normed, wq_ref[...], preferred_element_type=F32).astype(BF)
    q_s[...] = q * jnp.asarray(DH ** -0.5, BF)
    rows = q_s[pl.ds(pl.multiple_of(half_ref[0] * 16, 16), 16), :]
    out_ref[...] = jnp.broadcast_to(rows[None], out_ref.shape)


def keyval_kernel(mine_ref, other_ref, w_ref, up_ref, down_ref, kv_ref, mlp_ref):
    @pl.when(pl.program_id(0) == 0)
    def _():
        mlp_ref[:, :256] = up_ref[...]
        mlp_ref[:256, 256:] = down_ref[:, :256]
        mlp_ref[256:, 256:] = down_ref[:, 256:]

    for slot, obs_ref in enumerate((mine_ref, other_ref)):
        kv_ref[slot] = jnp.dot(obs_ref[...], w_ref[...], preferred_element_type=F32).astype(BF)


def pack_stats(lse):
    lane = lanes_of(lse.shape)
    high = lse.astype(BF).astype(F32)
    rest = lse - high
    mid = rest.astype(BF).astype(F32)
    low = rest - mid
    kept = jnp.where(lane < 8, high, jnp.where(lane < 16, mid, jnp.where(lane < 24, low, 0.0)))
    return kept.astype(BF)


def attend_kernel(shifts, meta_ref, vis_ref, near_ref, kv_in, *rest):
    outs, rest = rest[: len(shifts)], rest[len(shifts) :]
    kv_ref, list_ref, q_s, v_s, st_s, out_s, sems = rest
    copies = []
    for p in range(H // 2):
        parts = [pl.ds(128 * p, 128), pl.ds(D + 128 * p, 128)]
        copies.append(
            [
                pltpu.make_async_copy(kv_in.at[:, :, part], kv_ref.at[:, :, part], sems.at[k, p])
                for k, part in enumerate(parts)
            ]
        )
        for copy in copies[-1]:
            copy.start()
    counts = meta_ref[0], meta_ref[1]
    most = jnp.maximum(counts[0], counts[1])
    own, x = meta_ref[2], meta_ref[3]
    limit = NZ * len(shifts)
    columns = [lax.rem(x - d + NX, NX) for d in shifts]
    seen = jnp.int32(0)
    for j, column in enumerate(columns):
        for e in range(NZ):
            region = e * NX + column
            list_ref[0, seen] = region
            list_ref[1, seen] = jnp.int32(j * NZ + e)
            sees = (vis_ref[region] > 0) | (region == own)
            seen = seen + sees.astype(jnp.int32)
    last = jnp.maximum(seen - 1, 0)
    for k in range(limit):
        q_s[HALF * k : HALF * (k + 1), :] = near_ref[list_ref[0, jnp.minimum(k, last)]]

    lane = lanes_of((HALF, 128))
    out_s[:, :, :D] = jnp.zeros((limit, HALF, D), BF)
    out_s[:, :, D:] = jnp.broadcast_to(
        jnp.where(lane < 8, NEG, 0.0).astype(BF)[None], (limit, HALF, 128)
    )

    def pair(p, rows, blocks):
        keys = blocks * BLK
        low_half = lanes_of((rows, 128)) < DH
        here = pl.ds(pl.multiple_of(128 * p, 128), 128)
        there = pl.ds(pl.multiple_of(D + 128 * p, 128), 128)
        qp = q_s[:rows, here]
        zero = jnp.zeros_like(qp)
        both = jnp.concatenate([jnp.where(low_half, qp, zero), jnp.where(low_half, zero, qp)], 0)
        slots = []
        for slot in range(2):
            scores = lax.dot_general(
                both, kv_ref[slot, :keys, here], (((1,), (1,)), ((), ())), preferred_element_type=F32
            )
            parts = [scores[:, :BLK]]
            for j in range(1, blocks):
                parts.append(jnp.where(counts[slot] > j, scores[:, j * BLK : (j + 1) * BLK], NEG))
            slots.append(jnp.concatenate(parts, 1))
        peak = jnp.maximum(*[jnp.max(scores, axis=-1, keepdims=True) for scores in slots])
        even = odd = total = None
        for slot, scores in enumerate(slots):
            weights = jnp.exp(scores - peak)
            added = jnp.sum(weights, axis=-1, keepdims=True)
            weights, v = weights.astype(BF), kv_ref[slot, :keys, there]
            e = jnp.dot(weights[:rows], v, preferred_element_type=F32)
            o = jnp.dot(weights[rows:], v, preferred_element_type=F32)
            total = added if total is None else total + added
            even = e if even is None else even + e
            odd = o if odd is None else odd + o
        value = jnp.where(low_half, even / total[:rows], odd / total[rows:])
        v_s[:rows, here] = value.astype(BF)
        lse = peak + jnp.log(total)
        within = lanes_of((rows, 128)) & 7
        st_s[:rows, :] = jnp.where(
            within == 2 * p, lse[:rows], jnp.where(within == 2 * p + 1, lse[rows:], st_s[:rows, :])
        )

    sizes = [r for r in (12, 16, 24) if r <= limit] or [limit]

    def one_pair(p, carry):
        for q in range(H // 2):

            @pl.when(p == q)
            def _():
                for copy in copies[q]:
                    copy.wait()

        for blocks in (2, 8):
            for below, regions in zip([0] + sizes, sizes):
                fits = (seen > below) & (seen <= regions)

                @pl.when(fits & ((most <= 2) if blocks == 2 else (most > 2)))
                def _():
                    pair(p, regions * HALF, blocks)

        return carry

    lax.fori_loop(0, H // 2, one_pair, 0)
    for k in range(limit):

        @pl.when(k < seen)
        def _():
            e = list_ref[1, k]
            out_s[e, :, :D] = v_s[HALF * k : HALF * (k + 1), :]
            out_s[e, :, D:] = pack_stats(st_s[HALF * k : HALF * (k + 1), :])

    for j, out in enumerate(outs):
        out[...] = out_s[NZ * j : NZ * (j + 1)]


def attend(shifts, meta, seen_by, near, keyval):
    scalars = pl.BlockSpec(memory_space=pltpu.SMEM)
    vectors = pl.BlockSpec(memory_space=pltpu.VMEM)
    source = pl.BlockSpec(memory_space=pltpu.HBM)
    limit = NZ * len(shifts)
    return pl.pallas_call(
        functools.partial(attend_kernel, shifts),
        out_shape=[jax.ShapeDtypeStruct((NZ, HALF, WIDE), BF)] * len(shifts),
        in_specs=[scalars] * 2 + [vectors, source],
        out_specs=[vectors] * len(shifts),
        scratch_shapes=[
            pltpu.VMEM(keyval.shape, BF),
            pltpu.SMEM((2, 32), jnp.int32),
            pltpu.VMEM((limit * HALF, D), BF),
            pltpu.VMEM((limit * HALF, D), BF),
            pltpu.VMEM((limit * HALF, 128), F32),
            pltpu.VMEM((limit, HALF, WIDE), BF),
            pltpu.SemaphoreType.DMA((2, H // 2)),
        ],
        compiler_params=pltpu.CompilerParams(vmem_limit_bytes=58 << 20),
        cost_estimate=pl.CostEstimate(flops=4 << 30, bytes_accessed=12 << 20, transcendentals=4 << 20),
        name="attend",
    )(meta, seen_by, near, keyval)


def spread_matrix():
    row = lax.broadcasted_iota(jnp.int32, (128, WIDE), 0)
    col = lax.broadcasted_iota(jnp.int32, (128, WIDE), 1)
    head = jnp.where(col < D, col // DH, jnp.where(col < D + 24, col & 7, -1))
    return jnp.where((row < 24) & ((row & 7) == head), 1.0, 0.0).astype(BF)


def join(pieces, spread):
    lses = [jnp.dot(p[:, D:], spread, preferred_element_type=F32) for p in pieces]
    highest = functools.reduce(jnp.maximum, lses)
    scales = [jnp.exp(l - highest) for l in lses]
    total = functools.reduce(jnp.add, scales)
    value = functools.reduce(
        jnp.add, [p[:, :D].astype(F32) * s[:, :D] for p, s in zip(pieces, scales)]
    )
    return value / total[:, :D], (highest + jnp.log(total))[:, D:]


def join_kernel(*refs):
    *ins, out = refs
    pieces = [r[...] for r in ins] if len(ins) > 1 else [ins[0][k] for k in range(ins[0].shape[0])]
    value, lse = join(pieces, spread_matrix())
    out[..., :D] = jnp.broadcast_to(value.astype(BF), (*out.shape[:-1], D))
    out[..., D:] = jnp.broadcast_to(pack_stats(lse), (*out.shape[:-1], 128))


def joined(pieces, shape):
    return pl.pallas_call(
        join_kernel,
        out_shape=jax.ShapeDtypeStruct(shape, BF),
        in_specs=[pl.BlockSpec(memory_space=pltpu.VMEM)] * len(pieces),
        out_specs=pl.BlockSpec(memory_space=pltpu.VMEM),
        compiler_params=pltpu.CompilerParams(vmem_limit_bytes=ROOM),
        name="join_pieces",
    )(*pieces)


def final_kernel(row_ref, pieces_ref, lat_ref, gain_ref, wo_ref, *refs):
    weights, (res_ref, part_ref, sums) = refs[:4], refs[4:]
    spread = spread_matrix()
    halves = [join([pieces_ref[2 * k + c] for k in range(4)], spread)[0] for c in range(2)]
    attended = jnp.concatenate(halves, 0).astype(BF)
    residual = lat_ref[...].astype(F32) + jnp.dot(attended, wo_ref[...], preferred_element_type=F32)
    normed = norm_rows(residual, gain_ref[...]).astype(BF)
    res_ref[...] = residual
    for k, w in enumerate(weights):
        v = jnp.dot(normed, w[:, :256], preferred_element_type=F32)
        hidden = jax.nn.gelu(v, approximate=True).astype(BF)
        down = jnp.concatenate([w[:256, 256:], w[256:, 256:]], 1)
        sums[lax.rem(row_ref[0] - k + 4, 4)] = jnp.dot(hidden, down, preferred_element_type=F32)
    part_ref[...] = (sums[0] + sums[1]) + (sums[2] + sums[3])


def shifted_x(a, by):
    pairs = [
        (zz * NX + xx, zz * NX + (xx + by) % NX) for zz in range(NZ) for xx in range(NX)
    ]
    return lax.ppermute(a, "region", pairs) if by % NX else a


def shifted_y(a, by):
    return lax.ppermute(a, "tm", [(k, (k + 2 * by) % 8) for k in range(8)]) if by % 4 else a


def core_swapped(a):
    return lax.ppermute(a, "tm", [(k, k ^ 1) for k in range(8)])


def on_device(
    observations,
    counts,
    visible,
    latents,
    lat_gain,
    mlp_gain,
    w_query,
    w_keyval,
    w_out,
    w_up,
    w_down,
):
    own = lax.axis_index("region")
    slot = lax.axis_index("tm")
    x, row, core = own % NX, slot // 2, slot % 2
    observed = observations[0, 0]
    lat = latents[0]
    scalars = pl.BlockSpec(memory_space=pltpu.SMEM)
    vectors = pl.BlockSpec(memory_space=pltpu.VMEM)

    with jax.named_scope("queries"):
        q = pl.pallas_call(
            query_kernel,
            out_shape=jax.ShapeDtypeStruct((NZ * NX, HALF, D), BF),
            in_specs=[scalars] + [vectors] * 3,
            out_specs=vectors,
            scratch_shapes=[pltpu.VMEM((LR, D), BF)],
            name="queries",
        )(core[None], lat, lat_gain[None], w_query)
    with jax.named_scope("gather"):
        near = lax.all_to_all(q, "region", 0, 0, tiled=True)

    with jax.named_scope("keyval"):
        other = core_swapped(observed)
        count = counts[0, 0]
        other_count = core_swapped(count)
        length = observed.shape[0]
        block = pl.BlockSpec((BLK, D), lambda i: (i, 0))
        keyval, mlp = pl.pallas_call(
            keyval_kernel,
            grid=(length // BLK,),
            out_shape=[
                jax.ShapeDtypeStruct((2, length, 2 * D), BF),
                jax.ShapeDtypeStruct((D, D), BF),
            ],
            in_specs=[
                block,
                block,
                pl.BlockSpec((D, 2 * D), lambda i: (0, 0)),
                pl.BlockSpec((D, 256), lambda i: (0, 0)),
                pl.BlockSpec((256, D), lambda i: (0, 0)),
            ],
            out_specs=[
                pl.BlockSpec((2, BLK, 2 * D), lambda i: (0, i, 0)),
                pl.BlockSpec((D, D), lambda i: (0, 0)),
            ],
            compiler_params=pltpu.CompilerParams(vmem_limit_bytes=58 << 20),
            cost_estimate=pl.CostEstimate(flops=4 << 30, bytes_accessed=18 << 20, transcendentals=0),
            name="keyval",
        )(observed, other, w_keyval, w_up, w_down)

    with jax.named_scope("weights"):
        shards = [shifted_y(mlp, k) for k in range(4)]

    seen_by = lax.dynamic_slice_in_dim(visible, own, 1, 1)[:, 0]
    meta = jnp.stack([count, other_count, own, x]).astype(jnp.int32)
    with jax.named_scope("attend"):
        far_columns, near_columns = (2, 1, 3), (0,)
        parts = attend(far_columns, meta, seen_by, near, keyval)
        pieces = [
            shifted_x(part.reshape(NZ * HALF, WIDE), -d) for d, part in zip(far_columns, parts)
        ]
        meta, *shards = lax.optimization_barrier((meta, *shards))
        (part,) = attend(near_columns, meta, seen_by, near, keyval)
        pieces.append(part.reshape(NZ * HALF, WIDE))
    with jax.named_scope("join_x"):
        part = joined(pieces, (NZ * HALF, WIDE))
    with jax.named_scope("join_z"):
        groups = [[zz * NX + xx for zz in range(NZ)] for xx in range(NX)]
        part = lax.all_to_all(
            part.reshape(NZ, HALF, WIDE), "region", 0, 0, axis_index_groups=groups, tiled=True
        )
        part = joined([part], (8, HALF, WIDE))
    with jax.named_scope("join_t"):
        pieces = lax.all_to_all(part, "tm", 0, 0, tiled=True)
    with jax.named_scope("final"):
        residual, mine = pl.pallas_call(
            final_kernel,
            out_shape=[jax.ShapeDtypeStruct((LR, D), F32)] * 2,
            in_specs=[scalars] + [vectors] * 8,
            out_specs=[vectors] * 2,
            scratch_shapes=[pltpu.VMEM((4, LR, D), F32)],
            compiler_params=pltpu.CompilerParams(vmem_limit_bytes=ROOM),
            name="final",
        )(row[None], pieces, lat, mlp_gain[None], w_out, *shards)
        out = residual + (mine + core_swapped(mine))
    return out.astype(BF)[None]


def solution(mesh):
    placed = (
        P("region", "tm", None, None),
        P("region", "tm"),
        P(),
        P("region", None, None),
        P(),
        P(),
        P(),
        P(),
        P(),
        P(None, "tm"),
        P("tm", None),
    )
    return jax.shard_map(
        on_device, mesh=mesh, in_specs=placed, out_specs=P("region", None, None), check_vma=False
    )
```

time: 118 us -> 100 us (0.85)
  blocking collectives: 0 us -> 19.5 us
  local copies, waits for them, and re-layouts: 18.7 us -> 2.63 us
  starting transfers between devices: 43.1 us -> 28.9 us
  waiting for transfers between devices: 27.6 us -> 15.8 us
  Pallas kernels: 25.9 us -> 29.3 us
    all_to_all x0 -> x1, blocking collectives: none -> 19.5 us  [on_device(): lax.all_to_all(part.reshape(NZ, HALF, WIDE), 'region', 0, 0, axis_index_g...]
    unnamed x28 -> x14, local copies, waits for them, and re-layouts: 18.5 us -> 1.87 us
    all_to_all x2 -> x1, waiting for transfers between devices: 13.6 us -> 5.58 us  [on_device(): pieces = lax.all_to_all(part, 'tm', 0, 0, tiled=True)]
    ppermute x3, starting transfers between devices: 11.2 us -> 4.29 us  [shifted_x(): return lax.ppermute(a, 'region', pairs) if by % NX else a]
    all_to_all x2 -> x1, starting transfers between devices: 11.8 us -> 6.12 us  [on_device(): pieces = lax.all_to_all(part, 'tm', 0, 0, tiled=True)]
    pallas_call x1, Pallas kernels: 6.9 us -> 10.7 us  [on_device(): pl.pallas_call(keyval_kernel, grid=(length // BLK,), out_shape=[jax.Shape...]
    pallas_call x2, Pallas kernels: 11.7 us -> 13.7 us  [attend(): pl.pallas_call(functools.partial(attend_kernel, shifts), out_shape=[jax.S...]
    ppermute x3, waiting for transfers between devices: 1.97 us -> 0.01 us  [shifted_x(): return lax.ppermute(a, 'region', pairs) if by % NX else a]
  transfers between devices with their start and end apart: 13 -> 11, of which waited for: 7 -> 4; matrix products, arithmetic and copies ran while one was open for 1% -> 2% of each run, Pallas kernels for 14% -> 27%
where the time goes in v3:
time: 100 us; the launch traced here: 98.7 us
  Pallas kernels  29.3 us (29%)
  starting transfers between devices  28.9 us (29%)
  blocking collectives  19.5 us (20%)
  waiting for transfers between devices  15.8 us (16%)
  local copies, waits for them, and re-layouts  2.63 us (3%)
  other arithmetic  1.84 us (2%)
    all_to_all x1, blocking collectives, on_device(): lax.all_to_all(part.reshape(NZ, HALF, WIDE), 'region', 0, 0, axis_index_g...  19.5 us
    pallas_call x2, Pallas kernels, attend(): pl.pallas_call(functools.partial(attend_kernel, shifts), out_shape=[jax.S...  13.7 us
    pallas_call x1, Pallas kernels, on_device(): pl.pallas_call(keyval_kernel, grid=(length // BLK,), out_shape=[jax.Shape...  10.7 us
    all_to_all x1, starting transfers between devices, on_device(): near = lax.all_to_all(q, 'region', 0, 0, tiled=True)  9.3 us
    ppermute x3, waiting for transfers between devices, shifted_y(): lax.ppermute(a, 'tm', [(k, (k + 2 * by) % 8) for k in range(8)])  9.26 us
    all_to_all x1, starting transfers between devices, on_device(): pieces = lax.all_to_all(part, 'tm', 0, 0, tiled=True)  6.12 us
    all_to_all x1, waiting for transfers between devices, on_device(): pieces = lax.all_to_all(part, 'tm', 0, 0, tiled=True)  5.58 us
    ppermute x3, starting transfers between devices, core_swapped(): return lax.ppermute(a, 'tm', [(k, k ^ 1) for k in range(8)])  5.37 us
  transfers between devices with their start and end apart: 11, of which 4 were waited for; matrix products, arithmetic and copies ran while one was open for 2% of the time, Pallas kernels for 27%

profile of v3, /device:TPU:1, one launch (start us, length us, event | category | flops | bytes accessed | tf_op | source)
XLA Modules:
  0.0 98.7 jit_solution(6663389594960147890)
XLA Ops:
  0.0 0.0 copy-start
  0.0 3.2 %collective-permute-start.1 = (bf16[2048,512]{1,0:T(8,128)(2,1)}, bf16[2048,512]{1,0:T(8,128)(2,1)}, u32[]{:S(2)}, u32[]{:S(2)}) collective-permute-start(bf16[2048,512]{1,0:T(8,128)(2,1)} %bitcast.25), channel_id=1, source_target_pairs={{0,1},{1,0},{2,3},{3,2},{4,5},{5,4},{6,7},{7,6},{8,9},{9,8},{10,11... | collective-permute-start | bytes 6291464 | tf_op jit(solution)/shard_map/keyval/ppermute | solution.py:265
  3.2 2.3 %queries.1 = bf16[32,16,512]{2,1,0:T(8,128)(2,1)} custom-call(s32[1]{0:T(128)} %bitcast.6.half_ref, bf16[32,512]{1,0:T(8,128)(2,1)} %bitcast.21, f32[1,512]{1,0:T(1,128)} %bitcast.24, bf16[512,512]{1,0:T(8,128)(2,1)} %wq_ref.1), custom_call_target="tpu_custom_call" | custom-call | tf_op jit(solution)/shard_map/queries/queries/pallas_call | solution.py:290
  5.5 9.3 %all-to-all-start = ((bf16[32,16,512]{2,1,0:T(8,128)(2,1)}), bf16[32,16,512]{2,1,0:T(8,128)(2,1)S(1)}, u32[]{:S(2)}, u32[]{:S(2)}) async-start(bf16[32,16,512]{2,1,0:T(8,128)(2,1)} %queries.1), calls=%async_computation | async-start | bytes 1048576 | tf_op jit(solution)/shard_map/gather/all_to_all | solution.py:299
  14.8 0.0 collective-permute-done.1.other_ref
  14.8 10.7 %keyval.1 = (bf16[2,2048,1024]{2,1,0:T(8,128)(2,1)}, bf16[512,512]{1,0:T(8,128)(2,1)}) custom-call(bf16[2048,512]{1,0:T(8,128)(2,1)} %bitcast.26, bf16[2048,512]{1,0:T(8,128)(2,1)} %collective-permute-done.1.other_ref, bf16[512,1024]{1,0:T(8,128)(2,1)} %w_ref.1, bf16[512,256]{1,0:T(8,128)(2,1)} %up_ref.1, bf16[256,512]{1,0:T(8,128)(2,1)} %down_ref.1), custom_call_target="tpu_custom_call" | custom-call | flops 4294967296 | bytes 18874368 | tf_op jit(solution)/shard_map/keyval/keyval/pallas_call | solution.py:307
  25.5 2.7 %collective-permute-start.7 = (bf16[512,512]{1,0:T(8,128)(2,1)}, bf16[512,512]{1,0:T(8,128)(2,1)S(1)}, u32[]{:S(2)}, u32[]{:S(2)}) collective-permute-start(bf16[512,512]{1,0:T(8,128)(2,1)} %get-tuple-element.23.refs_0_), channel_id=1, source_target_pairs={{0,6},{1,7},{2,0},{3,1},{4,2},{5,3},{6,4},{7,5},{8,14},{9,15},{10,... | collective-permute-start | bytes 1572872 | tf_op jit(solution)/shard_map/weights/ppermute | solution.py:261
  28.3 0.4 collective-permute-start.6
  28.6 0.7 collective-permute-start.5
  29.3 1.1 %collective-permute-start = (s32[]{:T(128)}, s32[]{:T(128)}, u32[]{:S(2)}, u32[]{:S(2)}) collective-permute-start(s32[]{:T(128)} %bitcast.2), channel_id=1, source_target_pairs={{0,1},{1,0},{2,3},{3,2},{4,5},{5,4},{6,7},{7,6},{8,9},{9,8},{10,11... | collective-permute-start | bytes 20 | tf_op jit(solution)/shard_map/keyval/ppermute | solution.py:265
  31.1 0.0 copy-done
  31.1 0.8 dynamic-slice_reduce_fusion.vis_ref
  31.9 0.0 collective-permute-done
  31.9 1.2 %pad_add_fusion.meta_ref = s32[4]{0:T(128)} fusion(s32[1]{0:T(128)} %bitcast.5, s32[1]{0:T(128)} %bitcast.4, s32[1]{0:T(128)} %bitcast.3, s32[1]{0:T(128)} %bitcast.18), kind=kLoop, calls=%fused_computation.3 | loop fusion | flops 12 | bytes 32 | tf_op jit(solution)/shard_map/stack | solution.py:334
  33.1 0.0 all-to-all-done.near_ref
  33.1 0.0 copy-start.6
  33.1 0.9 copy-done.6
  34.0 7.5 %attend.2 = (bf16[8,16,640]{2,1,0:T(8,128)(2,1)}, bf16[8,16,640]{2,1,0:T(8,128)(2,1)}, bf16[8,16,640]{2,1,0:T(8,128)(2,1)}) custom-call(s32[4]{0:T(128)} %pad_add_fusion.meta_ref, s32[32]{0:T(128)} %dynamic-slice_reduce_fusion.vis_ref, bf16[32,16,512]{2,1,0:T(8,128)(2,1)} %copy-done.6, bf16[2,2048,1024]{2,1,0:T(8,128)(2,1)} %get-tuple-element.17.kv_in), custom_call_target="tpu_custom_call" | custom-call | flops 4294967296 | bytes 12582912 | tf_op jit(solution)/shard_map/attend/attend/pallas_call | solution.py:180
  41.5 2.8 %collective-permute-start.3 = (bf16[128,640]{1,0:T(8,128)(2,1)}, bf16[128,640]{1,0:T(8,128)(2,1)S(1)}, u32[]{:S(2)}, u32[]{:S(2)}) collective-permute-start(bf16[128,640]{1,0:T(8,128)(2,1)} %bitcast.29), channel_id=1, source_target_pairs={{0,24},{8,0},{16,8},{24,16},{32,56},{40,32},{48,40},{56,48},{64,88... | collective-permute-start | bytes 491528 | tf_op jit(solution)/shard_map/attend/ppermute | solution.py:257
  44.3 0.6 collective-permute-start.2
  44.9 5.8 %collective-permute-done.7.refs_3_ = bf16[512,512]{1,0:T(8,128)(2,1)S(1)} collective-permute-done((bf16[512,512]{1,0:T(8,128)(2,1)}, bf16[512,512]{1,0:T(8,128)(2,1)S(1)}, u32[]{:S(2)}, u32[]{:S(2)}) %collective-permute-start.7) | collective-permute-done | bytes 524320 | tf_op jit(solution)/shard_map/weights/ppermute | solution.py:261
  50.7 0.0 copy-start.4
  50.7 0.0 copy-start.5
  50.7 0.9 collective-permute-start.4
  51.6 0.0 collective-permute-done.6.refs_2_
  51.6 3.4 %collective-permute-done.5.refs_1_ = bf16[512,512]{1,0:T(8,128)(2,1)S(1)} collective-permute-done((bf16[512,512]{1,0:T(8,128)(2,1)}, bf16[512,512]{1,0:T(8,128)(2,1)S(1)}, u32[]{:S(2)}, u32[]{:S(2)}) %collective-permute-start.5) | collective-permute-done | bytes 524320 | tf_op jit(solution)/shard_map/weights/ppermute | solution.py:261
  55.1 6.2 %attend.3 = bf16[8,16,640]{2,1,0:T(8,128)(2,1)} custom-call(s32[4]{0:T(128)} %pad_add_fusion.meta_ref, s32[32]{0:T(128)} %dynamic-slice_reduce_fusion.vis_ref, bf16[32,16,512]{2,1,0:T(8,128)(2,1)} %copy-done.6, bf16[2,2048,1024]{2,1,0:T(8,128)(2,1)} %get-tuple-element.17.kv_in), custom_call_target="tpu_custom_call" | custom-call | flops 4294967296 | bytes 12582912 | tf_op jit(solution)/shard_map/attend/attend/pallas_call | solution.py:180
  61.3 0.0 copy-start.1
  61.3 0.0 copy-start.2
  61.3 0.0 collective-permute-done.3.refs_1_
  61.3 0.0 collective-permute-done.2.refs_0_
  61.3 0.0 collective-permute-done.4.refs_2_
  61.3 0.0 copy-start.3
  61.3 1.0 copy-done.3
  62.3 0.6 join_pieces.2
  62.9 19.5 %all_to_all.15.refs_0_ = bf16[8,16,640]{2,1,0:T(8,128)(2,1)S(1)} all-to-all(bf16[8,16,640]{2,1,0:T(8,128)(2,1)S(1)} %bitcast.19), channel_id=1, replica_groups={{0,32,64,96,128,160,192,224},{8,40,72,104,136,168,200,232},{16,48,80,11..., dimensions={0} | all-to-all | bytes 327680 | tf_op jit(solution)/shard_map/join_z/all_to_all | solution.py:348
  82.4 0.9 join_pieces.3
  83.3 6.1 %all-to-all-start.2 = ((bf16[8,16,640]{2,1,0:T(8,128)(2,1)}), bf16[8,16,640]{2,1,0:T(8,128)(2,1)S(1)}, u32[]{:S(2)}, u32[]{:S(2)}) async-start(bf16[8,16,640]{2,1,0:T(8,128)(2,1)} %join_pieces.3), calls=%async_computation.2 | async-start | bytes 327680 | tf_op jit(solution)/shard_map/join_t/all_to_all | solution.py:353
  89.5 5.6 %all-to-all-done.2.pieces_ref = bf16[8,16,640]{2,1,0:T(8,128)(2,1)S(1)} async-done(((bf16[8,16,640]{2,1,0:T(8,128)(2,1)}), bf16[8,16,640]{2,1,0:T(8,128)(2,1)S(1)}, u32[]{:S(2)}, u32[]{:S(2)}) %all-to-all-start.2) | async-done | bytes 163872 | tf_op jit(solution)/shard_map/join_t/all_to_all | solution.py:353
  95.0 0.0 copy-done.4
  95.0 0.0 copy-done.5
  95.1 0.0 copy-done.1
  95.1 0.0 copy-done.2
  95.1 1.1 %final.1 = (f32[32,512]{1,0:T(8,128)S(1)}, f32[32,512]{1,0:T(8,128)S(1)}) custom-call(s32[1]{0:T(128)} %bitcast.row_ref, bf16[8,16,640]{2,1,0:T(8,128)(2,1)S(1)} %all-to-all-done.2.pieces_ref, bf16[32,512]{1,0:T(8,128)(2,1)S(1)} %bitcast.22, f32[1,512]{1,0:T(1,128)S(1)} %bitcast.23, bf16[512,512]{1,0:T(8,128)(2,1)S(1)} %copy-done.1, ...), custom_call_target="tpu_custom_call" | custom-call | tf_op jit(solution)/shard_map/final/final/pallas_call | solution.py:355
  96.2 1.0 %collective-permute-start.8 = (f32[32,512]{1,0:T(8,128)S(1)}, f32[32,512]{1,0:T(8,128)S(1)}, u32[]{:S(2)}, u32[]{:S(2)}) collective-permute-start(f32[32,512]{1,0:T(8,128)S(1)} %get-tuple-element.28), channel_id=1, source_target_pairs={{0,1},{1,0},{2,3},{3,2},{4,5},{5,4},{6,7},{7,6},{8,9},{9,8},{10,11... | collective-permute-start | bytes 196616 | tf_op jit(solution)/shard_map/final/ppermute | solution.py:265
  97.1 0.9 collective-permute-done.8
  98.1 0.6 fusion
Async XLA Ops:
  0.0 31.1 %copy-start = (s32[32,32]{1,0:T(8,128)S(1)}, s32[32,32]{1,0:T(8,128)}, u32[]{:S(2)}) copy-start(s32[32,32]{1,0:T(8,128)} %param.13) | copy-start | bytes 12292
  0.0 14.8 %collective-permute-start.1 = (bf16[2048,512]{1,0:T(8,128)(2,1)}, bf16[2048,512]{1,0:T(8,128)(2,1)}, u32[]{:S(2)}, u32[]{:S(2)}) collective-permute-start(bf16[2048,512]{1,0:T(8,128)(2,1)} %bitcast.25), channel_id=1, source_target_pairs={{0,1},{1,0},{2,3},{3,2},{4,5},{5,4},{6,7},{7,6},{8,9},{9,8},{10,11... | collective-permute-start | bytes 6291464 | tf_op jit(solution)/shard_map/keyval/ppermute | solution.py:265
  5.5 27.6 %all-to-all-start = ((bf16[32,16,512]{2,1,0:T(8,128)(2,1)}), bf16[32,16,512]{2,1,0:T(8,128)(2,1)S(1)}, u32[]{:S(2)}, u32[]{:S(2)}) async-start(bf16[32,16,512]{2,1,0:T(8,128)(2,1)} %queries.1), calls=%async_computation | async-start | bytes 1048576 | tf_op jit(solution)/shard_map/gather/all_to_all | solution.py:299
  25.5 25.2 %collective-permute-start.7 = (bf16[512,512]{1,0:T(8,128)(2,1)}, bf16[512,512]{1,0:T(8,128)(2,1)S(1)}, u32[]{:S(2)}, u32[]{:S(2)}) collective-permute-start(bf16[512,512]{1,0:T(8,128)(2,1)} %get-tuple-element.23.refs_0_), channel_id=1, source_target_pairs={{0,6},{1,7},{2,0},{3,1},{4,2},{5,3},{6,4},{7,5},{8,14},{9,15},{10,... | collective-permute-start | bytes 1572872 | tf_op jit(solution)/shard_map/weights/ppermute | solution.py:261
  28.3 23.4 %collective-permute-start.6 = (bf16[512,512]{1,0:T(8,128)(2,1)}, bf16[512,512]{1,0:T(8,128)(2,1)S(1)}, u32[]{:S(2)}, u32[]{:S(2)}) collective-permute-start(bf16[512,512]{1,0:T(8,128)(2,1)} %get-tuple-element.23.refs_0_), channel_id=1, source_target_pairs={{0,4},{1,5},{2,6},{3,7},{4,0},{5,1},{6,2},{7,3},{8,12},{9,13},{10,... | collective-permute-start | bytes 1572872 | tf_op jit(solution)/shard_map/weights/ppermute | solution.py:261
  28.6 26.4 %collective-permute-start.5 = (bf16[512,512]{1,0:T(8,128)(2,1)}, bf16[512,512]{1,0:T(8,128)(2,1)S(1)}, u32[]{:S(2)}, u32[]{:S(2)}) collective-permute-start(bf16[512,512]{1,0:T(8,128)(2,1)} %get-tuple-element.23.refs_0_), channel_id=1, source_target_pairs={{0,2},{1,3},{2,4},{3,5},{4,6},{5,7},{6,0},{7,1},{8,10},{9,11},{10,... | collective-permute-start | bytes 1572872 | tf_op jit(solution)/shard_map/weights/ppermute | solution.py:261
  29.3 2.6 %collective-permute-start = (s32[]{:T(128)}, s32[]{:T(128)}, u32[]{:S(2)}, u32[]{:S(2)}) collective-permute-start(s32[]{:T(128)} %bitcast.2), channel_id=1, source_target_pairs={{0,1},{1,0},{2,3},{3,2},{4,5},{5,4},{6,7},{7,6},{8,9},{9,8},{10,11... | collective-permute-start | bytes 20 | tf_op jit(solution)/shard_map/keyval/ppermute | solution.py:265
  33.1 0.9 copy-start.6
  41.5 19.8 %collective-permute-start.3 = (bf16[128,640]{1,0:T(8,128)(2,1)}, bf16[128,640]{1,0:T(8,128)(2,1)S(1)}, u32[]{:S(2)}, u32[]{:S(2)}) collective-permute-start(bf16[128,640]{1,0:T(8,128)(2,1)} %bitcast.29), channel_id=1, source_target_pairs={{0,24},{8,0},{16,8},{24,16},{32,56},{40,32},{48,40},{56,48},{64,88... | collective-permute-start | bytes 491528 | tf_op jit(solution)/shard_map/attend/ppermute | solution.py:257
  44.3 17.0 %collective-permute-start.2 = (bf16[128,640]{1,0:T(8,128)(2,1)}, bf16[128,640]{1,0:T(8,128)(2,1)S(1)}, u32[]{:S(2)}, u32[]{:S(2)}) collective-permute-start(bf16[128,640]{1,0:T(8,128)(2,1)} %bitcast.28), channel_id=1, source_target_pairs={{0,16},{8,24},{16,0},{24,8},{32,48},{40,56},{48,32},{56,40},{64,80... | collective-permute-start | bytes 491528 | tf_op jit(solution)/shard_map/attend/ppermute | solution.py:257
  50.7 44.3 %copy-start.4 = (bf16[1,32,512]{2,1,0:T(8,128)(2,1)S(1)}, bf16[1,32,512]{2,1,0:T(8,128)(2,1)}, u32[]{:S(2)}) copy-start(bf16[1,32,512]{2,1,0:T(8,128)(2,1)} %param.14) | copy-start | bytes 98308
  50.7 44.3 %copy-start.5 = (f32[512]{0:T(512)S(1)}, f32[512]{0:T(512)}, u32[]{:S(2)}) copy-start(f32[512]{0:T(512)} %param.16) | copy-start | bytes 6148
  50.7 10.6 %collective-permute-start.4 = (bf16[128,640]{1,0:T(8,128)(2,1)}, bf16[128,640]{1,0:T(8,128)(2,1)S(1)}, u32[]{:S(2)}, u32[]{:S(2)}) collective-permute-start(bf16[128,640]{1,0:T(8,128)(2,1)} %bitcast.27), channel_id=1, source_target_pairs={{0,8},{8,16},{16,24},{24,0},{32,40},{40,48},{48,56},{56,32},{64,72... | collective-permute-start | bytes 491528 | tf_op jit(solution)/shard_map/attend/ppermute | solution.py:257
  61.3 33.8 %copy-start.1 = (bf16[512,512]{1,0:T(8,128)(2,1)S(1)}, bf16[512,512]{1,0:T(8,128)(2,1)}, u32[]{:S(2)}) copy-start(bf16[512,512]{1,0:T(8,128)(2,1)} %wo_ref.1) | copy-start | bytes 1572868
  61.3 33.8 %copy-start.2 = (bf16[512,512]{1,0:T(8,128)(2,1)S(1)}, bf16[512,512]{1,0:T(8,128)(2,1)}, u32[]{:S(2)}) copy-start(bf16[512,512]{1,0:T(8,128)(2,1)} %get-tuple-element.23.refs_0_) | copy-start | bytes 1572868
  61.3 1.0 %copy-start.3 = (bf16[8,16,640]{2,1,0:T(8,128)(2,1)S(1)}, bf16[8,16,640]{2,1,0:T(8,128)(2,1)}, u32[]{:S(2)}) copy-start(bf16[8,16,640]{2,1,0:T(8,128)(2,1)} %attend.3) | copy-start | bytes 491524
  83.3 11.7 %all-to-all-start.2 = ((bf16[8,16,640]{2,1,0:T(8,128)(2,1)}), bf16[8,16,640]{2,1,0:T(8,128)(2,1)S(1)}, u32[]{:S(2)}, u32[]{:S(2)}) async-start(bf16[8,16,640]{2,1,0:T(8,128)(2,1)} %join_pieces.3), calls=%async_computation.2 | async-start | bytes 327680 | tf_op jit(solution)/shard_map/join_t/all_to_all | solution.py:353
  96.2 1.9 %collective-permute-start.8 = (f32[32,512]{1,0:T(8,128)S(1)}, f32[32,512]{1,0:T(8,128)S(1)}, u32[]{:S(2)}, u32[]{:S(2)}) collective-permute-start(f32[32,512]{1,0:T(8,128)S(1)} %get-tuple-element.28), channel_id=1, source_target_pairs={{0,1},{1,0},{2,3},{3,2},{4,5},{5,4},{6,7},{7,6},{8,9},{9,8},{10,11... | collective-permute-start | bytes 196616 | tf_op jit(solution)/shard_map/final/ppermute | solution.py:265

commit v4 on v1

--- a/solution.py
+++ b/solution.py
@@ -70,9 +70,10 @@
     return kept.astype(BF)
 
 
-def attend_kernel(meta_ref, vis_ref, near_ref, far_ref, k_ref, va_ref, out_ref, list_ref, q_s):
+def attend_kernel(shift, meta_ref, vis_ref, near_ref, far_ref, k_ref, va_ref, out_ref, list_ref, q_s):
     count = meta_ref[0]
-    own, core, column = meta_ref[1], meta_ref[2], meta_ref[3]
+    own, core = meta_ref[1], meta_ref[2]
+    column = lax.rem(meta_ref[3] - shift + NX, NX)
     seen = jnp.int32(0)
     for e in range(NZ):
         region = e * NX + column
@@ -155,11 +156,11 @@
             group(0, regions, 8, unroll)
 
 
-def attend(meta, seen_by, near, far, keys, values):
+def attend(shift, meta, seen_by, near, far, keys, values):
     scalars = pl.BlockSpec(memory_space=pltpu.SMEM)
     vectors = pl.BlockSpec(memory_space=pltpu.VMEM)
     return pl.pallas_call(
-        attend_kernel,
+        functools.partial(attend_kernel, shift),
         out_shape=jax.ShapeDtypeStruct((NZ, LR, WIDE), BF),
         in_specs=[scalars] * 2 + [vectors] * 4,
         out_specs=vectors,
@@ -291,25 +292,25 @@
                 pl.BlockSpec((BLK, 2 * D), lambda i: (i, 0)),
                 pl.BlockSpec((D, D), lambda i: (0, 0)),
             ],
-            compiler_params=pltpu.CompilerParams(vmem_limit_bytes=16 << 20),
+            compiler_params=pltpu.CompilerParams(vmem_limit_bytes=58 << 20),
             cost_estimate=pl.CostEstimate(flops=2 << 30, bytes_accessed=9 << 20, transcendentals=0),
             name="keyval",
         )(observed, w_keyval, w_up, w_down)
 
-    near, values = lax.optimization_barrier((near, values))
+    seen_by = lax.dynamic_slice_in_dim(visible, own, 1, 1)[:, 0]
+    meta = jnp.stack([counts[0, 0], own, core, x]).astype(jnp.int32)
+    near, values, seen_by, meta = lax.optimization_barrier((near, values, seen_by, meta))
     with jax.named_scope("gather"):
         far = core_swapped(near)
     with jax.named_scope("weights"):
         shards = [shifted_y(mlp, k) for k in range(4)]
 
-    seen_by = lax.dynamic_slice_in_dim(visible, own, 1, 1)[:, 0]
     with jax.named_scope("attend"):
         pieces = []
         for d in (2, 1, 3, 0):
-            meta = jnp.stack([counts[0, 0], own, core, (x - d) % NX]).astype(jnp.int32)
             if d == 0:
                 meta, *shards = lax.optimization_barrier((meta, *shards))
-            part = attend(meta, seen_by, near, far, keys, values)
+            part = attend(d, meta, seen_by, near, far, keys, values)
             pieces.append(shifted_x(part.reshape(NZ * LR, WIDE), -d))
     with jax.named_scope("join_x"):
         part = joined(pieces, (NZ * LR, WIDE)).reshape(NZ, LR, WIDE)

time: 104 us -> 104 us (level)
  Pallas kernels: 24.5 us -> 33.7 us
  local copies, waits for them, and re-layouts: 10.4 us -> 3.99 us
  starting transfers between devices: 34.8 us -> 32.3 us
    unnamed x24 -> x14, local copies, waits for them, and re-layouts: 10.2 us -> 3.81 us
    pallas_call x4, Pallas kernels: 14.9 us -> 19.9 us  [attend(): pl.pallas_call(functools.partial(attend_kernel, shift), out_shape=jax.Sha...]
    pallas_call x1, Pallas kernels: 3.76 us -> 8.25 us  [on_device(): pl.pallas_call(keyval_kernel, grid=(observed.shape[0] // BLK,), out_shape...]
    ppermute x3, waiting for transfers between devices: 4.13 us -> 0.57 us  [shifted_x(): return lax.ppermute(a, 'region', pairs) if by % NX else a]
    ppermute x3, starting transfers between devices: 7.88 us -> 4.52 us  [shifted_x(): return lax.ppermute(a, 'region', pairs) if by % NX else a]
    ppermute x3, waiting for transfers between devices: 0.96 us -> 3.08 us  [shifted_y(): lax.ppermute(a, 'tm', [(k, (k + 2 * by) % 8) for k in range(8)])]
  transfers between devices with their start and end apart: 10 -> 10, of which waited for: 5 -> 5; matrix products, arithmetic and copies ran while one was open for 0% -> 0% of each run, Pallas kernels for 18% -> 27%
where the time goes in v4:
time: 104 us; the launch traced here: 103 us
  Pallas kernels  33.7 us (32%)
  starting transfers between devices  32.3 us (31%)
  waiting for transfers between devices  18.8 us (18%)
  blocking collectives  12.8 us (12%)
  local copies, waits for them, and re-layouts  3.99 us (4%)
    pallas_call x4, Pallas kernels, attend(): pl.pallas_call(functools.partial(attend_kernel, shift), out_shape=jax.Sha...  19.9 us
    all_to_all x1, blocking collectives, on_device(): lax.all_to_all(part, 'region', 0, 0, axis_index_groups=groups, tiled=True)  12.8 us
    all_to_all x1, starting transfers between devices, on_device(): near = lax.all_to_all(q, 'region', 0, 0, tiled=True)  11.9 us
    all_to_all x1, starting transfers between devices, on_device(): pieces = lax.all_to_all(part, 'tm', 0, 0, tiled=True)  8.55 us
    pallas_call x1, Pallas kernels, on_device(): pl.pallas_call(keyval_kernel, grid=(observed.shape[0] // BLK,), out_shape...  8.25 us
    all_to_all x1, waiting for transfers between devices, on_device(): pieces = lax.all_to_all(part, 'tm', 0, 0, tiled=True)  7.12 us
    all_to_all x1, waiting for transfers between devices, on_device(): near = lax.all_to_all(q, 'region', 0, 0, tiled=True)  7.1 us
    ppermute x3, starting transfers between devices, shifted_x(): return lax.ppermute(a, 'region', pairs) if by % NX else a  4.52 us
  transfers between devices with their start and end apart: 10, of which 5 were waited for; matrix products, arithmetic and copies ran while one was open for 0% of the time, Pallas kernels for 27%

profile of v4, /device:TPU:1, one launch (start us, length us, event | category | flops | bytes accessed | tf_op | source)
XLA Modules:
  0.0 103.1 jit_solution(2199418987469330631)
XLA Ops:
  0.0 0.0 copy-start
  0.0 2.3 %queries.1 = bf16[32,16,512]{2,1,0:T(8,128)(2,1)} custom-call(s32[1]{0:T(128)} %bitcast.1.half_ref, bf16[32,512]{1,0:T(8,128)(2,1)} %bitcast.19, f32[1,512]{1,0:T(1,128)} %bitcast.25, bf16[512,512]{1,0:T(8,128)(2,1)} %wq_ref.1), custom_call_target="tpu_custom_call" | custom-call | tf_op jit(solution)/shard_map/queries/queries/pallas_call | solution.py:264
  2.3 11.9 %all-to-all-start = ((bf16[32,16,512]{2,1,0:T(8,128)(2,1)}), bf16[32,16,512]{2,1,0:T(8,128)(2,1)S(1)}, u32[]{:S(2)}, u32[]{:S(2)}) async-start(bf16[32,16,512]{2,1,0:T(8,128)(2,1)} %queries.1), calls=%async_computation | async-start | bytes 1048576 | tf_op jit(solution)/shard_map/gather/all_to_all | solution.py:273
  14.8 0.0 copy-done
  14.8 0.2 dynamic-slice_reduce_fusion.vis_ref
  15.0 0.1 pad_add_fusion.meta_ref
  15.1 8.3 %keyval.1 = (bf16[2048,512]{1,0:T(8,128)(2,1)}, bf16[2048,1024]{1,0:T(8,128)(2,1)}, bf16[512,512]{1,0:T(8,128)(2,1)}) custom-call(bf16[2048,512]{1,0:T(8,128)(2,1)} %bitcast.26, bf16[512,1024]{1,0:T(8,128)(2,1)} %w_ref.1, bf16[512,256]{1,0:T(8,128)(2,1)} %up_ref.1, bf16[256,512]{1,0:T(8,128)(2,1)} %down_ref.1), custom_call_target="tpu_custom_call" | custom-call | flops 2147483648 | bytes 9437184 | tf_op jit(solution)/shard_map/keyval/keyval/pallas_call | solution.py:276
  23.3 7.1 %all-to-all-done.near_ref = bf16[32,16,512]{2,1,0:T(8,128)(2,1)S(1)} async-done(((bf16[32,16,512]{2,1,0:T(8,128)(2,1)}), bf16[32,16,512]{2,1,0:T(8,128)(2,1)S(1)}, u32[]{:S(2)}, u32[]{:S(2)}) %all-to-all-start) | async-done | bytes 524320 | tf_op jit(solution)/shard_map/gather/all_to_all | solution.py:273
  30.4 2.4 %collective-permute-start = (bf16[32,16,512]{2,1,0:T(8,128)(2,1)S(1)}, bf16[32,16,512]{2,1,0:T(8,128)(2,1)S(1)}, u32[]{:S(2)}, u32[]{:S(2)}) collective-permute-start(bf16[32,16,512]{2,1,0:T(8,128)(2,1)S(1)} %all-to-all-done.near_ref), channel_id=1, source_target_pairs={{0,1},{1,0},{2,3},{3,2},{4,5},{5,4},{6,7},{7,6},{8,9},{9,8},{10,11... | collective-permute-start | bytes 1572872 | tf_op jit(solution)/shard_map/gather/ppermute | solution.py:239
  32.8 2.7 %collective-permute-start.6 = (bf16[512,512]{1,0:T(8,128)(2,1)}, bf16[512,512]{1,0:T(8,128)(2,1)S(1)}, u32[]{:S(2)}, u32[]{:S(2)}) collective-permute-start(bf16[512,512]{1,0:T(8,128)(2,1)} %get-tuple-element.27.refs_0_), channel_id=1, source_target_pairs={{0,6},{1,7},{2,0},{3,1},{4,2},{5,3},{6,4},{7,5},{8,14},{9,15},{10,... | collective-permute-start | bytes 1572872 | tf_op jit(solution)/shard_map/weights/ppermute | solution.py:235
  35.6 0.3 collective-permute-start.5
  35.9 0.7 collective-permute-start.4
  36.6 0.0 collective-permute-done.far_ref
  36.6 0.0 copy-start.5
  36.6 2.2 %copy-done.5 = bf16[2048,1024]{1,0:T(8,128)(2,1)S(1)} copy-done((bf16[2048,1024]{1,0:T(8,128)(2,1)S(1)}, bf16[2048,1024]{1,0:T(8,128)(2,1)}, u32[]{:S(2)}) %copy-start.5) | copy-done | bytes 4194328
  38.8 0.0 copy-start.6
  38.8 1.6 %copy-done.6 = bf16[2048,512]{1,0:T(8,128)(2,1)S(1)} copy-done((bf16[2048,512]{1,0:T(8,128)(2,1)S(1)}, bf16[2048,512]{1,0:T(8,128)(2,1)}, u32[]{:S(2)}) %copy-start.6) | copy-done | bytes 2097176
  40.4 5.5 %attend.4 = bf16[8,32,640]{2,1,0:T(8,128)(2,1)S(1)} custom-call(s32[4]{0:T(128)S(1)} %pad_add_fusion.meta_ref, s32[32]{0:T(128)S(1)} %dynamic-slice_reduce_fusion.vis_ref, bf16[32,16,512]{2,1,0:T(8,128)(2,1)S(1)} %all-to-all-done.near_ref, bf16[32,16,512]{2,1,0:T(8,128)(2,1)S(1)} %collective-permute-done.far_ref, bf16[2048,512]{1,0:T(8,128)(2,1)S(1)} %copy-done.6, ...), custom_call_target="tpu_custom_call" | custom-call | flops 2147483648 | bytes 8388608 | tf_op jit(solution)/shard_map/attend/attend/pallas_call | solution.py:162
  45.9 1.9 %collective-permute-start.1 = (bf16[256,640]{1,0:T(8,128)(2,1)S(1)}, bf16[256,640]{1,0:T(8,128)(2,1)S(1)}, u32[]{:S(2)}, u32[]{:S(2)}) collective-permute-start(bf16[256,640]{1,0:T(8,128)(2,1)S(1)} %bitcast.22), channel_id=1, source_target_pairs={{0,16},{8,24},{16,0},{24,8},{32,48},{40,56},{48,32},{56,40},{64,80... | collective-permute-start | bytes 983048 | tf_op jit(solution)/shard_map/attend/ppermute | solution.py:231
  47.8 3.3 %attend.5 = bf16[8,32,640]{2,1,0:T(8,128)(2,1)S(1)} custom-call(s32[4]{0:T(128)S(1)} %pad_add_fusion.meta_ref, s32[32]{0:T(128)S(1)} %dynamic-slice_reduce_fusion.vis_ref, bf16[32,16,512]{2,1,0:T(8,128)(2,1)S(1)} %all-to-all-done.near_ref, bf16[32,16,512]{2,1,0:T(8,128)(2,1)S(1)} %collective-permute-done.far_ref, bf16[2048,512]{1,0:T(8,128)(2,1)S(1)} %copy-done.6, ...), custom_call_target="tpu_custom_call" | custom-call | flops 2147483648 | bytes 8388608 | tf_op jit(solution)/shard_map/attend/attend/pallas_call | solution.py:162
  51.1 2.3 %collective-permute-start.2 = (bf16[256,640]{1,0:T(8,128)(2,1)S(1)}, bf16[256,640]{1,0:T(8,128)(2,1)S(1)}, u32[]{:S(2)}, u32[]{:S(2)}) collective-permute-start(bf16[256,640]{1,0:T(8,128)(2,1)S(1)} %bitcast.23), channel_id=1, source_target_pairs={{0,24},{8,0},{16,8},{24,16},{32,56},{40,32},{48,40},{56,48},{64,88... | collective-permute-start | bytes 983048 | tf_op jit(solution)/shard_map/attend/ppermute | solution.py:231
  53.4 5.5 %attend.6 = bf16[8,32,640]{2,1,0:T(8,128)(2,1)S(1)} custom-call(s32[4]{0:T(128)S(1)} %pad_add_fusion.meta_ref, s32[32]{0:T(128)S(1)} %dynamic-slice_reduce_fusion.vis_ref, bf16[32,16,512]{2,1,0:T(8,128)(2,1)S(1)} %all-to-all-done.near_ref, bf16[32,16,512]{2,1,0:T(8,128)(2,1)S(1)} %collective-permute-done.far_ref, bf16[2048,512]{1,0:T(8,128)(2,1)S(1)} %copy-done.6, ...), custom_call_target="tpu_custom_call" | custom-call | flops 2147483648 | bytes 8388608 | tf_op jit(solution)/shard_map/attend/attend/pallas_call | solution.py:162
  58.9 0.0 collective-permute-done.6.refs_3_
  59.0 0.3 collective-permute-start.3
  59.3 0.0 collective-permute-done.5.refs_2_
  59.3 3.1 %collective-permute-done.4.refs_1_ = bf16[512,512]{1,0:T(8,128)(2,1)S(1)} collective-permute-done((bf16[512,512]{1,0:T(8,128)(2,1)}, bf16[512,512]{1,0:T(8,128)(2,1)S(1)}, u32[]{:S(2)}, u32[]{:S(2)}) %collective-permute-start.4) | collective-permute-done | bytes 524320 | tf_op jit(solution)/shard_map/weights/ppermute | solution.py:235
  62.3 5.5 %attend.7 = bf16[8,32,640]{2,1,0:T(8,128)(2,1)S(1)} custom-call(s32[4]{0:T(128)S(1)} %pad_add_fusion.meta_ref, s32[32]{0:T(128)S(1)} %dynamic-slice_reduce_fusion.vis_ref, bf16[32,16,512]{2,1,0:T(8,128)(2,1)S(1)} %all-to-all-done.near_ref, bf16[32,16,512]{2,1,0:T(8,128)(2,1)S(1)} %collective-permute-done.far_ref, bf16[2048,512]{1,0:T(8,128)(2,1)S(1)} %copy-done.6, ...), custom_call_target="tpu_custom_call" | custom-call | flops 2147483648 | bytes 8388608 | tf_op jit(solution)/shard_map/attend/attend/pallas_call | solution.py:162
  67.9 0.0 copy-start.1
  67.9 0.0 copy-start.2
  67.9 0.0 copy-start.3
  67.9 0.0 copy-start.4
  67.9 0.0 collective-permute-done.1.refs_0_
  67.9 0.0 collective-permute-done.2.refs_1_
  68.0 0.6 collective-permute-done.3.refs_2_
  68.5 1.0 %join_pieces.2 = bf16[256,640]{1,0:T(8,128)(2,1)S(1)} custom-call(bf16[256,640]{1,0:T(8,128)(2,1)S(1)} %collective-permute-done.1.refs_0_, bf16[256,640]{1,0:T(8,128)(2,1)S(1)} %collective-permute-done.2.refs_1_, bf16[256,640]{1,0:T(8,128)(2,1)S(1)} %collective-permute-done.3.refs_2_, bf16[256,640]{1,0:T(8,128)(2,1)S(1)} %bitcast.18), custom_call_target="tpu_custom_call" | custom-call | tf_op jit(solution)/shard_map/join_x/join_pieces/pallas_call | solution.py:201
  69.6 12.8 %all_to_all.15.refs_0_ = bf16[8,32,640]{2,1,0:T(8,128)(2,1)S(1)} all-to-all(bf16[8,32,640]{2,1,0:T(8,128)(2,1)S(1)} %bitcast.17), channel_id=1, replica_groups={{0,32,64,96,128,160,192,224},{8,40,72,104,136,168,200,232},{16,48,80,11..., dimensions={0} | all-to-all | bytes 655360 | tf_op jit(solution)/shard_map/join_z/all_to_all | solution.py:319
  82.3 1.1 %join_pieces.3 = bf16[8,32,640]{2,1,0:T(8,128)(2,1)} custom-call(bf16[8,32,640]{2,1,0:T(8,128)(2,1)S(1)} %all_to_all.15.refs_0_), custom_call_target="tpu_custom_call" | custom-call | tf_op jit(solution)/shard_map/join_z/join_pieces/pallas_call | solution.py:201
  83.4 8.6 %all-to-all-start.2 = ((bf16[8,32,640]{2,1,0:T(8,128)(2,1)}), bf16[8,32,640]{2,1,0:T(8,128)(2,1)S(1)}, u32[]{:S(2)}, u32[]{:S(2)}) async-start(bf16[8,32,640]{2,1,0:T(8,128)(2,1)} %join_pieces.3), calls=%async_computation.2 | async-start | bytes 655360 | tf_op jit(solution)/shard_map/join_t/all_to_all | solution.py:322
  92.0 7.1 %all-to-all-done.2.pieces_ref = bf16[8,32,640]{2,1,0:T(8,128)(2,1)S(1)} async-done(((bf16[8,32,640]{2,1,0:T(8,128)(2,1)}), bf16[8,32,640]{2,1,0:T(8,128)(2,1)S(1)}, u32[]{:S(2)}, u32[]{:S(2)}) %all-to-all-start.2) | async-done | bytes 327712 | tf_op jit(solution)/shard_map/join_t/all_to_all | solution.py:322
  99.1 0.0 copy-done.1
  99.1 0.0 copy-done.2
  99.1 0.0 copy-done.3
  99.1 0.0 copy-done.4
  99.1 1.2 %final.1 = (f32[32,512]{1,0:T(8,128)S(1)}, f32[32,512]{1,0:T(8,128)S(1)}) custom-call(s32[1]{0:T(128)} %bitcast.row_ref, bf16[8,32,640]{2,1,0:T(8,128)(2,1)S(1)} %all-to-all-done.2.pieces_ref, bf16[32,512]{1,0:T(8,128)(2,1)S(1)} %bitcast.20, f32[1,512]{1,0:T(1,128)S(1)} %bitcast.21, bf16[512,512]{1,0:T(8,128)(2,1)S(1)} %copy-done.1, ...), custom_call_target="tpu_custom_call" | custom-call | tf_op jit(solution)/shard_map/final/final/pallas_call | solution.py:324
  100.3 1.2 %collective-permute-start.7 = (f32[32,512]{1,0:T(8,128)S(1)}, f32[32,512]{1,0:T(8,128)S(1)}, u32[]{:S(2)}, u32[]{:S(2)}) collective-permute-start(f32[32,512]{1,0:T(8,128)S(1)} %get-tuple-element.32), channel_id=1, source_target_pairs={{0,1},{1,0},{2,3},{3,2},{4,5},{5,4},{6,7},{7,6},{8,9},{9,8},{10,11... | collective-permute-start | bytes 196616 | tf_op jit(solution)/shard_map/final/ppermute | solution.py:239
  101.5 0.9 collective-permute-done.7
  102.4 0.6 fusion
Async XLA Ops:
  0.0 14.8 %copy-start = (s32[32,32]{1,0:T(8,128)S(1)}, s32[32,32]{1,0:T(8,128)}, u32[]{:S(2)}) copy-start(s32[32,32]{1,0:T(8,128)} %param.13) | copy-start | bytes 12292
  2.3 28.2 %all-to-all-start = ((bf16[32,16,512]{2,1,0:T(8,128)(2,1)}), bf16[32,16,512]{2,1,0:T(8,128)(2,1)S(1)}, u32[]{:S(2)}, u32[]{:S(2)}) async-start(bf16[32,16,512]{2,1,0:T(8,128)(2,1)} %queries.1), calls=%async_computation | async-start | bytes 1048576 | tf_op jit(solution)/shard_map/gather/all_to_all | solution.py:273
  30.4 6.2 %collective-permute-start = (bf16[32,16,512]{2,1,0:T(8,128)(2,1)S(1)}, bf16[32,16,512]{2,1,0:T(8,128)(2,1)S(1)}, u32[]{:S(2)}, u32[]{:S(2)}) collective-permute-start(bf16[32,16,512]{2,1,0:T(8,128)(2,1)S(1)} %all-to-all-done.near_ref), channel_id=1, source_target_pairs={{0,1},{1,0},{2,3},{3,2},{4,5},{5,4},{6,7},{7,6},{8,9},{9,8},{10,11... | collective-permute-start | bytes 1572872 | tf_op jit(solution)/shard_map/gather/ppermute | solution.py:239
  32.8 26.1 %collective-permute-start.6 = (bf16[512,512]{1,0:T(8,128)(2,1)}, bf16[512,512]{1,0:T(8,128)(2,1)S(1)}, u32[]{:S(2)}, u32[]{:S(2)}) collective-permute-start(bf16[512,512]{1,0:T(8,128)(2,1)} %get-tuple-element.27.refs_0_), channel_id=1, source_target_pairs={{0,6},{1,7},{2,0},{3,1},{4,2},{5,3},{6,4},{7,5},{8,14},{9,15},{10,... | collective-permute-start | bytes 1572872 | tf_op jit(solution)/shard_map/weights/ppermute | solution.py:235
  35.6 23.7 %collective-permute-start.5 = (bf16[512,512]{1,0:T(8,128)(2,1)}, bf16[512,512]{1,0:T(8,128)(2,1)S(1)}, u32[]{:S(2)}, u32[]{:S(2)}) collective-permute-start(bf16[512,512]{1,0:T(8,128)(2,1)} %get-tuple-element.27.refs_0_), channel_id=1, source_target_pairs={{0,4},{1,5},{2,6},{3,7},{4,0},{5,1},{6,2},{7,3},{8,12},{9,13},{10,... | collective-permute-start | bytes 1572872 | tf_op jit(solution)/shard_map/weights/ppermute | solution.py:235
  35.9 26.4 %collective-permute-start.4 = (bf16[512,512]{1,0:T(8,128)(2,1)}, bf16[512,512]{1,0:T(8,128)(2,1)S(1)}, u32[]{:S(2)}, u32[]{:S(2)}) collective-permute-start(bf16[512,512]{1,0:T(8,128)(2,1)} %get-tuple-element.27.refs_0_), channel_id=1, source_target_pairs={{0,2},{1,3},{2,4},{3,5},{4,6},{5,7},{6,0},{7,1},{8,10},{9,11},{10,... | collective-permute-start | bytes 1572872 | tf_op jit(solution)/shard_map/weights/ppermute | solution.py:235
  36.6 2.2 %copy-start.5 = (bf16[2048,1024]{1,0:T(8,128)(2,1)S(1)}, bf16[2048,1024]{1,0:T(8,128)(2,1)}, u32[]{:S(2)}) copy-start(bf16[2048,1024]{1,0:T(8,128)(2,1)} %get-tuple-element.24.va_ref) | copy-start | bytes 12582916
  38.8 1.6 %copy-start.6 = (bf16[2048,512]{1,0:T(8,128)(2,1)S(1)}, bf16[2048,512]{1,0:T(8,128)(2,1)}, u32[]{:S(2)}) copy-start(bf16[2048,512]{1,0:T(8,128)(2,1)} %get-tuple-element.23.k_ref) | copy-start | bytes 6291460
  45.9 22.0 %collective-permute-start.1 = (bf16[256,640]{1,0:T(8,128)(2,1)S(1)}, bf16[256,640]{1,0:T(8,128)(2,1)S(1)}, u32[]{:S(2)}, u32[]{:S(2)}) collective-permute-start(bf16[256,640]{1,0:T(8,128)(2,1)S(1)} %bitcast.22), channel_id=1, source_target_pairs={{0,16},{8,24},{16,0},{24,8},{32,48},{40,56},{48,32},{56,40},{64,80... | collective-permute-start | bytes 983048 | tf_op jit(solution)/shard_map/attend/ppermute | solution.py:231
  51.1 16.9 %collective-permute-start.2 = (bf16[256,640]{1,0:T(8,128)(2,1)S(1)}, bf16[256,640]{1,0:T(8,128)(2,1)S(1)}, u32[]{:S(2)}, u32[]{:S(2)}) collective-permute-start(bf16[256,640]{1,0:T(8,128)(2,1)S(1)} %bitcast.23), channel_id=1, source_target_pairs={{0,24},{8,0},{16,8},{24,16},{32,56},{40,32},{48,40},{56,48},{64,88... | collective-permute-start | bytes 983048 | tf_op jit(solution)/shard_map/attend/ppermute | solution.py:231
  59.0 9.6 %collective-permute-start.3 = (bf16[256,640]{1,0:T(8,128)(2,1)S(1)}, bf16[256,640]{1,0:T(8,128)(2,1)S(1)}, u32[]{:S(2)}, u32[]{:S(2)}) collective-permute-start(bf16[256,640]{1,0:T(8,128)(2,1)S(1)} %bitcast.24), channel_id=1, source_target_pairs={{0,8},{8,16},{16,24},{24,0},{32,40},{40,48},{48,56},{56,32},{64,72... | collective-permute-start | bytes 983048 | tf_op jit(solution)/shard_map/attend/ppermute | solution.py:231
  67.9 31.2 %copy-start.1 = (bf16[512,512]{1,0:T(8,128)(2,1)S(1)}, bf16[512,512]{1,0:T(8,128)(2,1)}, u32[]{:S(2)}) copy-start(bf16[512,512]{1,0:T(8,128)(2,1)} %wo_ref.1) | copy-start | bytes 1572868
  67.9 31.2 %copy-start.2 = (bf16[512,512]{1,0:T(8,128)(2,1)S(1)}, bf16[512,512]{1,0:T(8,128)(2,1)}, u32[]{:S(2)}) copy-start(bf16[512,512]{1,0:T(8,128)(2,1)} %get-tuple-element.27.refs_0_) | copy-start | bytes 1572868
  67.9 31.2 %copy-start.3 = (bf16[1,32,512]{2,1,0:T(8,128)(2,1)S(1)}, bf16[1,32,512]{2,1,0:T(8,128)(2,1)}, u32[]{:S(2)}) copy-start(bf16[1,32,512]{2,1,0:T(8,128)(2,1)} %param.14) | copy-start | bytes 98308
  67.9 31.2 %copy-start.4 = (f32[512]{0:T(512)S(1)}, f32[512]{0:T(512)}, u32[]{:S(2)}) copy-start(f32[512]{0:T(512)} %param.16) | copy-start | bytes 6148
  83.4 15.7 %all-to-all-start.2 = ((bf16[8,32,640]{2,1,0:T(8,128)(2,1)}), bf16[8,32,640]{2,1,0:T(8,128)(2,1)S(1)}, u32[]{:S(2)}, u32[]{:S(2)}) async-start(bf16[8,32,640]{2,1,0:T(8,128)(2,1)} %join_pieces.3), calls=%async_computation.2 | async-start | bytes 655360 | tf_op jit(solution)/shard_map/join_t/all_to_all | solution.py:322
  100.3 2.1 %collective-permute-start.7 = (f32[32,512]{1,0:T(8,128)S(1)}, f32[32,512]{1,0:T(8,128)S(1)}, u32[]{:S(2)}, u32[]{:S(2)}) collective-permute-start(f32[32,512]{1,0:T(8,128)S(1)} %get-tuple-element.32), channel_id=1, source_target_pairs={{0,1},{1,0},{2,3},{3,2},{4,5},{5,4},{6,7},{7,6},{8,9},{9,8},{10,11... | collective-permute-start | bytes 196616 | tf_op jit(solution)/shard_map/final/ppermute | solution.py:239

commit v5 on v4

--- a/solution.py
+++ b/solution.py
@@ -302,18 +302,16 @@
     near, values, seen_by, meta = lax.optimization_barrier((near, values, seen_by, meta))
     with jax.named_scope("gather"):
         far = core_swapped(near)
-    with jax.named_scope("weights"):
-        shards = [shifted_y(mlp, k) for k in range(4)]
-
     with jax.named_scope("attend"):
         pieces = []
         for d in (2, 1, 3, 0):
-            if d == 0:
-                meta, *shards = lax.optimization_barrier((meta, *shards))
             part = attend(d, meta, seen_by, near, far, keys, values)
             pieces.append(shifted_x(part.reshape(NZ * LR, WIDE), -d))
     with jax.named_scope("join_x"):
         part = joined(pieces, (NZ * LR, WIDE)).reshape(NZ, LR, WIDE)
+    part, mlp = lax.optimization_barrier((part, mlp))
+    with jax.named_scope("weights"):
+        shards = [shifted_y(mlp, k) for k in range(4)]
     with jax.named_scope("join_z"):
         groups = [[zz * NX + xx for zz in range(NZ)] for xx in range(NX)]
         part = lax.all_to_all(part, "region", 0, 0, axis_index_groups=groups, tiled=True)

time: 104 us -> 110 us (1.058)
  waiting for transfers between devices: 18.8 us -> 32.3 us
  blocking collectives: 12.8 us -> 0 us
  starting transfers between devices: 32.3 us -> 35.8 us
    all_to_all x1 -> x0, blocking collectives: 12.8 us -> none  [on_device(): lax.all_to_all(part, 'region', 0, 0, axis_index_groups=groups, tiled=True)]
    all_to_all x0 -> x1, waiting for transfers between devices: none -> 7.31 us  [on_device(): lax.all_to_all(part, 'region', 0, 0, axis_index_groups=groups, tiled=True)]
    ppermute x3, waiting for transfers between devices: 3.08 us -> 10 us  [shifted_y(): lax.ppermute(a, 'tm', [(k, (k + 2 * by) % 8) for k in range(8)])]
    all_to_all x1, waiting for transfers between devices: 7.12 us -> 2.48 us  [on_device(): pieces = lax.all_to_all(part, 'tm', 0, 0, tiled=True)]
    all_to_all x0 -> x1, starting transfers between devices: none -> 4.09 us  [on_device(): lax.all_to_all(part, 'region', 0, 0, axis_index_groups=groups, tiled=True)]
    ppermute x3, waiting for transfers between devices: 0.57 us -> 2.96 us  [shifted_x(): return lax.ppermute(a, 'region', pairs) if by % NX else a]
    ppermute x2, waiting for transfers between devices: 0.9 us -> 2.44 us  [core_swapped(): return lax.ppermute(a, 'tm', [(k, k ^ 1) for k in range(8)])]
  transfers between devices with their start and end apart: 10 -> 11, of which waited for: 5 -> 7; matrix products, arithmetic and copies ran while one was open for 0% -> 0% of each run, Pallas kernels for 27% -> 22%
where the time goes in v5:
time: 110 us; the launch traced here: 108 us
  starting transfers between devices  35.8 us (33%)
  Pallas kernels  34.7 us (32%)
  waiting for transfers between devices  32.3 us (29%)
  local copies, waits for them, and re-layouts  3.99 us (4%)
    pallas_call x4, Pallas kernels, attend(): pl.pallas_call(functools.partial(attend_kernel, shift), out_shape=jax.Sha...  20.1 us
    all_to_all x1, starting transfers between devices, on_device(): near = lax.all_to_all(q, 'region', 0, 0, tiled=True)  11.9 us
    ppermute x3, waiting for transfers between devices, shifted_y(): lax.ppermute(a, 'tm', [(k, (k + 2 * by) % 8) for k in range(8)])  10 us
    pallas_call x1, Pallas kernels, on_device(): pl.pallas_call(keyval_kernel, grid=(observed.shape[0] // BLK,), out_shape...  8.24 us
    all_to_all x1, starting transfers between devices, on_device(): pieces = lax.all_to_all(part, 'tm', 0, 0, tiled=True)  7.53 us
    all_to_all x1, waiting for transfers between devices, on_device(): lax.all_to_all(part, 'region', 0, 0, axis_index_groups=groups, tiled=True)  7.31 us
    all_to_all x1, waiting for transfers between devices, on_device(): near = lax.all_to_all(q, 'region', 0, 0, tiled=True)  7.12 us
    ppermute x3, starting transfers between devices, shifted_x(): return lax.ppermute(a, 'region', pairs) if by % NX else a  4.85 us
  transfers between devices with their start and end apart: 11, of which 7 were waited for; matrix products, arithmetic and copies ran while one was open for 0% of the time, Pallas kernels for 22%

profile of v5, /device:TPU:1, one launch (start us, length us, event | category | flops | bytes accessed | tf_op | source)
XLA Modules:
  0.0 108.3 jit_solution(2288231980444126175)
XLA Ops:
  0.0 0.0 copy-start
  0.0 2.3 %queries.1 = bf16[32,16,512]{2,1,0:T(8,128)(2,1)} custom-call(s32[1]{0:T(128)} %bitcast.1.half_ref, bf16[32,512]{1,0:T(8,128)(2,1)} %bitcast.18, f32[1,512]{1,0:T(1,128)} %bitcast.24, bf16[512,512]{1,0:T(8,128)(2,1)} %wq_ref.1), custom_call_target="tpu_custom_call" | custom-call | tf_op jit(solution)/shard_map/queries/queries/pallas_call | solution.py:264
  2.3 11.9 %all-to-all-start = ((bf16[32,16,512]{2,1,0:T(8,128)(2,1)}), bf16[32,16,512]{2,1,0:T(8,128)(2,1)S(1)}, u32[]{:S(2)}, u32[]{:S(2)}) async-start(bf16[32,16,512]{2,1,0:T(8,128)(2,1)} %queries.1), calls=%async_computation | async-start | bytes 1048576 | tf_op jit(solution)/shard_map/gather/all_to_all | solution.py:273
  14.8 0.0 copy-done
  14.8 0.2 dynamic-slice_reduce_fusion.vis_ref
  15.0 0.1 pad_add_fusion.meta_ref
  15.1 8.2 %keyval.1 = (bf16[2048,512]{1,0:T(8,128)(2,1)}, bf16[2048,1024]{1,0:T(8,128)(2,1)}, bf16[512,512]{1,0:T(8,128)(2,1)}) custom-call(bf16[2048,512]{1,0:T(8,128)(2,1)} %bitcast.25, bf16[512,1024]{1,0:T(8,128)(2,1)} %w_ref.1, bf16[512,256]{1,0:T(8,128)(2,1)} %up_ref.1, bf16[256,512]{1,0:T(8,128)(2,1)} %down_ref.1), custom_call_target="tpu_custom_call" | custom-call | flops 2147483648 | bytes 9437184 | tf_op jit(solution)/shard_map/keyval/keyval/pallas_call | solution.py:276
  23.3 7.1 %all-to-all-done.near_ref = bf16[32,16,512]{2,1,0:T(8,128)(2,1)S(1)} async-done(((bf16[32,16,512]{2,1,0:T(8,128)(2,1)}), bf16[32,16,512]{2,1,0:T(8,128)(2,1)S(1)}, u32[]{:S(2)}, u32[]{:S(2)}) %all-to-all-start) | async-done | bytes 524320 | tf_op jit(solution)/shard_map/gather/all_to_all | solution.py:273
  30.4 2.4 %collective-permute-start = (bf16[32,16,512]{2,1,0:T(8,128)(2,1)S(1)}, bf16[32,16,512]{2,1,0:T(8,128)(2,1)S(1)}, u32[]{:S(2)}, u32[]{:S(2)}) collective-permute-start(bf16[32,16,512]{2,1,0:T(8,128)(2,1)S(1)} %all-to-all-done.near_ref), channel_id=1, source_target_pairs={{0,1},{1,0},{2,3},{3,2},{4,5},{5,4},{6,7},{7,6},{8,9},{9,8},{10,11... | collective-permute-start | bytes 1572872 | tf_op jit(solution)/shard_map/gather/ppermute | solution.py:239
  32.8 1.5 %collective-permute-done.far_ref = bf16[32,16,512]{2,1,0:T(8,128)(2,1)S(1)} collective-permute-done((bf16[32,16,512]{2,1,0:T(8,128)(2,1)S(1)}, bf16[32,16,512]{2,1,0:T(8,128)(2,1)S(1)}, u32[]{:S(2)}, u32[]{:S(2)}) %collective-permute-start) | collective-permute-done | bytes 524320 | tf_op jit(solution)/shard_map/gather/ppermute | solution.py:239
  34.4 0.0 copy-start.5
  34.4 2.2 %copy-done.5 = bf16[2048,1024]{1,0:T(8,128)(2,1)S(1)} copy-done((bf16[2048,1024]{1,0:T(8,128)(2,1)S(1)}, bf16[2048,1024]{1,0:T(8,128)(2,1)}, u32[]{:S(2)}) %copy-start.5) | copy-done | bytes 4194328
  36.5 0.0 copy-start.6
  36.5 1.6 %copy-done.6 = bf16[2048,512]{1,0:T(8,128)(2,1)S(1)} copy-done((bf16[2048,512]{1,0:T(8,128)(2,1)S(1)}, bf16[2048,512]{1,0:T(8,128)(2,1)}, u32[]{:S(2)}) %copy-start.6) | copy-done | bytes 2097176
  38.1 5.6 %attend.5 = bf16[8,32,640]{2,1,0:T(8,128)(2,1)S(1)} custom-call(s32[4]{0:T(128)S(1)} %pad_add_fusion.meta_ref, s32[32]{0:T(128)S(1)} %dynamic-slice_reduce_fusion.vis_ref, bf16[32,16,512]{2,1,0:T(8,128)(2,1)S(1)} %all-to-all-done.near_ref, bf16[32,16,512]{2,1,0:T(8,128)(2,1)S(1)} %collective-permute-done.far_ref, bf16[2048,512]{1,0:T(8,128)(2,1)S(1)} %copy-done.6, ...), custom_call_target="tpu_custom_call" | custom-call | flops 2147483648 | bytes 8388608 | tf_op jit(solution)/shard_map/attend/attend/pallas_call | solution.py:162
  43.7 1.6 %collective-permute-start.2 = (bf16[256,640]{1,0:T(8,128)(2,1)S(1)}, bf16[256,640]{1,0:T(8,128)(2,1)S(1)}, u32[]{:S(2)}, u32[]{:S(2)}) collective-permute-start(bf16[256,640]{1,0:T(8,128)(2,1)S(1)} %bitcast.21), channel_id=1, source_target_pairs={{0,24},{8,0},{16,8},{24,16},{32,56},{40,32},{48,40},{56,48},{64,88... | collective-permute-start | bytes 983048 | tf_op jit(solution)/shard_map/attend/ppermute | solution.py:231
  45.3 3.3 %attend.4 = bf16[8,32,640]{2,1,0:T(8,128)(2,1)S(1)} custom-call(s32[4]{0:T(128)S(1)} %pad_add_fusion.meta_ref, s32[32]{0:T(128)S(1)} %dynamic-slice_reduce_fusion.vis_ref, bf16[32,16,512]{2,1,0:T(8,128)(2,1)S(1)} %all-to-all-done.near_ref, bf16[32,16,512]{2,1,0:T(8,128)(2,1)S(1)} %collective-permute-done.far_ref, bf16[2048,512]{1,0:T(8,128)(2,1)S(1)} %copy-done.6, ...), custom_call_target="tpu_custom_call" | custom-call | flops 2147483648 | bytes 8388608 | tf_op jit(solution)/shard_map/attend/attend/pallas_call | solution.py:162
  48.5 1.0 collective-permute-start.1
  49.5 5.5 %attend.6 = bf16[8,32,640]{2,1,0:T(8,128)(2,1)S(1)} custom-call(s32[4]{0:T(128)S(1)} %pad_add_fusion.meta_ref, s32[32]{0:T(128)S(1)} %dynamic-slice_reduce_fusion.vis_ref, bf16[32,16,512]{2,1,0:T(8,128)(2,1)S(1)} %all-to-all-done.near_ref, bf16[32,16,512]{2,1,0:T(8,128)(2,1)S(1)} %collective-permute-done.far_ref, bf16[2048,512]{1,0:T(8,128)(2,1)S(1)} %copy-done.6, ...), custom_call_target="tpu_custom_call" | custom-call | flops 2147483648 | bytes 8388608 | tf_op jit(solution)/shard_map/attend/attend/pallas_call | solution.py:162
  55.1 2.3 %collective-permute-start.3 = (bf16[256,640]{1,0:T(8,128)(2,1)S(1)}, bf16[256,640]{1,0:T(8,128)(2,1)S(1)}, u32[]{:S(2)}, u32[]{:S(2)}) collective-permute-start(bf16[256,640]{1,0:T(8,128)(2,1)S(1)} %bitcast.23), channel_id=1, source_target_pairs={{0,8},{8,16},{16,24},{24,0},{32,40},{40,48},{48,56},{56,32},{64,72... | collective-permute-start | bytes 983048 | tf_op jit(solution)/shard_map/attend/ppermute | solution.py:231
  57.4 5.8 %attend.7 = bf16[8,32,640]{2,1,0:T(8,128)(2,1)S(1)} custom-call(s32[4]{0:T(128)S(1)} %pad_add_fusion.meta_ref, s32[32]{0:T(128)S(1)} %dynamic-slice_reduce_fusion.vis_ref, bf16[32,16,512]{2,1,0:T(8,128)(2,1)S(1)} %all-to-all-done.near_ref, bf16[32,16,512]{2,1,0:T(8,128)(2,1)S(1)} %collective-permute-done.far_ref, bf16[2048,512]{1,0:T(8,128)(2,1)S(1)} %copy-done.6, ...), custom_call_target="tpu_custom_call" | custom-call | flops 2147483648 | bytes 8388608 | tf_op jit(solution)/shard_map/attend/attend/pallas_call | solution.py:162
  63.1 0.0 copy-start.2
  63.1 0.0 copy-start.1
  63.1 0.0 copy-start.3
  63.2 0.0 copy-start.4
  63.2 0.0 collective-permute-done.2.refs_1_
  63.2 0.0 collective-permute-done.1.refs_0_
  63.2 3.0 %collective-permute-done.3.refs_2_ = bf16[256,640]{1,0:T(8,128)(2,1)S(1)} collective-permute-done((bf16[256,640]{1,0:T(8,128)(2,1)S(1)}, bf16[256,640]{1,0:T(8,128)(2,1)S(1)}, u32[]{:S(2)}, u32[]{:S(2)}) %collective-permute-start.3) | collective-permute-done | bytes 327712 | tf_op jit(solution)/shard_map/attend/ppermute | solution.py:231
  66.1 1.8 %join_pieces.2 = bf16[256,640]{1,0:T(8,128)(2,1)} custom-call(bf16[256,640]{1,0:T(8,128)(2,1)S(1)} %collective-permute-done.1.refs_0_, bf16[256,640]{1,0:T(8,128)(2,1)S(1)} %collective-permute-done.2.refs_1_, bf16[256,640]{1,0:T(8,128)(2,1)S(1)} %collective-permute-done.3.refs_2_, bf16[256,640]{1,0:T(8,128)(2,1)S(1)} %bitcast.17), custom_call_target="tpu_custom_call" | custom-call | tf_op jit(solution)/shard_map/join_x/join_pieces/pallas_call | solution.py:201
  67.9 4.1 %all-to-all-start.1 = ((bf16[8,32,640]{2,1,0:T(8,128)(2,1)}), bf16[8,32,640]{2,1,0:T(8,128)(2,1)S(1)}, u32[]{:S(2)}, u32[]{:S(2)}) async-start(bf16[8,32,640]{2,1,0:T(8,128)(2,1)} %bitcast.12), calls=%async_computation.1 | async-start | bytes 655360 | tf_op jit(solution)/shard_map/join_z/all_to_all | solution.py:317
  72.0 0.0 copy-done.2
  72.0 2.8 %collective-permute-start.6 = (bf16[512,512]{1,0:T(8,128)(2,1)S(1)}, bf16[512,512]{1,0:T(8,128)(2,1)S(1)}, u32[]{:S(2)}, u32[]{:S(2)}) collective-permute-start(bf16[512,512]{1,0:T(8,128)(2,1)S(1)} %copy-done.2), channel_id=1, source_target_pairs={{0,6},{1,7},{2,0},{3,1},{4,2},{5,3},{6,4},{7,5},{8,14},{9,15},{10,... | collective-permute-start | bytes 1572872 | tf_op jit(solution)/shard_map/weights/ppermute | solution.py:235
  74.8 0.3 collective-permute-start.5
  75.2 0.7 collective-permute-start.4
  75.9 7.3 %all-to-all-done.1.refs_0_ = bf16[8,32,640]{2,1,0:T(8,128)(2,1)S(1)} async-done(((bf16[8,32,640]{2,1,0:T(8,128)(2,1)}), bf16[8,32,640]{2,1,0:T(8,128)(2,1)S(1)}, u32[]{:S(2)}, u32[]{:S(2)}) %all-to-all-start.1) | async-done | bytes 327712 | tf_op jit(solution)/shard_map/join_z/all_to_all | solution.py:317
  83.2 1.1 %join_pieces.3 = bf16[8,32,640]{2,1,0:T(8,128)(2,1)} custom-call(bf16[8,32,640]{2,1,0:T(8,128)(2,1)S(1)} %all-to-all-done.1.refs_0_), custom_call_target="tpu_custom_call" | custom-call | tf_op jit(solution)/shard_map/join_z/join_pieces/pallas_call | solution.py:201
  84.3 7.5 %all-to-all-start.2 = ((bf16[8,32,640]{2,1,0:T(8,128)(2,1)}), bf16[8,32,640]{2,1,0:T(8,128)(2,1)S(1)}, u32[]{:S(2)}, u32[]{:S(2)}) async-start(bf16[8,32,640]{2,1,0:T(8,128)(2,1)} %join_pieces.3), calls=%async_computation.2 | async-start | bytes 655360 | tf_op jit(solution)/shard_map/join_t/all_to_all | solution.py:320
  91.8 0.0 collective-permute-done.6.refs_3_
  91.8 0.0 collective-permute-done.5.refs_2_
  91.8 10.0 %collective-permute-done.4.refs_1_ = bf16[512,512]{1,0:T(8,128)(2,1)S(1)} collective-permute-done((bf16[512,512]{1,0:T(8,128)(2,1)S(1)}, bf16[512,512]{1,0:T(8,128)(2,1)S(1)}, u32[]{:S(2)}, u32[]{:S(2)}) %collective-permute-start.4) | collective-permute-done | bytes 524320 | tf_op jit(solution)/shard_map/weights/ppermute | solution.py:235
  101.9 2.5 %all-to-all-done.2.pieces_ref = bf16[8,32,640]{2,1,0:T(8,128)(2,1)S(1)} async-done(((bf16[8,32,640]{2,1,0:T(8,128)(2,1)}), bf16[8,32,640]{2,1,0:T(8,128)(2,1)S(1)}, u32[]{:S(2)}, u32[]{:S(2)}) %all-to-all-start.2) | async-done | bytes 327712 | tf_op jit(solution)/shard_map/join_t/all_to_all | solution.py:320
  104.3 0.0 copy-done.1
  104.3 0.0 copy-done.3
  104.3 0.0 copy-done.4
  104.3 1.2 %final.1 = (f32[32,512]{1,0:T(8,128)S(1)}, f32[32,512]{1,0:T(8,128)S(1)}) custom-call(s32[1]{0:T(128)} %bitcast.row_ref, bf16[8,32,640]{2,1,0:T(8,128)(2,1)S(1)} %all-to-all-done.2.pieces_ref, bf16[32,512]{1,0:T(8,128)(2,1)S(1)} %bitcast.19, f32[1,512]{1,0:T(1,128)S(1)} %bitcast.20, bf16[512,512]{1,0:T(8,128)(2,1)S(1)} %copy-done.1, ...), custom_call_target="tpu_custom_call" | custom-call | tf_op jit(solution)/shard_map/final/final/pallas_call | solution.py:322
  105.5 1.2 %collective-permute-start.7 = (f32[32,512]{1,0:T(8,128)S(1)}, f32[32,512]{1,0:T(8,128)S(1)}, u32[]{:S(2)}, u32[]{:S(2)}) collective-permute-start(f32[32,512]{1,0:T(8,128)S(1)} %get-tuple-element.26), channel_id=1, source_target_pairs={{0,1},{1,0},{2,3},{3,2},{4,5},{5,4},{6,7},{7,6},{8,9},{9,8},{10,11... | collective-permute-start | bytes 196616 | tf_op jit(solution)/shard_map/final/ppermute | solution.py:239
  106.8 0.9 collective-permute-done.7
  107.7 0.6 fusion
Async XLA Ops:
  0.0 14.8 %copy-start = (s32[32,32]{1,0:T(8,128)S(1)}, s32[32,32]{1,0:T(8,128)}, u32[]{:S(2)}) copy-start(s32[32,32]{1,0:T(8,128)} %param.13) | copy-start | bytes 12292
  2.3 28.2 %all-to-all-start = ((bf16[32,16,512]{2,1,0:T(8,128)(2,1)}), bf16[32,16,512]{2,1,0:T(8,128)(2,1)S(1)}, u32[]{:S(2)}, u32[]{:S(2)}) async-start(bf16[32,16,512]{2,1,0:T(8,128)(2,1)} %queries.1), calls=%async_computation | async-start | bytes 1048576 | tf_op jit(solution)/shard_map/gather/all_to_all | solution.py:273
  30.4 3.9 %collective-permute-start = (bf16[32,16,512]{2,1,0:T(8,128)(2,1)S(1)}, bf16[32,16,512]{2,1,0:T(8,128)(2,1)S(1)}, u32[]{:S(2)}, u32[]{:S(2)}) collective-permute-start(bf16[32,16,512]{2,1,0:T(8,128)(2,1)S(1)} %all-to-all-done.near_ref), channel_id=1, source_target_pairs={{0,1},{1,0},{2,3},{3,2},{4,5},{5,4},{6,7},{7,6},{8,9},{9,8},{10,11... | collective-permute-start | bytes 1572872 | tf_op jit(solution)/shard_map/gather/ppermute | solution.py:239
  34.4 2.2 %copy-start.5 = (bf16[2048,1024]{1,0:T(8,128)(2,1)S(1)}, bf16[2048,1024]{1,0:T(8,128)(2,1)}, u32[]{:S(2)}) copy-start(bf16[2048,1024]{1,0:T(8,128)(2,1)} %get-tuple-element.21.va_ref) | copy-start | bytes 12582916
  36.5 1.6 %copy-start.6 = (bf16[2048,512]{1,0:T(8,128)(2,1)S(1)}, bf16[2048,512]{1,0:T(8,128)(2,1)}, u32[]{:S(2)}) copy-start(bf16[2048,512]{1,0:T(8,128)(2,1)} %get-tuple-element.20.k_ref) | copy-start | bytes 6291460
  43.7 19.5 %collective-permute-start.2 = (bf16[256,640]{1,0:T(8,128)(2,1)S(1)}, bf16[256,640]{1,0:T(8,128)(2,1)S(1)}, u32[]{:S(2)}, u32[]{:S(2)}) collective-permute-start(bf16[256,640]{1,0:T(8,128)(2,1)S(1)} %bitcast.21), channel_id=1, source_target_pairs={{0,24},{8,0},{16,8},{24,16},{32,56},{40,32},{48,40},{56,48},{64,88... | collective-permute-start | bytes 983048 | tf_op jit(solution)/shard_map/attend/ppermute | solution.py:231
  48.5 14.6 %collective-permute-start.1 = (bf16[256,640]{1,0:T(8,128)(2,1)S(1)}, bf16[256,640]{1,0:T(8,128)(2,1)S(1)}, u32[]{:S(2)}, u32[]{:S(2)}) collective-permute-start(bf16[256,640]{1,0:T(8,128)(2,1)S(1)} %bitcast.22), channel_id=1, source_target_pairs={{0,16},{8,24},{16,0},{24,8},{32,48},{40,56},{48,32},{56,40},{64,80... | collective-permute-start | bytes 983048 | tf_op jit(solution)/shard_map/attend/ppermute | solution.py:231
  55.1 11.1 %collective-permute-start.3 = (bf16[256,640]{1,0:T(8,128)(2,1)S(1)}, bf16[256,640]{1,0:T(8,128)(2,1)S(1)}, u32[]{:S(2)}, u32[]{:S(2)}) collective-permute-start(bf16[256,640]{1,0:T(8,128)(2,1)S(1)} %bitcast.23), channel_id=1, source_target_pairs={{0,8},{8,16},{16,24},{24,0},{32,40},{40,48},{48,56},{56,32},{64,72... | collective-permute-start | bytes 983048 | tf_op jit(solution)/shard_map/attend/ppermute | solution.py:231
  63.1 8.9 %copy-start.2 = (bf16[512,512]{1,0:T(8,128)(2,1)S(1)}, bf16[512,512]{1,0:T(8,128)(2,1)}, u32[]{:S(2)}) copy-start(bf16[512,512]{1,0:T(8,128)(2,1)} %get-tuple-element.24.refs_0_) | copy-start | bytes 1572868
  63.1 41.2 %copy-start.1 = (bf16[512,512]{1,0:T(8,128)(2,1)S(1)}, bf16[512,512]{1,0:T(8,128)(2,1)}, u32[]{:S(2)}) copy-start(bf16[512,512]{1,0:T(8,128)(2,1)} %wo_ref.1) | copy-start | bytes 1572868
  63.1 41.2 %copy-start.3 = (bf16[1,32,512]{2,1,0:T(8,128)(2,1)S(1)}, bf16[1,32,512]{2,1,0:T(8,128)(2,1)}, u32[]{:S(2)}) copy-start(bf16[1,32,512]{2,1,0:T(8,128)(2,1)} %param.14) | copy-start | bytes 98308
  63.2 41.2 %copy-start.4 = (f32[512]{0:T(512)S(1)}, f32[512]{0:T(512)}, u32[]{:S(2)}) copy-start(f32[512]{0:T(512)} %param.16) | copy-start | bytes 6148
  67.9 15.3 %all-to-all-start.1 = ((bf16[8,32,640]{2,1,0:T(8,128)(2,1)}), bf16[8,32,640]{2,1,0:T(8,128)(2,1)S(1)}, u32[]{:S(2)}, u32[]{:S(2)}) async-start(bf16[8,32,640]{2,1,0:T(8,128)(2,1)} %bitcast.12), calls=%async_computation.1 | async-start | bytes 655360 | tf_op jit(solution)/shard_map/join_z/all_to_all | solution.py:317
  72.0 19.8 %collective-permute-start.6 = (bf16[512,512]{1,0:T(8,128)(2,1)S(1)}, bf16[512,512]{1,0:T(8,128)(2,1)S(1)}, u32[]{:S(2)}, u32[]{:S(2)}) collective-permute-start(bf16[512,512]{1,0:T(8,128)(2,1)S(1)} %copy-done.2), channel_id=1, source_target_pairs={{0,6},{1,7},{2,0},{3,1},{4,2},{5,3},{6,4},{7,5},{8,14},{9,15},{10,... | collective-permute-start | bytes 1572872 | tf_op jit(solution)/shard_map/weights/ppermute | solution.py:235
  74.8 17.0 %collective-permute-start.5 = (bf16[512,512]{1,0:T(8,128)(2,1)S(1)}, bf16[512,512]{1,0:T(8,128)(2,1)S(1)}, u32[]{:S(2)}, u32[]{:S(2)}) collective-permute-start(bf16[512,512]{1,0:T(8,128)(2,1)S(1)} %copy-done.2), channel_id=1, source_target_pairs={{0,4},{1,5},{2,6},{3,7},{4,0},{5,1},{6,2},{7,3},{8,12},{9,13},{10,... | collective-permute-start | bytes 1572872 | tf_op jit(solution)/shard_map/weights/ppermute | solution.py:235
  75.2 26.7 %collective-permute-start.4 = (bf16[512,512]{1,0:T(8,128)(2,1)S(1)}, bf16[512,512]{1,0:T(8,128)(2,1)S(1)}, u32[]{:S(2)}, u32[]{:S(2)}) collective-permute-start(bf16[512,512]{1,0:T(8,128)(2,1)S(1)} %copy-done.2), channel_id=1, source_target_pairs={{0,2},{1,3},{2,4},{3,5},{4,6},{5,7},{6,0},{7,1},{8,10},{9,11},{10,... | collective-permute-start | bytes 1572872 | tf_op jit(solution)/shard_map/weights/ppermute | solution.py:235
  84.3 20.0 %all-to-all-start.2 = ((bf16[8,32,640]{2,1,0:T(8,128)(2,1)}), bf16[8,32,640]{2,1,0:T(8,128)(2,1)S(1)}, u32[]{:S(2)}, u32[]{:S(2)}) async-start(bf16[8,32,640]{2,1,0:T(8,128)(2,1)} %join_pieces.3), calls=%async_computation.2 | async-start | bytes 655360 | tf_op jit(solution)/shard_map/join_t/all_to_all | solution.py:320
  105.5 2.1 %collective-permute-start.7 = (f32[32,512]{1,0:T(8,128)S(1)}, f32[32,512]{1,0:T(8,128)S(1)}, u32[]{:S(2)}, u32[]{:S(2)}) collective-permute-start(f32[32,512]{1,0:T(8,128)S(1)} %get-tuple-element.26), channel_id=1, source_target_pairs={{0,1},{1,0},{2,3},{3,2},{4,5},{5,4},{6,7},{7,6},{8,9},{9,8},{10,11... | collective-permute-start | bytes 196616 | tf_op jit(solution)/shard_map/final/ppermute | solution.py:239

commit v6 on v5

--- a/solution.py
+++ b/solution.py
@@ -302,16 +302,20 @@
     near, values, seen_by, meta = lax.optimization_barrier((near, values, seen_by, meta))
     with jax.named_scope("gather"):
         far = core_swapped(near)
+    with jax.named_scope("weights"):
+        across = shifted_y(mlp, 2)
     with jax.named_scope("attend"):
         pieces = []
         for d in (2, 1, 3, 0):
+            if d == 0:
+                meta, across = lax.optimization_barrier((meta, across))
             part = attend(d, meta, seen_by, near, far, keys, values)
             pieces.append(shifted_x(part.reshape(NZ * LR, WIDE), -d))
     with jax.named_scope("join_x"):
         part = joined(pieces, (NZ * LR, WIDE)).reshape(NZ, LR, WIDE)
     part, mlp = lax.optimization_barrier((part, mlp))
     with jax.named_scope("weights"):
-        shards = [shifted_y(mlp, k) for k in range(4)]
+        shards = [mlp, shifted_y(mlp, 1), across, shifted_y(mlp, 3)]
     with jax.named_scope("join_z"):
         groups = [[zz * NX + xx for zz in range(NZ)] for xx in range(NX)]
         part = lax.all_to_all(part, "region", 0, 0, axis_index_groups=groups, tiled=True)

time: 110 us -> 104 us (0.945); the launches traced: 108 us -> 104 us
  Pallas kernels: 34.7 us -> 27.3 us
  starting transfers between devices: 35.8 us -> 40.4 us
  waiting for transfers between devices: 32.3 us -> 30.9 us
    ppermute x3, waiting for transfers between devices: 10 us -> 0.01 us  [shifted_y(): lax.ppermute(a, 'tm', [(k, (k + 2 * by) % 8) for k in range(8)])]
    pallas_call x4, Pallas kernels: 20.1 us -> 12.7 us  [attend(): pl.pallas_call(functools.partial(attend_kernel, shift), out_shape=jax.Sha...]
    all_to_all x1, waiting for transfers between devices: 2.48 us -> 7.13 us  [on_device(): pieces = lax.all_to_all(part, 'tm', 0, 0, tiled=True)]
    all_to_all x1, starting transfers between devices: 4.09 us -> 8.33 us  [on_device(): lax.all_to_all(part, 'region', 0, 0, axis_index_groups=groups, tiled=True)]
    ppermute x3, waiting for transfers between devices: 2.96 us -> 6.2 us  [shifted_x(): return lax.ppermute(a, 'region', pairs) if by % NX else a]
    all_to_all x1, waiting for transfers between devices: 7.31 us -> 9.58 us  [on_device(): lax.all_to_all(part, 'region', 0, 0, axis_index_groups=groups, tiled=True)]
    ppermute x2, waiting for transfers between devices: 2.44 us -> 0.9 us  [core_swapped(): return lax.ppermute(a, 'tm', [(k, k ^ 1) for k in range(8)])]
  transfers between devices with their start and end apart: 11 -> 11, of which waited for: 7 -> 6; matrix products, arithmetic and copies ran while one was open for 0% -> 0% of each run, Pallas kernels for 22% -> 21%
where the time goes in v6:
time: 104 us
  starting transfers between devices  40.4 us (39%)
  waiting for transfers between devices  30.9 us (30%)
  Pallas kernels  27.3 us (26%)
  local copies, waits for them, and re-layouts  3.99 us (4%)
    pallas_call x4, Pallas kernels, attend(): pl.pallas_call(functools.partial(attend_kernel, shift), out_shape=jax.Sha...  12.7 us
    all_to_all x1, starting transfers between devices, on_device(): near = lax.all_to_all(q, 'region', 0, 0, tiled=True)  11.9 us
    all_to_all x1, waiting for transfers between devices, on_device(): lax.all_to_all(part, 'region', 0, 0, axis_index_groups=groups, tiled=True)  9.58 us
    all_to_all x1, starting transfers between devices, on_device(): lax.all_to_all(part, 'region', 0, 0, axis_index_groups=groups, tiled=True)  8.33 us
    pallas_call x1, Pallas kernels, on_device(): pl.pallas_call(keyval_kernel, grid=(observed.shape[0] // BLK,), out_shape...  8.24 us
    all_to_all x1, waiting for transfers between devices, on_device(): pieces = lax.all_to_all(part, 'tm', 0, 0, tiled=True)  7.13 us
    all_to_all x1, waiting for transfers between devices, on_device(): near = lax.all_to_all(q, 'region', 0, 0, tiled=True)  7.12 us
    all_to_all x1, starting transfers between devices, on_device(): pieces = lax.all_to_all(part, 'tm', 0, 0, tiled=True)  6.44 us
  transfers between devices with their start and end apart: 11, of which 6 were waited for; matrix products, arithmetic and copies ran while one was open for 0% of the time, Pallas kernels for 21%

profile of v6, /device:TPU:1, one launch (start us, length us, event | category | flops | bytes accessed | tf_op | source)
XLA Modules:
  0.0 104.2 jit_solution(9006001772823301818)
XLA Ops:
  0.0 0.0 copy-start
  0.0 2.3 %queries.1 = bf16[32,16,512]{2,1,0:T(8,128)(2,1)} custom-call(s32[1]{0:T(128)} %bitcast.1.half_ref, bf16[32,512]{1,0:T(8,128)(2,1)} %bitcast.18, f32[1,512]{1,0:T(1,128)} %bitcast.24, bf16[512,512]{1,0:T(8,128)(2,1)} %wq_ref.1), custom_call_target="tpu_custom_call" | custom-call | tf_op jit(solution)/shard_map/queries/queries/pallas_call | solution.py:264
  2.3 11.9 %all-to-all-start = ((bf16[32,16,512]{2,1,0:T(8,128)(2,1)}), bf16[32,16,512]{2,1,0:T(8,128)(2,1)S(1)}, u32[]{:S(2)}, u32[]{:S(2)}) async-start(bf16[32,16,512]{2,1,0:T(8,128)(2,1)} %queries.1), calls=%async_computation | async-start | bytes 1048576 | tf_op jit(solution)/shard_map/gather/all_to_all | solution.py:273
  14.8 0.0 copy-done
  14.8 0.2 dynamic-slice_reduce_fusion.vis_ref
  15.0 0.1 pad_add_fusion.meta_ref
  15.1 8.2 %keyval.1 = (bf16[2048,512]{1,0:T(8,128)(2,1)}, bf16[2048,1024]{1,0:T(8,128)(2,1)}, bf16[512,512]{1,0:T(8,128)(2,1)}) custom-call(bf16[2048,512]{1,0:T(8,128)(2,1)} %bitcast.25, bf16[512,1024]{1,0:T(8,128)(2,1)} %w_ref.1, bf16[512,256]{1,0:T(8,128)(2,1)} %up_ref.1, bf16[256,512]{1,0:T(8,128)(2,1)} %down_ref.1), custom_call_target="tpu_custom_call" | custom-call | flops 2147483648 | bytes 9437184 | tf_op jit(solution)/shard_map/keyval/keyval/pallas_call | solution.py:276
  23.3 7.1 %all-to-all-done.near_ref = bf16[32,16,512]{2,1,0:T(8,128)(2,1)S(1)} async-done(((bf16[32,16,512]{2,1,0:T(8,128)(2,1)}), bf16[32,16,512]{2,1,0:T(8,128)(2,1)S(1)}, u32[]{:S(2)}, u32[]{:S(2)}) %all-to-all-start) | async-done | bytes 524320 | tf_op jit(solution)/shard_map/gather/all_to_all | solution.py:273
  30.4 2.4 %collective-permute-start = (bf16[32,16,512]{2,1,0:T(8,128)(2,1)S(1)}, bf16[32,16,512]{2,1,0:T(8,128)(2,1)S(1)}, u32[]{:S(2)}, u32[]{:S(2)}) collective-permute-start(bf16[32,16,512]{2,1,0:T(8,128)(2,1)S(1)} %all-to-all-done.near_ref), channel_id=1, source_target_pairs={{0,1},{1,0},{2,3},{3,2},{4,5},{5,4},{6,7},{7,6},{8,9},{9,8},{10,11... | collective-permute-start | bytes 1572872 | tf_op jit(solution)/shard_map/gather/ppermute | solution.py:239
  32.8 2.9 %collective-permute-start.4 = (bf16[512,512]{1,0:T(8,128)(2,1)}, bf16[512,512]{1,0:T(8,128)(2,1)S(1)}, u32[]{:S(2)}, u32[]{:S(2)}) collective-permute-start(bf16[512,512]{1,0:T(8,128)(2,1)} %get-tuple-element.27.refs_0_), channel_id=1, source_target_pairs={{0,4},{1,5},{2,6},{3,7},{4,0},{5,1},{6,2},{7,3},{8,12},{9,13},{10,... | collective-permute-start | bytes 1572872 | tf_op jit(solution)/shard_map/weights/ppermute | solution.py:235
  35.7 0.0 collective-permute-done.far_ref
  35.7 0.0 copy-start.5
  35.7 2.2 %copy-done.5 = bf16[2048,1024]{1,0:T(8,128)(2,1)S(1)} copy-done((bf16[2048,1024]{1,0:T(8,128)(2,1)S(1)}, bf16[2048,1024]{1,0:T(8,128)(2,1)}, u32[]{:S(2)}) %copy-start.5) | copy-done | bytes 4194328
  37.9 0.0 copy-start.6
  37.9 1.6 %copy-done.6 = bf16[2048,512]{1,0:T(8,128)(2,1)S(1)} copy-done((bf16[2048,512]{1,0:T(8,128)(2,1)S(1)}, bf16[2048,512]{1,0:T(8,128)(2,1)}, u32[]{:S(2)}) %copy-start.6) | copy-done | bytes 2097176
  39.5 3.1 %attend.4 = bf16[8,32,640]{2,1,0:T(8,128)(2,1)S(1)} custom-call(s32[4]{0:T(128)S(1)} %pad_add_fusion.meta_ref, s32[32]{0:T(128)S(1)} %dynamic-slice_reduce_fusion.vis_ref, bf16[32,16,512]{2,1,0:T(8,128)(2,1)S(1)} %all-to-all-done.near_ref, bf16[32,16,512]{2,1,0:T(8,128)(2,1)S(1)} %collective-permute-done.far_ref, bf16[2048,512]{1,0:T(8,128)(2,1)S(1)} %copy-done.6, ...), custom_call_target="tpu_custom_call" | custom-call | flops 2147483648 | bytes 8388608 | tf_op jit(solution)/shard_map/attend/attend/pallas_call | solution.py:162
  42.6 2.2 %collective-permute-start.1 = (bf16[256,640]{1,0:T(8,128)(2,1)S(1)}, bf16[256,640]{1,0:T(8,128)(2,1)S(1)}, u32[]{:S(2)}, u32[]{:S(2)}) collective-permute-start(bf16[256,640]{1,0:T(8,128)(2,1)S(1)} %bitcast.21), channel_id=1, source_target_pairs={{0,16},{8,24},{16,0},{24,8},{32,48},{40,56},{48,32},{56,40},{64,80... | collective-permute-start | bytes 983048 | tf_op jit(solution)/shard_map/attend/ppermute | solution.py:231
  44.8 3.3 %attend.5 = bf16[8,32,640]{2,1,0:T(8,128)(2,1)S(1)} custom-call(s32[4]{0:T(128)S(1)} %pad_add_fusion.meta_ref, s32[32]{0:T(128)S(1)} %dynamic-slice_reduce_fusion.vis_ref, bf16[32,16,512]{2,1,0:T(8,128)(2,1)S(1)} %all-to-all-done.near_ref, bf16[32,16,512]{2,1,0:T(8,128)(2,1)S(1)} %collective-permute-done.far_ref, bf16[2048,512]{1,0:T(8,128)(2,1)S(1)} %copy-done.6, ...), custom_call_target="tpu_custom_call" | custom-call | flops 2147483648 | bytes 8388608 | tf_op jit(solution)/shard_map/attend/attend/pallas_call | solution.py:162
  48.1 3.4 %collective-permute-start.2 = (bf16[256,640]{1,0:T(8,128)(2,1)S(1)}, bf16[256,640]{1,0:T(8,128)(2,1)S(1)}, u32[]{:S(2)}, u32[]{:S(2)}) collective-permute-start(bf16[256,640]{1,0:T(8,128)(2,1)S(1)} %bitcast.22), channel_id=1, source_target_pairs={{0,24},{8,0},{16,8},{24,16},{32,56},{40,32},{48,40},{56,48},{64,88... | collective-permute-start | bytes 983048 | tf_op jit(solution)/shard_map/attend/ppermute | solution.py:231
  51.5 3.1 %attend.6 = bf16[8,32,640]{2,1,0:T(8,128)(2,1)S(1)} custom-call(s32[4]{0:T(128)S(1)} %pad_add_fusion.meta_ref, s32[32]{0:T(128)S(1)} %dynamic-slice_reduce_fusion.vis_ref, bf16[32,16,512]{2,1,0:T(8,128)(2,1)S(1)} %all-to-all-done.near_ref, bf16[32,16,512]{2,1,0:T(8,128)(2,1)S(1)} %collective-permute-done.far_ref, bf16[2048,512]{1,0:T(8,128)(2,1)S(1)} %copy-done.6, ...), custom_call_target="tpu_custom_call" | custom-call | flops 2147483648 | bytes 8388608 | tf_op jit(solution)/shard_map/attend/attend/pallas_call | solution.py:162
  54.6 0.1 collective-permute-start.3
  54.7 0.0 collective-permute-done.4.refs_2_
  54.7 3.3 %attend.7 = bf16[8,32,640]{2,1,0:T(8,128)(2,1)S(1)} custom-call(s32[4]{0:T(128)S(1)} %pad_add_fusion.meta_ref, s32[32]{0:T(128)S(1)} %dynamic-slice_reduce_fusion.vis_ref, bf16[32,16,512]{2,1,0:T(8,128)(2,1)S(1)} %all-to-all-done.near_ref, bf16[32,16,512]{2,1,0:T(8,128)(2,1)S(1)} %collective-permute-done.far_ref, bf16[2048,512]{1,0:T(8,128)(2,1)S(1)} %copy-done.6, ...), custom_call_target="tpu_custom_call" | custom-call | flops 2147483648 | bytes 8388608 | tf_op jit(solution)/shard_map/attend/attend/pallas_call | solution.py:162
  58.0 0.0 copy-start.2
  58.0 0.0 copy-start.1
  58.0 0.0 copy-start.3
  58.1 0.0 copy-start.4
  58.1 0.0 collective-permute-done.1.refs_0_
  58.1 1.6 %collective-permute-done.2.refs_1_ = bf16[256,640]{1,0:T(8,128)(2,1)S(1)} collective-permute-done((bf16[256,640]{1,0:T(8,128)(2,1)S(1)}, bf16[256,640]{1,0:T(8,128)(2,1)S(1)}, u32[]{:S(2)}, u32[]{:S(2)}) %collective-permute-start.2) | collective-permute-done | bytes 327712 | tf_op jit(solution)/shard_map/attend/ppermute | solution.py:231
  59.7 4.6 %collective-permute-done.3.refs_2_ = bf16[256,640]{1,0:T(8,128)(2,1)S(1)} collective-permute-done((bf16[256,640]{1,0:T(8,128)(2,1)S(1)}, bf16[256,640]{1,0:T(8,128)(2,1)S(1)}, u32[]{:S(2)}, u32[]{:S(2)}) %collective-permute-start.3) | collective-permute-done | bytes 327712 | tf_op jit(solution)/shard_map/attend/ppermute | solution.py:231
  64.3 1.8 %join_pieces.2 = bf16[256,640]{1,0:T(8,128)(2,1)} custom-call(bf16[256,640]{1,0:T(8,128)(2,1)S(1)} %collective-permute-done.1.refs_0_, bf16[256,640]{1,0:T(8,128)(2,1)S(1)} %collective-permute-done.2.refs_1_, bf16[256,640]{1,0:T(8,128)(2,1)S(1)} %collective-permute-done.3.refs_2_, bf16[256,640]{1,0:T(8,128)(2,1)S(1)} %bitcast.17), custom_call_target="tpu_custom_call" | custom-call | tf_op jit(solution)/shard_map/join_x/join_pieces/pallas_call | solution.py:201
  66.1 8.3 %all-to-all-start.1 = ((bf16[8,32,640]{2,1,0:T(8,128)(2,1)}), bf16[8,32,640]{2,1,0:T(8,128)(2,1)S(1)}, u32[]{:S(2)}, u32[]{:S(2)}) async-start(bf16[8,32,640]{2,1,0:T(8,128)(2,1)} %bitcast.12), calls=%async_computation.1 | async-start | bytes 655360 | tf_op jit(solution)/shard_map/join_z/all_to_all | solution.py:321
  74.4 0.0 copy-done.2
  74.4 1.3 %collective-permute-start.6 = (bf16[512,512]{1,0:T(8,128)(2,1)S(1)}, bf16[512,512]{1,0:T(8,128)(2,1)S(1)}, u32[]{:S(2)}, u32[]{:S(2)}) collective-permute-start(bf16[512,512]{1,0:T(8,128)(2,1)S(1)} %copy-done.2), channel_id=1, source_target_pairs={{0,6},{1,7},{2,0},{3,1},{4,2},{5,3},{6,4},{7,5},{8,14},{9,15},{10,... | collective-permute-start | bytes 1572872 | tf_op jit(solution)/shard_map/weights/ppermute | solution.py:235
  75.7 0.2 collective-permute-start.5
  75.9 9.6 %all-to-all-done.1.refs_0_ = bf16[8,32,640]{2,1,0:T(8,128)(2,1)S(1)} async-done(((bf16[8,32,640]{2,1,0:T(8,128)(2,1)}), bf16[8,32,640]{2,1,0:T(8,128)(2,1)S(1)}, u32[]{:S(2)}, u32[]{:S(2)}) %all-to-all-start.1) | async-done | bytes 327712 | tf_op jit(solution)/shard_map/join_z/all_to_all | solution.py:321
  85.5 1.1 %join_pieces.3 = bf16[8,32,640]{2,1,0:T(8,128)(2,1)} custom-call(bf16[8,32,640]{2,1,0:T(8,128)(2,1)S(1)} %all-to-all-done.1.refs_0_), custom_call_target="tpu_custom_call" | custom-call | tf_op jit(solution)/shard_map/join_z/join_pieces/pallas_call | solution.py:201
  86.6 6.4 %all-to-all-start.2 = ((bf16[8,32,640]{2,1,0:T(8,128)(2,1)}), bf16[8,32,640]{2,1,0:T(8,128)(2,1)S(1)}, u32[]{:S(2)}, u32[]{:S(2)}) async-start(bf16[8,32,640]{2,1,0:T(8,128)(2,1)} %join_pieces.3), calls=%async_computation.2 | async-start | bytes 655360 | tf_op jit(solution)/shard_map/join_t/all_to_all | solution.py:324
  93.1 0.0 collective-permute-done.6.refs_3_
  93.1 0.0 collective-permute-done.5.refs_1_
  93.1 7.1 %all-to-all-done.2.pieces_ref = bf16[8,32,640]{2,1,0:T(8,128)(2,1)S(1)} async-done(((bf16[8,32,640]{2,1,0:T(8,128)(2,1)}), bf16[8,32,640]{2,1,0:T(8,128)(2,1)S(1)}, u32[]{:S(2)}, u32[]{:S(2)}) %all-to-all-start.2) | async-done | bytes 327712 | tf_op jit(solution)/shard_map/join_t/all_to_all | solution.py:324
  100.2 0.0 copy-done.1
  100.2 0.0 copy-done.3
  100.2 0.0 copy-done.4
  100.2 1.2 %final.1 = (f32[32,512]{1,0:T(8,128)S(1)}, f32[32,512]{1,0:T(8,128)S(1)}) custom-call(s32[1]{0:T(128)} %bitcast.row_ref, bf16[8,32,640]{2,1,0:T(8,128)(2,1)S(1)} %all-to-all-done.2.pieces_ref, bf16[32,512]{1,0:T(8,128)(2,1)S(1)} %bitcast.19, f32[1,512]{1,0:T(1,128)S(1)} %bitcast.20, bf16[512,512]{1,0:T(8,128)(2,1)S(1)} %copy-done.1, ...), custom_call_target="tpu_custom_call" | custom-call | tf_op jit(solution)/shard_map/final/final/pallas_call | solution.py:326
  101.4 1.2 %collective-permute-start.7 = (f32[32,512]{1,0:T(8,128)S(1)}, f32[32,512]{1,0:T(8,128)S(1)}, u32[]{:S(2)}, u32[]{:S(2)}) collective-permute-start(f32[32,512]{1,0:T(8,128)S(1)} %get-tuple-element.30), channel_id=1, source_target_pairs={{0,1},{1,0},{2,3},{3,2},{4,5},{5,4},{6,7},{7,6},{8,9},{9,8},{10,11... | collective-permute-start | bytes 196616 | tf_op jit(solution)/shard_map/final/ppermute | solution.py:239
  102.6 0.9 collective-permute-done.7
  103.5 0.6 fusion
Async XLA Ops:
  0.0 14.8 %copy-start = (s32[32,32]{1,0:T(8,128)S(1)}, s32[32,32]{1,0:T(8,128)}, u32[]{:S(2)}) copy-start(s32[32,32]{1,0:T(8,128)} %param.13) | copy-start | bytes 12292
  2.3 28.2 %all-to-all-start = ((bf16[32,16,512]{2,1,0:T(8,128)(2,1)}), bf16[32,16,512]{2,1,0:T(8,128)(2,1)S(1)}, u32[]{:S(2)}, u32[]{:S(2)}) async-start(bf16[32,16,512]{2,1,0:T(8,128)(2,1)} %queries.1), calls=%async_computation | async-start | bytes 1048576 | tf_op jit(solution)/shard_map/gather/all_to_all | solution.py:273
  30.4 5.3 %collective-permute-start = (bf16[32,16,512]{2,1,0:T(8,128)(2,1)S(1)}, bf16[32,16,512]{2,1,0:T(8,128)(2,1)S(1)}, u32[]{:S(2)}, u32[]{:S(2)}) collective-permute-start(bf16[32,16,512]{2,1,0:T(8,128)(2,1)S(1)} %all-to-all-done.near_ref), channel_id=1, source_target_pairs={{0,1},{1,0},{2,3},{3,2},{4,5},{5,4},{6,7},{7,6},{8,9},{9,8},{10,11... | collective-permute-start | bytes 1572872 | tf_op jit(solution)/shard_map/gather/ppermute | solution.py:239
  32.8 21.9 %collective-permute-start.4 = (bf16[512,512]{1,0:T(8,128)(2,1)}, bf16[512,512]{1,0:T(8,128)(2,1)S(1)}, u32[]{:S(2)}, u32[]{:S(2)}) collective-permute-start(bf16[512,512]{1,0:T(8,128)(2,1)} %get-tuple-element.27.refs_0_), channel_id=1, source_target_pairs={{0,4},{1,5},{2,6},{3,7},{4,0},{5,1},{6,2},{7,3},{8,12},{9,13},{10,... | collective-permute-start | bytes 1572872 | tf_op jit(solution)/shard_map/weights/ppermute | solution.py:235
  35.7 2.2 %copy-start.5 = (bf16[2048,1024]{1,0:T(8,128)(2,1)S(1)}, bf16[2048,1024]{1,0:T(8,128)(2,1)}, u32[]{:S(2)}) copy-start(bf16[2048,1024]{1,0:T(8,128)(2,1)} %get-tuple-element.23.va_ref) | copy-start | bytes 12582916
  37.9 1.6 %copy-start.6 = (bf16[2048,512]{1,0:T(8,128)(2,1)S(1)}, bf16[2048,512]{1,0:T(8,128)(2,1)}, u32[]{:S(2)}) copy-start(bf16[2048,512]{1,0:T(8,128)(2,1)} %get-tuple-element.22.k_ref) | copy-start | bytes 6291460
  42.6 15.5 %collective-permute-start.1 = (bf16[256,640]{1,0:T(8,128)(2,1)S(1)}, bf16[256,640]{1,0:T(8,128)(2,1)S(1)}, u32[]{:S(2)}, u32[]{:S(2)}) collective-permute-start(bf16[256,640]{1,0:T(8,128)(2,1)S(1)} %bitcast.21), channel_id=1, source_target_pairs={{0,16},{8,24},{16,0},{24,8},{32,48},{40,56},{48,32},{56,40},{64,80... | collective-permute-start | bytes 983048 | tf_op jit(solution)/shard_map/attend/ppermute | solution.py:231
  48.1 11.6 %collective-permute-start.2 = (bf16[256,640]{1,0:T(8,128)(2,1)S(1)}, bf16[256,640]{1,0:T(8,128)(2,1)S(1)}, u32[]{:S(2)}, u32[]{:S(2)}) collective-permute-start(bf16[256,640]{1,0:T(8,128)(2,1)S(1)} %bitcast.22), channel_id=1, source_target_pairs={{0,24},{8,0},{16,8},{24,16},{32,56},{40,32},{48,40},{56,48},{64,88... | collective-permute-start | bytes 983048 | tf_op jit(solution)/shard_map/attend/ppermute | solution.py:231
  54.6 9.7 %collective-permute-start.3 = (bf16[256,640]{1,0:T(8,128)(2,1)S(1)}, bf16[256,640]{1,0:T(8,128)(2,1)S(1)}, u32[]{:S(2)}, u32[]{:S(2)}) collective-permute-start(bf16[256,640]{1,0:T(8,128)(2,1)S(1)} %bitcast.23), channel_id=1, source_target_pairs={{0,8},{8,16},{16,24},{24,0},{32,40},{40,48},{48,56},{56,32},{64,72... | collective-permute-start | bytes 983048 | tf_op jit(solution)/shard_map/attend/ppermute | solution.py:231
  58.0 16.4 %copy-start.2 = (bf16[512,512]{1,0:T(8,128)(2,1)S(1)}, bf16[512,512]{1,0:T(8,128)(2,1)}, u32[]{:S(2)}) copy-start(bf16[512,512]{1,0:T(8,128)(2,1)} %get-tuple-element.27.refs_0_) | copy-start | bytes 1572868
  58.0 42.2 %copy-start.1 = (bf16[512,512]{1,0:T(8,128)(2,1)S(1)}, bf16[512,512]{1,0:T(8,128)(2,1)}, u32[]{:S(2)}) copy-start(bf16[512,512]{1,0:T(8,128)(2,1)} %wo_ref.1) | copy-start | bytes 1572868
  58.0 42.2 %copy-start.3 = (bf16[1,32,512]{2,1,0:T(8,128)(2,1)S(1)}, bf16[1,32,512]{2,1,0:T(8,128)(2,1)}, u32[]{:S(2)}) copy-start(bf16[1,32,512]{2,1,0:T(8,128)(2,1)} %param.14) | copy-start | bytes 98308
  58.1 42.2 %copy-start.4 = (f32[512]{0:T(512)S(1)}, f32[512]{0:T(512)}, u32[]{:S(2)}) copy-start(f32[512]{0:T(512)} %param.16) | copy-start | bytes 6148
  66.1 19.5 %all-to-all-start.1 = ((bf16[8,32,640]{2,1,0:T(8,128)(2,1)}), bf16[8,32,640]{2,1,0:T(8,128)(2,1)S(1)}, u32[]{:S(2)}, u32[]{:S(2)}) async-start(bf16[8,32,640]{2,1,0:T(8,128)(2,1)} %bitcast.12), calls=%async_computation.1 | async-start | bytes 655360 | tf_op jit(solution)/shard_map/join_z/all_to_all | solution.py:321
  74.4 18.7 %collective-permute-start.6 = (bf16[512,512]{1,0:T(8,128)(2,1)S(1)}, bf16[512,512]{1,0:T(8,128)(2,1)S(1)}, u32[]{:S(2)}, u32[]{:S(2)}) collective-permute-start(bf16[512,512]{1,0:T(8,128)(2,1)S(1)} %copy-done.2), channel_id=1, source_target_pairs={{0,6},{1,7},{2,0},{3,1},{4,2},{5,3},{6,4},{7,5},{8,14},{9,15},{10,... | collective-permute-start | bytes 1572872 | tf_op jit(solution)/shard_map/weights/ppermute | solution.py:235
  75.7 17.4 %collective-permute-start.5 = (bf16[512,512]{1,0:T(8,128)(2,1)S(1)}, bf16[512,512]{1,0:T(8,128)(2,1)S(1)}, u32[]{:S(2)}, u32[]{:S(2)}) collective-permute-start(bf16[512,512]{1,0:T(8,128)(2,1)S(1)} %copy-done.2), channel_id=1, source_target_pairs={{0,2},{1,3},{2,4},{3,5},{4,6},{5,7},{6,0},{7,1},{8,10},{9,11},{10,... | collective-permute-start | bytes 1572872 | tf_op jit(solution)/shard_map/weights/ppermute | solution.py:235
  86.6 13.6 %all-to-all-start.2 = ((bf16[8,32,640]{2,1,0:T(8,128)(2,1)}), bf16[8,32,640]{2,1,0:T(8,128)(2,1)S(1)}, u32[]{:S(2)}, u32[]{:S(2)}) async-start(bf16[8,32,640]{2,1,0:T(8,128)(2,1)} %join_pieces.3), calls=%async_computation.2 | async-start | bytes 655360 | tf_op jit(solution)/shard_map/join_t/all_to_all | solution.py:324
  101.4 2.1 %collective-permute-start.7 = (f32[32,512]{1,0:T(8,128)S(1)}, f32[32,512]{1,0:T(8,128)S(1)}, u32[]{:S(2)}, u32[]{:S(2)}) collective-permute-start(f32[32,512]{1,0:T(8,128)S(1)} %get-tuple-element.30), channel_id=1, source_target_pairs={{0,1},{1,0},{2,3},{3,2},{4,5},{5,4},{6,7},{7,6},{8,9},{9,8},{10,11... | collective-permute-start | bytes 196616 | tf_op jit(solution)/shard_map/final/ppermute | solution.py:239

commit v7 on v4

--- a/solution.py
+++ b/solution.py
@@ -70,31 +70,37 @@
     return kept.astype(BF)
 
 
-def attend_kernel(shift, meta_ref, vis_ref, near_ref, far_ref, k_ref, va_ref, out_ref, list_ref, q_s):
+def attend_kernel(shifts, meta_ref, vis_ref, near_ref, far_ref, k_ref, va_ref, *rest):
+    outs = rest[: len(shifts)]
+    list_ref, q_s, out_ref = rest[len(shifts) :]
     count = meta_ref[0]
     own, core = meta_ref[1], meta_ref[2]
-    column = lax.rem(meta_ref[3] - shift + NX, NX)
     seen = jnp.int32(0)
-    for e in range(NZ):
-        region = e * NX + column
-        list_ref[seen] = jnp.int32(e)
-        sees = (vis_ref[region] > 0) | (region == own)
-        seen = seen + sees.astype(jnp.int32)
-    last = list_ref[jnp.maximum(seen - 1, 0)]
-    for k in range(3):
-        list_ref[seen + k] = last
+    for j, shift in enumerate(shifts):
+        column = lax.rem(meta_ref[3] - shift + NX, NX)
+        for e in range(NZ):
+            region = e * NX + column
+            list_ref[0, seen] = region
+            list_ref[1, seen] = jnp.int32(j * NZ + e)
+            sees = (vis_ref[region] > 0) | (region == own)
+            seen = seen + sees.astype(jnp.int32)
+    last = jnp.maximum(seen - 1, 0)
+    for k in range(4):
+        for row in range(2):
+            list_ref[row, seen + k] = list_ref[row, last]
 
     lane = lanes_of((LR, 128))
-    out_ref[:, :, :D] = jnp.zeros((NZ, LR, D), BF)
+    cells = NZ * len(shifts)
+    out_ref[:, :, :D] = jnp.zeros((cells, LR, D), BF)
     out_ref[:, :, D:] = jnp.broadcast_to(
-        jnp.where(lane < 8, NEG, 0.0).astype(BF)[None], (NZ, LR, 128)
+        jnp.where(lane < 8, NEG, 0.0).astype(BF)[None], (cells, LR, 128)
     )
 
     def group(start, regions, blocks, unroll):
         keys, rows = blocks * BLK, regions * LR
-        entries = [list_ref[start + k] for k in range(regions)]
-        for k, e in enumerate(entries):
-            region = e * NX + column
+        entries = [list_ref[1, start + k] for k in range(regions)]
+        for k in range(regions):
+            region = list_ref[0, start + k]
             q_s[pl.ds(pl.multiple_of(32 * k + 16 * core, 16), 16), :] = near_ref[region]
             q_s[pl.ds(pl.multiple_of(32 * k + 16 - 16 * core, 16), 16), :] = far_ref[region]
         wide = lanes_of((rows, 128))
@@ -149,24 +155,35 @@
 
             lax.fori_loop(0, (seen + 3) // 4, body, 0)
 
-    for fewest, regions, unroll in ((1, 4, 1), (5, 6, 2), (7, 8, 1)):
-
-        @pl.when((count > 4) & (seen >= fewest) & (seen <= regions))
+    sizes = ((4, 1), (6, 2), (8, 1)) if len(shifts) == 1 else ((8, 1), (10, 1), (12, 1), (16, 1))
+    for below, (regions, unroll) in zip([0] + [r for r, _ in sizes], sizes):
+
+        @pl.when((count > 4) & (seen > below) & (seen <= regions))
         def _():
             group(0, regions, 8, unroll)
 
-
-def attend(shift, meta, seen_by, near, far, keys, values):
+    for j, out in enumerate(outs):
+        out[...] = out_ref[NZ * j : NZ * (j + 1)]
+
+
+def attend(shifts, meta, seen_by, near, far, keys, values):
     scalars = pl.BlockSpec(memory_space=pltpu.SMEM)
     vectors = pl.BlockSpec(memory_space=pltpu.VMEM)
+    cells = NZ * len(shifts)
     return pl.pallas_call(
-        functools.partial(attend_kernel, shift),
-        out_shape=jax.ShapeDtypeStruct((NZ, LR, WIDE), BF),
+        functools.partial(attend_kernel, shifts),
+        out_shape=[jax.ShapeDtypeStruct((NZ, LR, WIDE), BF)] * len(shifts),
         in_specs=[scalars] * 2 + [vectors] * 4,
-        out_specs=vectors,
-        scratch_shapes=[pltpu.SMEM((16,), jnp.int32), pltpu.VMEM((256, D), BF)],
-        compiler_params=pltpu.CompilerParams(vmem_limit_bytes=24 << 20),
-        cost_estimate=pl.CostEstimate(flops=2 << 30, bytes_accessed=8 << 20, transcendentals=2 << 20),
+        out_specs=[vectors] * len(shifts),
+        scratch_shapes=[
+            pltpu.SMEM((2, 24), jnp.int32),
+            pltpu.VMEM((cells * LR, D), BF),
+            pltpu.VMEM((cells, LR, WIDE), BF),
+        ],
+        compiler_params=pltpu.CompilerParams(vmem_limit_bytes=32 << 20),
+        cost_estimate=pl.CostEstimate(
+            flops=2 << 30, bytes_accessed=8 << 20, transcendentals=2 << 20
+        ),
         name="attend",
     )(meta, seen_by, near, far, keys, values)
 
@@ -307,11 +324,12 @@
 
     with jax.named_scope("attend"):
         pieces = []
-        for d in (2, 1, 3, 0):
-            if d == 0:
+        for shifts in ((2,), (1, 3), (0,)):
+            if shifts == (0,):
                 meta, *shards = lax.optimization_barrier((meta, *shards))
-            part = attend(d, meta, seen_by, near, far, keys, values)
-            pieces.append(shifted_x(part.reshape(NZ * LR, WIDE), -d))
+            parts = attend(shifts, meta, seen_by, near, far, keys, values)
+            for d, part in zip(shifts, parts):
+                pieces.append(shifted_x(part.reshape(NZ * LR, WIDE), -d))
     with jax.named_scope("join_x"):
         part = joined(pieces, (NZ * LR, WIDE)).reshape(NZ, LR, WIDE)
     with jax.named_scope("join_z"):

time: 104 us -> 103 us (level)
  starting transfers between devices: 32.3 us -> 30.2 us
    all_to_all x1, starting transfers between devices: 8.55 us -> 7.19 us  [on_device(): pieces = lax.all_to_all(part, 'tm', 0, 0, tiled=True)]
    ppermute x3, waiting for transfers between devices: 3.08 us -> 4.18 us  [shifted_y(): lax.ppermute(a, 'tm', [(k, (k + 2 * by) % 8) for k in range(8)])]
    pallas_call x4 -> x3, Pallas kernels: 19.9 us -> 19.8 us  [attend(): pl.pallas_call(functools.partial(attend_kernel, shifts), out_shape=[jax.S...]
where the time goes in v7:
time: 103 us; the launch traced here: 102 us
  Pallas kernels  33.6 us (33%)
  starting transfers between devices  30.2 us (29%)
  waiting for transfers between devices  19.3 us (19%)
  blocking collectives  13.3 us (13%)
  local copies, waits for them, and re-layouts  3.99 us (4%)
    pallas_call x3, Pallas kernels, attend(): pl.pallas_call(functools.partial(attend_kernel, shifts), out_shape=[jax.S...  19.8 us
    all_to_all x1, blocking collectives, on_device(): lax.all_to_all(part, 'region', 0, 0, axis_index_groups=groups, tiled=True)  13.3 us
    all_to_all x1, starting transfers between devices, on_device(): near = lax.all_to_all(q, 'region', 0, 0, tiled=True)  11.9 us
    pallas_call x1, Pallas kernels, on_device(): pl.pallas_call(keyval_kernel, grid=(observed.shape[0] // BLK,), out_shape...  8.25 us
    all_to_all x1, starting transfers between devices, on_device(): pieces = lax.all_to_all(part, 'tm', 0, 0, tiled=True)  7.19 us
    all_to_all x1, waiting for transfers between devices, on_device(): pieces = lax.all_to_all(part, 'tm', 0, 0, tiled=True)  7.12 us
    all_to_all x1, waiting for transfers between devices, on_device(): near = lax.all_to_all(q, 'region', 0, 0, tiled=True)  7.11 us
    ppermute x3, waiting for transfers between devices, shifted_y(): lax.ppermute(a, 'tm', [(k, (k + 2 * by) % 8) for k in range(8)])  4.18 us
  transfers between devices with their start and end apart: 10, of which 5 were waited for; matrix products, arithmetic and copies ran while one was open for 0% of the time, Pallas kernels for 27%

profile of v7, /device:TPU:1, one launch (start us, length us, event | category | flops | bytes accessed | tf_op | source)
XLA Modules:
  0.0 102.0 jit_solution(16709516613848199868)
XLA Ops:
  0.0 0.0 copy-start
  0.0 2.3 %queries.1 = bf16[32,16,512]{2,1,0:T(8,128)(2,1)} custom-call(s32[1]{0:T(128)} %bitcast.1.half_ref, bf16[32,512]{1,0:T(8,128)(2,1)} %bitcast.19, f32[1,512]{1,0:T(1,128)} %bitcast.25, bf16[512,512]{1,0:T(8,128)(2,1)} %wq_ref.1), custom_call_target="tpu_custom_call" | custom-call | tf_op jit(solution)/shard_map/queries/queries/pallas_call | solution.py:281
  2.3 11.9 %all-to-all-start = ((bf16[32,16,512]{2,1,0:T(8,128)(2,1)}), bf16[32,16,512]{2,1,0:T(8,128)(2,1)S(1)}, u32[]{:S(2)}, u32[]{:S(2)}) async-start(bf16[32,16,512]{2,1,0:T(8,128)(2,1)} %queries.1), calls=%async_computation | async-start | bytes 1048576 | tf_op jit(solution)/shard_map/gather/all_to_all | solution.py:290
  14.8 0.0 copy-done
  14.8 0.2 dynamic-slice_reduce_fusion.vis_ref
  15.0 0.1 pad_add_fusion.meta_ref
  15.1 8.2 %keyval.1 = (bf16[2048,512]{1,0:T(8,128)(2,1)}, bf16[2048,1024]{1,0:T(8,128)(2,1)}, bf16[512,512]{1,0:T(8,128)(2,1)}) custom-call(bf16[2048,512]{1,0:T(8,128)(2,1)} %bitcast.26, bf16[512,1024]{1,0:T(8,128)(2,1)} %w_ref.1, bf16[512,256]{1,0:T(8,128)(2,1)} %up_ref.1, bf16[256,512]{1,0:T(8,128)(2,1)} %down_ref.1), custom_call_target="tpu_custom_call" | custom-call | flops 2147483648 | bytes 9437184 | tf_op jit(solution)/shard_map/keyval/keyval/pallas_call | solution.py:293
  23.3 7.1 %all-to-all-done.near_ref = bf16[32,16,512]{2,1,0:T(8,128)(2,1)S(1)} async-done(((bf16[32,16,512]{2,1,0:T(8,128)(2,1)}), bf16[32,16,512]{2,1,0:T(8,128)(2,1)S(1)}, u32[]{:S(2)}, u32[]{:S(2)}) %all-to-all-start) | async-done | bytes 524320 | tf_op jit(solution)/shard_map/gather/all_to_all | solution.py:290
  30.4 2.4 %collective-permute-start = (bf16[32,16,512]{2,1,0:T(8,128)(2,1)S(1)}, bf16[32,16,512]{2,1,0:T(8,128)(2,1)S(1)}, u32[]{:S(2)}, u32[]{:S(2)}) collective-permute-start(bf16[32,16,512]{2,1,0:T(8,128)(2,1)S(1)} %all-to-all-done.near_ref), channel_id=1, source_target_pairs={{0,1},{1,0},{2,3},{3,2},{4,5},{5,4},{6,7},{7,6},{8,9},{9,8},{10,11... | collective-permute-start | bytes 1572872 | tf_op jit(solution)/shard_map/gather/ppermute | solution.py:256
  32.8 2.7 %collective-permute-start.6 = (bf16[512,512]{1,0:T(8,128)(2,1)}, bf16[512,512]{1,0:T(8,128)(2,1)S(1)}, u32[]{:S(2)}, u32[]{:S(2)}) collective-permute-start(bf16[512,512]{1,0:T(8,128)(2,1)} %get-tuple-element.31.refs_0_), channel_id=1, source_target_pairs={{0,6},{1,7},{2,0},{3,1},{4,2},{5,3},{6,4},{7,5},{8,14},{9,15},{10,... | collective-permute-start | bytes 1572872 | tf_op jit(solution)/shard_map/weights/ppermute | solution.py:252
  35.6 0.3 collective-permute-start.5
  35.9 0.7 collective-permute-start.4
  36.6 0.0 collective-permute-done.far_ref
  36.6 0.0 copy-start.5
  36.6 2.2 %copy-done.5 = bf16[2048,1024]{1,0:T(8,128)(2,1)S(1)} copy-done((bf16[2048,1024]{1,0:T(8,128)(2,1)S(1)}, bf16[2048,1024]{1,0:T(8,128)(2,1)}, u32[]{:S(2)}) %copy-start.5) | copy-done | bytes 4194328
  38.8 0.0 copy-start.6
  38.8 1.6 %copy-done.6 = bf16[2048,512]{1,0:T(8,128)(2,1)S(1)} copy-done((bf16[2048,512]{1,0:T(8,128)(2,1)S(1)}, bf16[2048,512]{1,0:T(8,128)(2,1)}, u32[]{:S(2)}) %copy-start.6) | copy-done | bytes 2097176
  40.4 5.6 %attend.3 = bf16[8,32,640]{2,1,0:T(8,128)(2,1)S(1)} custom-call(s32[4]{0:T(128)S(1)} %pad_add_fusion.meta_ref, s32[32]{0:T(128)S(1)} %dynamic-slice_reduce_fusion.vis_ref, bf16[32,16,512]{2,1,0:T(8,128)(2,1)S(1)} %all-to-all-done.near_ref, bf16[32,16,512]{2,1,0:T(8,128)(2,1)S(1)} %collective-permute-done.far_ref, bf16[2048,512]{1,0:T(8,128)(2,1)S(1)} %copy-done.6, ...), custom_call_target="tpu_custom_call" | custom-call | flops 2147483648 | bytes 8388608 | tf_op jit(solution)/shard_map/attend/attend/pallas_call | solution.py:173
  46.0 1.9 %collective-permute-start.1 = (bf16[256,640]{1,0:T(8,128)(2,1)S(1)}, bf16[256,640]{1,0:T(8,128)(2,1)S(1)}, u32[]{:S(2)}, u32[]{:S(2)}) collective-permute-start(bf16[256,640]{1,0:T(8,128)(2,1)S(1)} %bitcast.23), channel_id=1, source_target_pairs={{0,16},{8,24},{16,0},{24,8},{32,48},{40,56},{48,32},{56,40},{64,80... | collective-permute-start | bytes 983048 | tf_op jit(solution)/shard_map/attend/ppermute | solution.py:248
  47.9 8.3 %attend.4 = (bf16[8,32,640]{2,1,0:T(8,128)(2,1)S(1)}, bf16[8,32,640]{2,1,0:T(8,128)(2,1)S(1)}) custom-call(s32[4]{0:T(128)S(1)} %pad_add_fusion.meta_ref, s32[32]{0:T(128)S(1)} %dynamic-slice_reduce_fusion.vis_ref, bf16[32,16,512]{2,1,0:T(8,128)(2,1)S(1)} %all-to-all-done.near_ref, bf16[32,16,512]{2,1,0:T(8,128)(2,1)S(1)} %collective-permute-done.far_ref, ...), custom_call_target="tpu_custom_call" | custom-call | flops 2147483648 | bytes 8388608 | tf_op jit(solution)/shard_map/attend/attend/pallas_call | solution.py:173
  56.2 0.1 collective-permute-start.3
  56.3 2.0 %collective-permute-done.6.refs_3_ = bf16[512,512]{1,0:T(8,128)(2,1)S(1)} collective-permute-done((bf16[512,512]{1,0:T(8,128)(2,1)}, bf16[512,512]{1,0:T(8,128)(2,1)S(1)}, u32[]{:S(2)}, u32[]{:S(2)}) %collective-permute-start.6) | collective-permute-done | bytes 524320 | tf_op jit(solution)/shard_map/weights/ppermute | solution.py:252
  58.3 1.8 %collective-permute-start.2 = (bf16[256,640]{1,0:T(8,128)(2,1)S(1)}, bf16[256,640]{1,0:T(8,128)(2,1)S(1)}, u32[]{:S(2)}, u32[]{:S(2)}) collective-permute-start(bf16[256,640]{1,0:T(8,128)(2,1)S(1)} %bitcast.22), channel_id=1, source_target_pairs={{0,24},{8,0},{16,8},{24,16},{32,56},{40,32},{48,40},{56,48},{64,88... | collective-permute-start | bytes 983048 | tf_op jit(solution)/shard_map/attend/ppermute | solution.py:248
  60.2 0.0 collective-permute-done.5.refs_2_
  60.2 2.2 %collective-permute-done.4.refs_1_ = bf16[512,512]{1,0:T(8,128)(2,1)S(1)} collective-permute-done((bf16[512,512]{1,0:T(8,128)(2,1)}, bf16[512,512]{1,0:T(8,128)(2,1)S(1)}, u32[]{:S(2)}, u32[]{:S(2)}) %collective-permute-start.4) | collective-permute-done | bytes 524320 | tf_op jit(solution)/shard_map/weights/ppermute | solution.py:252
  62.4 5.8 %attend.5 = bf16[8,32,640]{2,1,0:T(8,128)(2,1)S(1)} custom-call(s32[4]{0:T(128)S(1)} %pad_add_fusion.meta_ref, s32[32]{0:T(128)S(1)} %dynamic-slice_reduce_fusion.vis_ref, bf16[32,16,512]{2,1,0:T(8,128)(2,1)S(1)} %all-to-all-done.near_ref, bf16[32,16,512]{2,1,0:T(8,128)(2,1)S(1)} %collective-permute-done.far_ref, bf16[2048,512]{1,0:T(8,128)(2,1)S(1)} %copy-done.6, ...), custom_call_target="tpu_custom_call" | custom-call | flops 2147483648 | bytes 8388608 | tf_op jit(solution)/shard_map/attend/attend/pallas_call | solution.py:173
  68.2 0.0 copy-start.1
  68.2 0.0 copy-start.2
  68.2 0.0 copy-start.3
  68.2 0.0 copy-start.4
  68.2 0.0 collective-permute-done.1.refs_0_
  68.2 0.0 collective-permute-done.3.refs_2_
  68.3 0.0 collective-permute-done.2.refs_1_
  68.3 1.0 %join_pieces.2 = bf16[256,640]{1,0:T(8,128)(2,1)S(1)} custom-call(bf16[256,640]{1,0:T(8,128)(2,1)S(1)} %collective-permute-done.1.refs_0_, bf16[256,640]{1,0:T(8,128)(2,1)S(1)} %collective-permute-done.2.refs_1_, bf16[256,640]{1,0:T(8,128)(2,1)S(1)} %collective-permute-done.3.refs_2_, bf16[256,640]{1,0:T(8,128)(2,1)S(1)} %bitcast.18), custom_call_target="tpu_custom_call" | custom-call | tf_op jit(solution)/shard_map/join_x/join_pieces/pallas_call | solution.py:218
  69.3 13.3 %all_to_all.15.refs_0_ = bf16[8,32,640]{2,1,0:T(8,128)(2,1)S(1)} all-to-all(bf16[8,32,640]{2,1,0:T(8,128)(2,1)S(1)} %bitcast.17), channel_id=1, replica_groups={{0,32,64,96,128,160,192,224},{8,40,72,104,136,168,200,232},{16,48,80,11..., dimensions={0} | all-to-all | bytes 655360 | tf_op jit(solution)/shard_map/join_z/all_to_all | solution.py:337
  82.6 1.1 %join_pieces.3 = bf16[8,32,640]{2,1,0:T(8,128)(2,1)} custom-call(bf16[8,32,640]{2,1,0:T(8,128)(2,1)S(1)} %all_to_all.15.refs_0_), custom_call_target="tpu_custom_call" | custom-call | tf_op jit(solution)/shard_map/join_z/join_pieces/pallas_call | solution.py:218
  83.7 7.2 %all-to-all-start.2 = ((bf16[8,32,640]{2,1,0:T(8,128)(2,1)}), bf16[8,32,640]{2,1,0:T(8,128)(2,1)S(1)}, u32[]{:S(2)}, u32[]{:S(2)}) async-start(bf16[8,32,640]{2,1,0:T(8,128)(2,1)} %join_pieces.3), calls=%async_computation.2 | async-start | bytes 655360 | tf_op jit(solution)/shard_map/join_t/all_to_all | solution.py:340
  90.9 7.1 %all-to-all-done.2.pieces_ref = bf16[8,32,640]{2,1,0:T(8,128)(2,1)S(1)} async-done(((bf16[8,32,640]{2,1,0:T(8,128)(2,1)}), bf16[8,32,640]{2,1,0:T(8,128)(2,1)S(1)}, u32[]{:S(2)}, u32[]{:S(2)}) %all-to-all-start.2) | async-done | bytes 327712 | tf_op jit(solution)/shard_map/join_t/all_to_all | solution.py:340
  98.1 0.0 copy-done.1
  98.1 0.0 copy-done.2
  98.1 0.0 copy-done.3
  98.1 0.0 copy-done.4
  98.1 1.2 %final.1 = (f32[32,512]{1,0:T(8,128)S(1)}, f32[32,512]{1,0:T(8,128)S(1)}) custom-call(s32[1]{0:T(128)} %bitcast.row_ref, bf16[8,32,640]{2,1,0:T(8,128)(2,1)S(1)} %all-to-all-done.2.pieces_ref, bf16[32,512]{1,0:T(8,128)(2,1)S(1)} %bitcast.20, f32[1,512]{1,0:T(1,128)S(1)} %bitcast.21, bf16[512,512]{1,0:T(8,128)(2,1)S(1)} %copy-done.1, ...), custom_call_target="tpu_custom_call" | custom-call | tf_op jit(solution)/shard_map/final/final/pallas_call | solution.py:342
  99.3 1.2 %collective-permute-start.7 = (f32[32,512]{1,0:T(8,128)S(1)}, f32[32,512]{1,0:T(8,128)S(1)}, u32[]{:S(2)}, u32[]{:S(2)}) collective-permute-start(f32[32,512]{1,0:T(8,128)S(1)} %get-tuple-element.36), channel_id=1, source_target_pairs={{0,1},{1,0},{2,3},{3,2},{4,5},{5,4},{6,7},{7,6},{8,9},{9,8},{10,11... | collective-permute-start | bytes 196616 | tf_op jit(solution)/shard_map/final/ppermute | solution.py:256
  100.5 0.9 collective-permute-done.7
  101.4 0.6 fusion
Async XLA Ops:
  0.0 14.8 %copy-start = (s32[32,32]{1,0:T(8,128)S(1)}, s32[32,32]{1,0:T(8,128)}, u32[]{:S(2)}) copy-start(s32[32,32]{1,0:T(8,128)} %param.13) | copy-start | bytes 12292
  2.3 28.2 %all-to-all-start = ((bf16[32,16,512]{2,1,0:T(8,128)(2,1)}), bf16[32,16,512]{2,1,0:T(8,128)(2,1)S(1)}, u32[]{:S(2)}, u32[]{:S(2)}) async-start(bf16[32,16,512]{2,1,0:T(8,128)(2,1)} %queries.1), calls=%async_computation | async-start | bytes 1048576 | tf_op jit(solution)/shard_map/gather/all_to_all | solution.py:290
  30.4 6.2 %collective-permute-start = (bf16[32,16,512]{2,1,0:T(8,128)(2,1)S(1)}, bf16[32,16,512]{2,1,0:T(8,128)(2,1)S(1)}, u32[]{:S(2)}, u32[]{:S(2)}) collective-permute-start(bf16[32,16,512]{2,1,0:T(8,128)(2,1)S(1)} %all-to-all-done.near_ref), channel_id=1, source_target_pairs={{0,1},{1,0},{2,3},{3,2},{4,5},{5,4},{6,7},{7,6},{8,9},{9,8},{10,11... | collective-permute-start | bytes 1572872 | tf_op jit(solution)/shard_map/gather/ppermute | solution.py:256
  32.8 25.5 %collective-permute-start.6 = (bf16[512,512]{1,0:T(8,128)(2,1)}, bf16[512,512]{1,0:T(8,128)(2,1)S(1)}, u32[]{:S(2)}, u32[]{:S(2)}) collective-permute-start(bf16[512,512]{1,0:T(8,128)(2,1)} %get-tuple-element.31.refs_0_), channel_id=1, source_target_pairs={{0,6},{1,7},{2,0},{3,1},{4,2},{5,3},{6,4},{7,5},{8,14},{9,15},{10,... | collective-permute-start | bytes 1572872 | tf_op jit(solution)/shard_map/weights/ppermute | solution.py:252
  35.6 24.6 %collective-permute-start.5 = (bf16[512,512]{1,0:T(8,128)(2,1)}, bf16[512,512]{1,0:T(8,128)(2,1)S(1)}, u32[]{:S(2)}, u32[]{:S(2)}) collective-permute-start(bf16[512,512]{1,0:T(8,128)(2,1)} %get-tuple-element.31.refs_0_), channel_id=1, source_target_pairs={{0,4},{1,5},{2,6},{3,7},{4,0},{5,1},{6,2},{7,3},{8,12},{9,13},{10,... | collective-permute-start | bytes 1572872 | tf_op jit(solution)/shard_map/weights/ppermute | solution.py:252
  35.9 26.4 %collective-permute-start.4 = (bf16[512,512]{1,0:T(8,128)(2,1)}, bf16[512,512]{1,0:T(8,128)(2,1)S(1)}, u32[]{:S(2)}, u32[]{:S(2)}) collective-permute-start(bf16[512,512]{1,0:T(8,128)(2,1)} %get-tuple-element.31.refs_0_), channel_id=1, source_target_pairs={{0,2},{1,3},{2,4},{3,5},{4,6},{5,7},{6,0},{7,1},{8,10},{9,11},{10,... | collective-permute-start | bytes 1572872 | tf_op jit(solution)/shard_map/weights/ppermute | solution.py:252
  36.6 2.2 %copy-start.5 = (bf16[2048,1024]{1,0:T(8,128)(2,1)S(1)}, bf16[2048,1024]{1,0:T(8,128)(2,1)}, u32[]{:S(2)}) copy-start(bf16[2048,1024]{1,0:T(8,128)(2,1)} %get-tuple-element.26.va_ref) | copy-start | bytes 12582916
  38.8 1.6 %copy-start.6 = (bf16[2048,512]{1,0:T(8,128)(2,1)S(1)}, bf16[2048,512]{1,0:T(8,128)(2,1)}, u32[]{:S(2)}) copy-start(bf16[2048,512]{1,0:T(8,128)(2,1)} %get-tuple-element.25.k_ref) | copy-start | bytes 6291460
  46.0 22.2 %collective-permute-start.1 = (bf16[256,640]{1,0:T(8,128)(2,1)S(1)}, bf16[256,640]{1,0:T(8,128)(2,1)S(1)}, u32[]{:S(2)}, u32[]{:S(2)}) collective-permute-start(bf16[256,640]{1,0:T(8,128)(2,1)S(1)} %bitcast.23), channel_id=1, source_target_pairs={{0,16},{8,24},{16,0},{24,8},{32,48},{40,56},{48,32},{56,40},{64,80... | collective-permute-start | bytes 983048 | tf_op jit(solution)/shard_map/attend/ppermute | solution.py:248
  56.2 12.0 %collective-permute-start.3 = (bf16[256,640]{1,0:T(8,128)(2,1)S(1)}, bf16[256,640]{1,0:T(8,128)(2,1)S(1)}, u32[]{:S(2)}, u32[]{:S(2)}) collective-permute-start(bf16[256,640]{1,0:T(8,128)(2,1)S(1)} %bitcast.24), channel_id=1, source_target_pairs={{0,8},{8,16},{16,24},{24,0},{32,40},{40,48},{48,56},{56,32},{64,72... | collective-permute-start | bytes 983048 | tf_op jit(solution)/shard_map/attend/ppermute | solution.py:248
  58.3 9.9 %collective-permute-start.2 = (bf16[256,640]{1,0:T(8,128)(2,1)S(1)}, bf16[256,640]{1,0:T(8,128)(2,1)S(1)}, u32[]{:S(2)}, u32[]{:S(2)}) collective-permute-start(bf16[256,640]{1,0:T(8,128)(2,1)S(1)} %bitcast.22), channel_id=1, source_target_pairs={{0,24},{8,0},{16,8},{24,16},{32,56},{40,32},{48,40},{56,48},{64,88... | collective-permute-start | bytes 983048 | tf_op jit(solution)/shard_map/attend/ppermute | solution.py:248
  68.2 29.9 %copy-start.1 = (bf16[512,512]{1,0:T(8,128)(2,1)S(1)}, bf16[512,512]{1,0:T(8,128)(2,1)}, u32[]{:S(2)}) copy-start(bf16[512,512]{1,0:T(8,128)(2,1)} %wo_ref.1) | copy-start | bytes 1572868
  68.2 29.9 %copy-start.2 = (bf16[512,512]{1,0:T(8,128)(2,1)S(1)}, bf16[512,512]{1,0:T(8,128)(2,1)}, u32[]{:S(2)}) copy-start(bf16[512,512]{1,0:T(8,128)(2,1)} %get-tuple-element.31.refs_0_) | copy-start | bytes 1572868
  68.2 29.8 %copy-start.3 = (bf16[1,32,512]{2,1,0:T(8,128)(2,1)S(1)}, bf16[1,32,512]{2,1,0:T(8,128)(2,1)}, u32[]{:S(2)}) copy-start(bf16[1,32,512]{2,1,0:T(8,128)(2,1)} %param.14) | copy-start | bytes 98308
  68.2 29.8 %copy-start.4 = (f32[512]{0:T(512)S(1)}, f32[512]{0:T(512)}, u32[]{:S(2)}) copy-start(f32[512]{0:T(512)} %param.16) | copy-start | bytes 6148
  83.7 14.3 %all-to-all-start.2 = ((bf16[8,32,640]{2,1,0:T(8,128)(2,1)}), bf16[8,32,640]{2,1,0:T(8,128)(2,1)S(1)}, u32[]{:S(2)}, u32[]{:S(2)}) async-start(bf16[8,32,640]{2,1,0:T(8,128)(2,1)} %join_pieces.3), calls=%async_computation.2 | async-start | bytes 655360 | tf_op jit(solution)/shard_map/join_t/all_to_all | solution.py:340
  99.3 2.1 %collective-permute-start.7 = (f32[32,512]{1,0:T(8,128)S(1)}, f32[32,512]{1,0:T(8,128)S(1)}, u32[]{:S(2)}, u32[]{:S(2)}) collective-permute-start(f32[32,512]{1,0:T(8,128)S(1)} %get-tuple-element.36), channel_id=1, source_target_pairs={{0,1},{1,0},{2,3},{3,2},{4,5},{5,4},{6,7},{7,6},{8,9},{9,8},{10,11... | collective-permute-start | bytes 196616 | tf_op jit(solution)/shard_map/final/ppermute | solution.py:256

commit v8 on v7

--- a/solution.py
+++ b/solution.py
@@ -85,7 +85,7 @@
             sees = (vis_ref[region] > 0) | (region == own)
             seen = seen + sees.astype(jnp.int32)
     last = jnp.maximum(seen - 1, 0)
-    for k in range(4):
+    for k in range(7):
         for row in range(2):
             list_ref[row, seen + k] = list_ref[row, last]
 

time: 103 us -> 103 us (level)
  blocking collectives: 13.3 us -> 15.3 us
  starting transfers between devices: 30.2 us -> 28.5 us
    all_to_all x1, starting transfers between devices: 7.19 us -> 5.13 us  [on_device(): pieces = lax.all_to_all(part, 'tm', 0, 0, tiled=True)]
    all_to_all x1, blocking collectives: 13.3 us -> 15.3 us  [on_device(): lax.all_to_all(part, 'region', 0, 0, axis_index_groups=groups, tiled=True)]
  transfers between devices with their start and end apart: 10 -> 10, of which waited for: 5 -> 5; matrix products, arithmetic and copies ran while one was open for 0% -> 0% of each run, Pallas kernels for 27% -> 28%
where the time goes in v8:
time: 103 us; the launch traced here: 102 us
  Pallas kernels  33.7 us (33%)
  starting transfers between devices  28.5 us (28%)
  waiting for transfers between devices  18.9 us (18%)
  blocking collectives  15.3 us (15%)
  local copies, waits for them, and re-layouts  3.99 us (4%)
    pallas_call x3, Pallas kernels, attend(): pl.pallas_call(functools.partial(attend_kernel, shifts), out_shape=[jax.S...  19.9 us
    all_to_all x1, blocking collectives, on_device(): lax.all_to_all(part, 'region', 0, 0, axis_index_groups=groups, tiled=True)  15.3 us
    all_to_all x1, starting transfers between devices, on_device(): near = lax.all_to_all(q, 'region', 0, 0, tiled=True)  11.9 us
    pallas_call x1, Pallas kernels, on_device(): pl.pallas_call(keyval_kernel, grid=(observed.shape[0] // BLK,), out_shape...  8.25 us
    all_to_all x1, waiting for transfers between devices, on_device(): pieces = lax.all_to_all(part, 'tm', 0, 0, tiled=True)  7.12 us
    all_to_all x1, waiting for transfers between devices, on_device(): near = lax.all_to_all(q, 'region', 0, 0, tiled=True)  7.11 us
    all_to_all x1, starting transfers between devices, on_device(): pieces = lax.all_to_all(part, 'tm', 0, 0, tiled=True)  5.13 us
    ppermute x3, starting transfers between devices, shifted_x(): return lax.ppermute(a, 'region', pairs) if by % NX else a  4.16 us
  transfers between devices with their start and end apart: 10, of which 5 were waited for; matrix products, arithmetic and copies ran while one was open for 0% of the time, Pallas kernels for 28%

profile of v8, /device:TPU:1, one launch (start us, length us, event | category | flops | bytes accessed | tf_op | source)
XLA Modules:
  0.0 102.0 jit_solution(3523123638220890918)
XLA Ops:
  0.0 0.0 copy-start
  0.0 2.3 %queries.1 = bf16[32,16,512]{2,1,0:T(8,128)(2,1)} custom-call(s32[1]{0:T(128)} %bitcast.1.half_ref, bf16[32,512]{1,0:T(8,128)(2,1)} %bitcast.19, f32[1,512]{1,0:T(1,128)} %bitcast.25, bf16[512,512]{1,0:T(8,128)(2,1)} %wq_ref.1), custom_call_target="tpu_custom_call" | custom-call | tf_op jit(solution)/shard_map/queries/queries/pallas_call | solution.py:281
  2.3 11.9 %all-to-all-start = ((bf16[32,16,512]{2,1,0:T(8,128)(2,1)}), bf16[32,16,512]{2,1,0:T(8,128)(2,1)S(1)}, u32[]{:S(2)}, u32[]{:S(2)}) async-start(bf16[32,16,512]{2,1,0:T(8,128)(2,1)} %queries.1), calls=%async_computation | async-start | bytes 1048576 | tf_op jit(solution)/shard_map/gather/all_to_all | solution.py:290
  14.8 0.0 copy-done
  14.8 0.2 dynamic-slice_reduce_fusion.vis_ref
  15.0 0.1 pad_add_fusion.meta_ref
  15.1 8.2 %keyval.1 = (bf16[2048,512]{1,0:T(8,128)(2,1)}, bf16[2048,1024]{1,0:T(8,128)(2,1)}, bf16[512,512]{1,0:T(8,128)(2,1)}) custom-call(bf16[2048,512]{1,0:T(8,128)(2,1)} %bitcast.26, bf16[512,1024]{1,0:T(8,128)(2,1)} %w_ref.1, bf16[512,256]{1,0:T(8,128)(2,1)} %up_ref.1, bf16[256,512]{1,0:T(8,128)(2,1)} %down_ref.1), custom_call_target="tpu_custom_call" | custom-call | flops 2147483648 | bytes 9437184 | tf_op jit(solution)/shard_map/keyval/keyval/pallas_call | solution.py:293
  23.3 7.1 %all-to-all-done.near_ref = bf16[32,16,512]{2,1,0:T(8,128)(2,1)S(1)} async-done(((bf16[32,16,512]{2,1,0:T(8,128)(2,1)}), bf16[32,16,512]{2,1,0:T(8,128)(2,1)S(1)}, u32[]{:S(2)}, u32[]{:S(2)}) %all-to-all-start) | async-done | bytes 524320 | tf_op jit(solution)/shard_map/gather/all_to_all | solution.py:290
  30.4 2.4 %collective-permute-start = (bf16[32,16,512]{2,1,0:T(8,128)(2,1)S(1)}, bf16[32,16,512]{2,1,0:T(8,128)(2,1)S(1)}, u32[]{:S(2)}, u32[]{:S(2)}) collective-permute-start(bf16[32,16,512]{2,1,0:T(8,128)(2,1)S(1)} %all-to-all-done.near_ref), channel_id=1, source_target_pairs={{0,1},{1,0},{2,3},{3,2},{4,5},{5,4},{6,7},{7,6},{8,9},{9,8},{10,11... | collective-permute-start | bytes 1572872 | tf_op jit(solution)/shard_map/gather/ppermute | solution.py:256
  32.8 2.7 %collective-permute-start.6 = (bf16[512,512]{1,0:T(8,128)(2,1)}, bf16[512,512]{1,0:T(8,128)(2,1)S(1)}, u32[]{:S(2)}, u32[]{:S(2)}) collective-permute-start(bf16[512,512]{1,0:T(8,128)(2,1)} %get-tuple-element.31.refs_0_), channel_id=1, source_target_pairs={{0,6},{1,7},{2,0},{3,1},{4,2},{5,3},{6,4},{7,5},{8,14},{9,15},{10,... | collective-permute-start | bytes 1572872 | tf_op jit(solution)/shard_map/weights/ppermute | solution.py:252
  35.6 0.3 collective-permute-start.5
  35.9 0.7 collective-permute-start.4
  36.6 0.0 collective-permute-done.far_ref
  36.6 0.0 copy-start.5
  36.6 2.2 %copy-done.5 = bf16[2048,1024]{1,0:T(8,128)(2,1)S(1)} copy-done((bf16[2048,1024]{1,0:T(8,128)(2,1)S(1)}, bf16[2048,1024]{1,0:T(8,128)(2,1)}, u32[]{:S(2)}) %copy-start.5) | copy-done | bytes 4194328
  38.8 0.0 copy-start.6
  38.8 1.6 %copy-done.6 = bf16[2048,512]{1,0:T(8,128)(2,1)S(1)} copy-done((bf16[2048,512]{1,0:T(8,128)(2,1)S(1)}, bf16[2048,512]{1,0:T(8,128)(2,1)}, u32[]{:S(2)}) %copy-start.6) | copy-done | bytes 2097176
  40.4 5.6 %attend.3 = bf16[8,32,640]{2,1,0:T(8,128)(2,1)S(1)} custom-call(s32[4]{0:T(128)S(1)} %pad_add_fusion.meta_ref, s32[32]{0:T(128)S(1)} %dynamic-slice_reduce_fusion.vis_ref, bf16[32,16,512]{2,1,0:T(8,128)(2,1)S(1)} %all-to-all-done.near_ref, bf16[32,16,512]{2,1,0:T(8,128)(2,1)S(1)} %collective-permute-done.far_ref, bf16[2048,512]{1,0:T(8,128)(2,1)S(1)} %copy-done.6, ...), custom_call_target="tpu_custom_call" | custom-call | flops 2147483648 | bytes 8388608 | tf_op jit(solution)/shard_map/attend/attend/pallas_call | solution.py:173
  46.0 2.2 %collective-permute-start.1 = (bf16[256,640]{1,0:T(8,128)(2,1)S(1)}, bf16[256,640]{1,0:T(8,128)(2,1)S(1)}, u32[]{:S(2)}, u32[]{:S(2)}) collective-permute-start(bf16[256,640]{1,0:T(8,128)(2,1)S(1)} %bitcast.23), channel_id=1, source_target_pairs={{0,16},{8,24},{16,0},{24,8},{32,48},{40,56},{48,32},{56,40},{64,80... | collective-permute-start | bytes 983048 | tf_op jit(solution)/shard_map/attend/ppermute | solution.py:248
  48.3 8.4 %attend.4 = (bf16[8,32,640]{2,1,0:T(8,128)(2,1)S(1)}, bf16[8,32,640]{2,1,0:T(8,128)(2,1)S(1)}) custom-call(s32[4]{0:T(128)S(1)} %pad_add_fusion.meta_ref, s32[32]{0:T(128)S(1)} %dynamic-slice_reduce_fusion.vis_ref, bf16[32,16,512]{2,1,0:T(8,128)(2,1)S(1)} %all-to-all-done.near_ref, bf16[32,16,512]{2,1,0:T(8,128)(2,1)S(1)} %collective-permute-done.far_ref, ...), custom_call_target="tpu_custom_call" | custom-call | flops 2147483648 | bytes 8388608 | tf_op jit(solution)/shard_map/attend/attend/pallas_call | solution.py:173
  56.6 0.1 collective-permute-start.3
  56.7 1.6 %collective-permute-done.6.refs_3_ = bf16[512,512]{1,0:T(8,128)(2,1)S(1)} collective-permute-done((bf16[512,512]{1,0:T(8,128)(2,1)}, bf16[512,512]{1,0:T(8,128)(2,1)S(1)}, u32[]{:S(2)}, u32[]{:S(2)}) %collective-permute-start.6) | collective-permute-done | bytes 524320 | tf_op jit(solution)/shard_map/weights/ppermute | solution.py:252
  58.3 1.8 %collective-permute-start.2 = (bf16[256,640]{1,0:T(8,128)(2,1)S(1)}, bf16[256,640]{1,0:T(8,128)(2,1)S(1)}, u32[]{:S(2)}, u32[]{:S(2)}) collective-permute-start(bf16[256,640]{1,0:T(8,128)(2,1)S(1)} %bitcast.22), channel_id=1, source_target_pairs={{0,24},{8,0},{16,8},{24,16},{32,56},{40,32},{48,40},{56,48},{64,88... | collective-permute-start | bytes 983048 | tf_op jit(solution)/shard_map/attend/ppermute | solution.py:248
  60.2 0.0 collective-permute-done.5.refs_2_
  60.2 2.2 %collective-permute-done.4.refs_1_ = bf16[512,512]{1,0:T(8,128)(2,1)S(1)} collective-permute-done((bf16[512,512]{1,0:T(8,128)(2,1)}, bf16[512,512]{1,0:T(8,128)(2,1)S(1)}, u32[]{:S(2)}, u32[]{:S(2)}) %collective-permute-start.4) | collective-permute-done | bytes 524320 | tf_op jit(solution)/shard_map/weights/ppermute | solution.py:252
  62.4 5.9 %attend.5 = bf16[8,32,640]{2,1,0:T(8,128)(2,1)S(1)} custom-call(s32[4]{0:T(128)S(1)} %pad_add_fusion.meta_ref, s32[32]{0:T(128)S(1)} %dynamic-slice_reduce_fusion.vis_ref, bf16[32,16,512]{2,1,0:T(8,128)(2,1)S(1)} %all-to-all-done.near_ref, bf16[32,16,512]{2,1,0:T(8,128)(2,1)S(1)} %collective-permute-done.far_ref, bf16[2048,512]{1,0:T(8,128)(2,1)S(1)} %copy-done.6, ...), custom_call_target="tpu_custom_call" | custom-call | flops 2147483648 | bytes 8388608 | tf_op jit(solution)/shard_map/attend/attend/pallas_call | solution.py:173
  68.2 0.0 copy-start.1
  68.2 0.0 copy-start.2
  68.2 0.0 copy-start.3
  68.3 0.0 copy-start.4
  68.3 0.0 collective-permute-done.1.refs_0_
  68.3 0.0 collective-permute-done.3.refs_2_
  68.3 0.0 collective-permute-done.2.refs_1_
  68.3 1.0 %join_pieces.2 = bf16[256,640]{1,0:T(8,128)(2,1)S(1)} custom-call(bf16[256,640]{1,0:T(8,128)(2,1)S(1)} %collective-permute-done.1.refs_0_, bf16[256,640]{1,0:T(8,128)(2,1)S(1)} %collective-permute-done.2.refs_1_, bf16[256,640]{1,0:T(8,128)(2,1)S(1)} %collective-permute-done.3.refs_2_, bf16[256,640]{1,0:T(8,128)(2,1)S(1)} %bitcast.18), custom_call_target="tpu_custom_call" | custom-call | tf_op jit(solution)/shard_map/join_x/join_pieces/pallas_call | solution.py:218
  69.3 15.3 %all_to_all.15.refs_0_ = bf16[8,32,640]{2,1,0:T(8,128)(2,1)S(1)} all-to-all(bf16[8,32,640]{2,1,0:T(8,128)(2,1)S(1)} %bitcast.17), channel_id=1, replica_groups={{0,32,64,96,128,160,192,224},{8,40,72,104,136,168,200,232},{16,48,80,11..., dimensions={0} | all-to-all | bytes 655360 | tf_op jit(solution)/shard_map/join_z/all_to_all | solution.py:337
  84.7 1.1 %join_pieces.3 = bf16[8,32,640]{2,1,0:T(8,128)(2,1)} custom-call(bf16[8,32,640]{2,1,0:T(8,128)(2,1)S(1)} %all_to_all.15.refs_0_), custom_call_target="tpu_custom_call" | custom-call | tf_op jit(solution)/shard_map/join_z/join_pieces/pallas_call | solution.py:218
  85.8 5.1 %all-to-all-start.2 = ((bf16[8,32,640]{2,1,0:T(8,128)(2,1)}), bf16[8,32,640]{2,1,0:T(8,128)(2,1)S(1)}, u32[]{:S(2)}, u32[]{:S(2)}) async-start(bf16[8,32,640]{2,1,0:T(8,128)(2,1)} %join_pieces.3), calls=%async_computation.2 | async-start | bytes 655360 | tf_op jit(solution)/shard_map/join_t/all_to_all | solution.py:340
  90.9 7.1 %all-to-all-done.2.pieces_ref = bf16[8,32,640]{2,1,0:T(8,128)(2,1)S(1)} async-done(((bf16[8,32,640]{2,1,0:T(8,128)(2,1)}), bf16[8,32,640]{2,1,0:T(8,128)(2,1)S(1)}, u32[]{:S(2)}, u32[]{:S(2)}) %all-to-all-start.2) | async-done | bytes 327712 | tf_op jit(solution)/shard_map/join_t/all_to_all | solution.py:340
  98.1 0.0 copy-done.1
  98.1 0.0 copy-done.2
  98.1 0.0 copy-done.3
  98.1 0.0 copy-done.4
  98.1 1.2 %final.1 = (f32[32,512]{1,0:T(8,128)S(1)}, f32[32,512]{1,0:T(8,128)S(1)}) custom-call(s32[1]{0:T(128)} %bitcast.row_ref, bf16[8,32,640]{2,1,0:T(8,128)(2,1)S(1)} %all-to-all-done.2.pieces_ref, bf16[32,512]{1,0:T(8,128)(2,1)S(1)} %bitcast.20, f32[1,512]{1,0:T(1,128)S(1)} %bitcast.21, bf16[512,512]{1,0:T(8,128)(2,1)S(1)} %copy-done.1, ...), custom_call_target="tpu_custom_call" | custom-call | tf_op jit(solution)/shard_map/final/final/pallas_call | solution.py:342
  99.3 1.2 %collective-permute-start.7 = (f32[32,512]{1,0:T(8,128)S(1)}, f32[32,512]{1,0:T(8,128)S(1)}, u32[]{:S(2)}, u32[]{:S(2)}) collective-permute-start(f32[32,512]{1,0:T(8,128)S(1)} %get-tuple-element.36), channel_id=1, source_target_pairs={{0,1},{1,0},{2,3},{3,2},{4,5},{5,4},{6,7},{7,6},{8,9},{9,8},{10,11... | collective-permute-start | bytes 196616 | tf_op jit(solution)/shard_map/final/ppermute | solution.py:256
  100.5 0.9 collective-permute-done.7
  101.4 0.6 fusion
Async XLA Ops:
  0.0 14.8 %copy-start = (s32[32,32]{1,0:T(8,128)S(1)}, s32[32,32]{1,0:T(8,128)}, u32[]{:S(2)}) copy-start(s32[32,32]{1,0:T(8,128)} %param.13) | copy-start | bytes 12292
  2.3 28.2 %all-to-all-start = ((bf16[32,16,512]{2,1,0:T(8,128)(2,1)}), bf16[32,16,512]{2,1,0:T(8,128)(2,1)S(1)}, u32[]{:S(2)}, u32[]{:S(2)}) async-start(bf16[32,16,512]{2,1,0:T(8,128)(2,1)} %queries.1), calls=%async_computation | async-start | bytes 1048576 | tf_op jit(solution)/shard_map/gather/all_to_all | solution.py:290
  30.4 6.2 %collective-permute-start = (bf16[32,16,512]{2,1,0:T(8,128)(2,1)S(1)}, bf16[32,16,512]{2,1,0:T(8,128)(2,1)S(1)}, u32[]{:S(2)}, u32[]{:S(2)}) collective-permute-start(bf16[32,16,512]{2,1,0:T(8,128)(2,1)S(1)} %all-to-all-done.near_ref), channel_id=1, source_target_pairs={{0,1},{1,0},{2,3},{3,2},{4,5},{5,4},{6,7},{7,6},{8,9},{9,8},{10,11... | collective-permute-start | bytes 1572872 | tf_op jit(solution)/shard_map/gather/ppermute | solution.py:256
  32.8 25.5 %collective-permute-start.6 = (bf16[512,512]{1,0:T(8,128)(2,1)}, bf16[512,512]{1,0:T(8,128)(2,1)S(1)}, u32[]{:S(2)}, u32[]{:S(2)}) collective-permute-start(bf16[512,512]{1,0:T(8,128)(2,1)} %get-tuple-element.31.refs_0_), channel_id=1, source_target_pairs={{0,6},{1,7},{2,0},{3,1},{4,2},{5,3},{6,4},{7,5},{8,14},{9,15},{10,... | collective-permute-start | bytes 1572872 | tf_op jit(solution)/shard_map/weights/ppermute | solution.py:252
  35.6 24.6 %collective-permute-start.5 = (bf16[512,512]{1,0:T(8,128)(2,1)}, bf16[512,512]{1,0:T(8,128)(2,1)S(1)}, u32[]{:S(2)}, u32[]{:S(2)}) collective-permute-start(bf16[512,512]{1,0:T(8,128)(2,1)} %get-tuple-element.31.refs_0_), channel_id=1, source_target_pairs={{0,4},{1,5},{2,6},{3,7},{4,0},{5,1},{6,2},{7,3},{8,12},{9,13},{10,... | collective-permute-start | bytes 1572872 | tf_op jit(solution)/shard_map/weights/ppermute | solution.py:252
  35.9 26.4 %collective-permute-start.4 = (bf16[512,512]{1,0:T(8,128)(2,1)}, bf16[512,512]{1,0:T(8,128)(2,1)S(1)}, u32[]{:S(2)}, u32[]{:S(2)}) collective-permute-start(bf16[512,512]{1,0:T(8,128)(2,1)} %get-tuple-element.31.refs_0_), channel_id=1, source_target_pairs={{0,2},{1,3},{2,4},{3,5},{4,6},{5,7},{6,0},{7,1},{8,10},{9,11},{10,... | collective-permute-start | bytes 1572872 | tf_op jit(solution)/shard_map/weights/ppermute | solution.py:252
  36.6 2.2 %copy-start.5 = (bf16[2048,1024]{1,0:T(8,128)(2,1)S(1)}, bf16[2048,1024]{1,0:T(8,128)(2,1)}, u32[]{:S(2)}) copy-start(bf16[2048,1024]{1,0:T(8,128)(2,1)} %get-tuple-element.26.va_ref) | copy-start | bytes 12582916
  38.8 1.6 %copy-start.6 = (bf16[2048,512]{1,0:T(8,128)(2,1)S(1)}, bf16[2048,512]{1,0:T(8,128)(2,1)}, u32[]{:S(2)}) copy-start(bf16[2048,512]{1,0:T(8,128)(2,1)} %get-tuple-element.25.k_ref) | copy-start | bytes 6291460
  46.0 22.2 %collective-permute-start.1 = (bf16[256,640]{1,0:T(8,128)(2,1)S(1)}, bf16[256,640]{1,0:T(8,128)(2,1)S(1)}, u32[]{:S(2)}, u32[]{:S(2)}) collective-permute-start(bf16[256,640]{1,0:T(8,128)(2,1)S(1)} %bitcast.23), channel_id=1, source_target_pairs={{0,16},{8,24},{16,0},{24,8},{32,48},{40,56},{48,32},{56,40},{64,80... | collective-permute-start | bytes 983048 | tf_op jit(solution)/shard_map/attend/ppermute | solution.py:248
  56.6 11.6 %collective-permute-start.3 = (bf16[256,640]{1,0:T(8,128)(2,1)S(1)}, bf16[256,640]{1,0:T(8,128)(2,1)S(1)}, u32[]{:S(2)}, u32[]{:S(2)}) collective-permute-start(bf16[256,640]{1,0:T(8,128)(2,1)S(1)} %bitcast.24), channel_id=1, source_target_pairs={{0,8},{8,16},{16,24},{24,0},{32,40},{40,48},{48,56},{56,32},{64,72... | collective-permute-start | bytes 983048 | tf_op jit(solution)/shard_map/attend/ppermute | solution.py:248
  58.3 10.0 %collective-permute-start.2 = (bf16[256,640]{1,0:T(8,128)(2,1)S(1)}, bf16[256,640]{1,0:T(8,128)(2,1)S(1)}, u32[]{:S(2)}, u32[]{:S(2)}) collective-permute-start(bf16[256,640]{1,0:T(8,128)(2,1)S(1)} %bitcast.22), channel_id=1, source_target_pairs={{0,24},{8,0},{16,8},{24,16},{32,56},{40,32},{48,40},{56,48},{64,88... | collective-permute-start | bytes 983048 | tf_op jit(solution)/shard_map/attend/ppermute | solution.py:248
  68.2 29.8 %copy-start.1 = (bf16[512,512]{1,0:T(8,128)(2,1)S(1)}, bf16[512,512]{1,0:T(8,128)(2,1)}, u32[]{:S(2)}) copy-start(bf16[512,512]{1,0:T(8,128)(2,1)} %wo_ref.1) | copy-start | bytes 1572868
  68.2 29.8 %copy-start.2 = (bf16[512,512]{1,0:T(8,128)(2,1)S(1)}, bf16[512,512]{1,0:T(8,128)(2,1)}, u32[]{:S(2)}) copy-start(bf16[512,512]{1,0:T(8,128)(2,1)} %get-tuple-element.31.refs_0_) | copy-start | bytes 1572868
  68.2 29.8 %copy-start.3 = (bf16[1,32,512]{2,1,0:T(8,128)(2,1)S(1)}, bf16[1,32,512]{2,1,0:T(8,128)(2,1)}, u32[]{:S(2)}) copy-start(bf16[1,32,512]{2,1,0:T(8,128)(2,1)} %param.14) | copy-start | bytes 98308
  68.3 29.8 %copy-start.4 = (f32[512]{0:T(512)S(1)}, f32[512]{0:T(512)}, u32[]{:S(2)}) copy-start(f32[512]{0:T(512)} %param.16) | copy-start | bytes 6148
  85.8 12.3 %all-to-all-start.2 = ((bf16[8,32,640]{2,1,0:T(8,128)(2,1)}), bf16[8,32,640]{2,1,0:T(8,128)(2,1)S(1)}, u32[]{:S(2)}, u32[]{:S(2)}) async-start(bf16[8,32,640]{2,1,0:T(8,128)(2,1)} %join_pieces.3), calls=%async_computation.2 | async-start | bytes 655360 | tf_op jit(solution)/shard_map/join_t/all_to_all | solution.py:340
  99.3 2.1 %collective-permute-start.7 = (f32[32,512]{1,0:T(8,128)S(1)}, f32[32,512]{1,0:T(8,128)S(1)}, u32[]{:S(2)}, u32[]{:S(2)}) collective-permute-start(f32[32,512]{1,0:T(8,128)S(1)} %get-tuple-element.36), channel_id=1, source_target_pairs={{0,1},{1,0},{2,3},{3,2},{4,5},{5,4},{6,7},{7,6},{8,9},{9,8},{10,11... | collective-permute-start | bytes 196616 | tf_op jit(solution)/shard_map/final/ppermute | solution.py:256
